TPU v7x, 256 devices: a whole 4x4x8 slice. The times are simulated.
256 devices in a mesh: ctx: 64 (over x, y_hi, z), ch: 4 (over y_lo, core).
Axes of the slice: x: 4, y: 4 (y_hi: 2, y_lo: 2; y = y_hi * 2 + y_lo), z: 8, core: 2. Of those that a mesh axis runs over, the one named last changes fastest.
Arguments:
- inputs: bfloat16 [32, 16, 8192], P(None, 'ch', 'ctx'), may hold values from -0.0390625 to 0.0390625
- short_filter: float32 [3, 32, 16], P(None, None, 'ch'), may hold values from -3.5 to 3.5
- long_filter: bfloat16 [32, 8192], P(None, 'ctx'), may hold values from -0.15625 to 0.15625
- grad_out: bfloat16 [32, 16, 8192], P(None, 'ch', 'ctx'), may hold values from -6 to 6
Outputs:
- grad_in: bfloat16 [32, 16, 8192], P(None, 'ch', 'ctx')
- grad_long: float32 [32, 8192], P(None, 'ctx')
- grad_short: float32 [3, 32, 16], P(None, None, 'ch')
All inputs are finite; a program needn't handle non-finite values.
Results may differ from a plain program's by a relative error of at most 0.0031.
Values may be sent and summed in bfloat16 or wider, within the bound.
A program may use at most 128 MiB of HBM per device.

v0:
```python
import jax
import jax.numpy as jnp
from jax import lax
from jax.experimental import pallas as pl
from jax.experimental.pallas import tpu as pltpu
from jax.sharding import PartitionSpec as P


def delayed(values, by, length):
    return jnp.pad(values, ((0, 0), (by, 0)))[:, :length]


def conv_kernel(grad_ref, rev_ref, hidden_ref, long_ref, hankel, toeplitz):
    chans, _, block_len = grad_ref.shape
    block_count = hidden_ref.shape[1]
    sources, lags, _ = rev_ref.shape

    def fill_hankel(lag, carry):
        col = pl.multiple_of(lag * block_len, block_len)
        for g in range(chans):
            hankel[g, :, pl.ds(col, block_len)] = grad_ref[g, pl.ds(lag, block_count), :].astype(
                hankel.dtype
            )
        return carry

    lax.fori_loop(0, lags, fill_hankel, 0)

    def fill_toeplitz(lag, carry):
        row = pl.multiple_of(lag * block_len, block_len)
        for s in range(sources):
            line = rev_ref[s, pl.ds(lag, 1), :]
            tiled = jnp.broadcast_to(line, (block_len, 2 * block_len))
            skewed = pltpu.roll(tiled, block_len + 1, 1, stride=1, stride_axis=0)
            toeplitz[s, pl.ds(row, block_len), :] = skewed[:, :block_len].astype(toeplitz.dtype)
        return carry

    lax.fori_loop(0, lags, fill_toeplitz, 0)

    for g in range(chans):
        hidden_ref[g] = jnp.dot(hankel[g], toeplitz[0], preferred_element_type=jnp.float32)
    acc = jnp.dot(hankel[0], toeplitz[1], preferred_element_type=jnp.float32)
    for g in range(1, chans):
        acc = acc + jnp.dot(hankel[g], toeplitz[1 + g], preferred_element_type=jnp.float32)
    long_ref[...] = acc


def correlate_all(grad_seq, sources, block_len):
    chans, total_len = grad_seq.shape
    count = sources.shape[0]
    block_count = total_len // block_len
    grad_pad = jnp.pad(
        grad_seq.astype(jnp.float32).reshape(chans, block_count, block_len),
        ((0, 0), (0, block_count), (0, 0)),
    )
    blocks = sources.reshape(count, block_count, block_len)
    padded = jnp.pad(blocks, ((0, 0), (1, 1), (0, 0)))
    pairs = jnp.concatenate([padded[:, :-1], padded[:, 1:]], axis=2)
    rev = pairs[..., ::-1].astype(jnp.float32)
    lags = block_count + 1
    hidden, long = pl.pallas_call(
        conv_kernel,
        out_shape=(
            jax.ShapeDtypeStruct((chans, block_count, block_len), jnp.float32),
            jax.ShapeDtypeStruct((block_count, block_len), jnp.float32),
        ),
        scratch_shapes=[
            pltpu.VMEM((chans, block_count, lags * block_len), jnp.bfloat16),
            pltpu.VMEM((count, lags * block_len, block_len), jnp.bfloat16),
        ],
        compiler_params=pltpu.CompilerParams(vmem_limit_bytes=48 * 1024 * 1024),
    )(grad_pad, rev)
    return hidden.reshape(chans, total_len), long.reshape(total_len)


def per_device(inputs, short_filter, long_filter, grad_out):
    tap_count = short_filter.shape[0]
    filter_count, chan_count, shard_len = inputs.shape
    ctx_count = lax.axis_size("ctx")
    my_index = lax.axis_index("ctx")
    total_len = shard_len * ctx_count
    per_dev = filter_count * chan_count // ctx_count
    per_filter = chan_count // per_dev
    block_len = 128
    block_count = total_len // block_len

    send = jnp.concatenate(
        [
            grad_out.reshape(ctx_count, per_dev, shard_len),
            inputs.reshape(ctx_count, per_dev, shard_len),
            jnp.repeat(long_filter, per_filter, axis=0)[:, None, :],
        ],
        axis=1,
    )
    recv = lax.all_to_all(send, "ctx", 0, 0, tiled=True)
    seqs = recv.transpose(1, 0, 2).reshape(2 * per_dev + 1, total_len)
    grad_seq = seqs[:per_dev]
    in_seq = seqs[per_dev : 2 * per_dev].astype(jnp.float32)
    filt_seq = seqs[2 * per_dev :]
    taps = short_filter.reshape(tap_count, ctx_count, per_dev)
    taps = lax.dynamic_index_in_dim(taps, my_index, axis=1, keepdims=False)

    hidden = sum(
        (taps[offset][:, None] * delayed(in_seq, offset, total_len) for offset in range(tap_count))
    )
    hidden = hidden.astype(jnp.bfloat16)

    grad_hidden, grad_long = correlate_all(
        grad_seq, jnp.concatenate([filt_seq, hidden], axis=0), block_len
    )

    padded_grad = jnp.pad(grad_hidden, ((0, 0), (0, tap_count - 1)))
    grad_in = sum(
        (
            taps[offset][:, None] * padded_grad[:, offset : offset + total_len]
            for offset in range(tap_count)
        )
    )
    grad_in = grad_in.astype(jnp.bfloat16)
    grad_short = jnp.stack(
        [
            jnp.sum(grad_hidden * delayed(in_seq, offset, total_len), axis=1)
            for offset in range(tap_count)
        ]
    )

    short_row = jnp.pad(
        grad_short.reshape(1, tap_count * per_dev),
        ((0, 0), (0, shard_len - tap_count * per_dev)),
    )
    back = jnp.concatenate(
        [
            grad_in.astype(jnp.float32).reshape(per_dev, ctx_count, shard_len).transpose(1, 0, 2),
            grad_long.reshape(ctx_count, 1, shard_len),
            jnp.broadcast_to(short_row[None], (ctx_count, 1, shard_len)),
        ],
        axis=1,
    )
    got = lax.all_to_all(back, "ctx", 0, 0, tiled=True)
    grad_in_out = got[:, :per_dev].reshape(filter_count, chan_count, shard_len)
    grad_in_out = grad_in_out.astype(jnp.bfloat16)
    long_part = got[:, per_dev].reshape(filter_count, per_filter, shard_len).sum(axis=1)
    grad_long_out = lax.psum(long_part, "ch")
    short_all = got[:, per_dev + 1, : tap_count * per_dev].reshape(ctx_count, tap_count, per_dev)
    grad_short_out = short_all.transpose(1, 0, 2).reshape(tap_count, filter_count, chan_count)
    return (grad_in_out, grad_long_out, grad_short_out)


def solution(mesh):
    in_specs = (P(None, "ch", "ctx"), P(None, None, "ch"), P(None, "ctx"), P(None, "ch", "ctx"))
    out_specs = (P(None, "ch", "ctx"), P(None, "ctx"), P(None, None, "ch"))
    return jax.shard_map(
        per_device, mesh=mesh, in_specs=in_specs, out_specs=out_specs, check_vma=False
    )
```

profile of v0, /device:TPU:8, one launch (start us, length us, event | category | flops | bytes accessed | tf_op | source)
XLA Modules:
  0.0 70.3 jit_solution(7093438780771744969)
XLA Ops:
  0.6 0.0 copy-start.1
  0.6 0.7 %broadcast_in_dim.11 = bf16[32,2,128]{2,1,0:T(2,128)(2,1)S(1)} broadcast(bf16[32,128]{1,0:T(8,128)(2,1)} %param.6), dimensions={0,2} | broadcast | bytes 24576 | tf_op jit(solution)/shard_map/broadcast_in_dim | solution.py:90
  1.4 0.0 copy-start
  1.4 0.0 copy-done.1
  1.4 0.7 %copy-done = bf16[32,4,128]{2,1,0:T(4,128)(2,1)S(1)} copy-done((bf16[32,4,128]{2,1,0:T(4,128)(2,1)S(1)}, bf16[32,4,128]{2,1,0:T(4,128)(2,1)}, u32[]{:S(2)}) %copy-start) | copy-done | bytes 32792
  2.1 0.8 %pad_maximum_fusion = bf16[64,5,128]{2,1,0:T(8,128)(2,1)} fusion(bf16[64,1,128]{2,1,0:T(2,128)(2,1)S(1)} %copy.37, bf16[64,2,128]{2,1,0:T(2,128)(2,1)S(1)} %bitcast.62, bf16[64,2,128]{2,1,0:T(2,128)(2,1)S(1)} %bitcast.63), kind=kLoop, calls=%fused_computation.2 | loop fusion | flops 245760 | bytes 163840 | tf_op jit(solution)/shard_map/concatenate | solution.py:86
  2.9 13.7 %all-to-all-start = ((bf16[64,5,128]{2,1,0:T(8,128)(2,1)}), bf16[64,5,128]{2,1,0:T(8,128)(2,1)S(1)}, u32[]{:S(2)}, u32[]{:S(2)}) async-start(bf16[64,5,128]{2,1,0:T(8,128)(2,1)} %pad_maximum_fusion), calls=%async_computation | async-start | bytes 262144 | tf_op jit(solution)/shard_map/all_to_all | solution.py:94
  16.5 0.0 copy-start.2
  16.6 0.7 copy-done.2
  17.2 0.1 copy.36
  17.4 0.2 slice_reduce_fusion.2
  17.6 11.7 %all-to-all-done = bf16[64,5,128]{2,1,0:T(8,128)(2,1)S(1)} async-done(((bf16[64,5,128]{2,1,0:T(8,128)(2,1)}), bf16[64,5,128]{2,1,0:T(8,128)(2,1)S(1)}, u32[]{:S(2)}, u32[]{:S(2)}) %all-to-all-start) | async-done | bytes 81952 | tf_op jit(solution)/shard_map/all_to_all | solution.py:94
  29.3 0.1 copy.61
  29.3 0.2 fusion.5
  29.6 0.5 rev.3
  30.2 10.1 %shard_map.67 = (f32[2,64,128]{2,1,0:T(8,128)S(1)}, f32[64,128]{1,0:T(8,128)S(1)}) custom-call(f32[2,128,128]{2,1,0:T(8,128)S(1)} %pad_convert_fusion.grad_ref, f32[3,65,256]{2,1,0:T(8,128)S(1)} %convert_element_type.42.rev_ref), custom_call_target="tpu_custom_call" | custom-call | tf_op jit(solution)/shard_map/pallas_call | solution.py:60
  40.3 0.1 copy.60
  40.3 0.3 multiply_reduce_fusion.1
  40.7 0.1 fusion.3
  40.8 0.2 convert_bitcast_fusion.1
  41.0 0.1 reshape.58
  41.1 0.1 copy.39
  41.2 16.7 %all_to_all.10 = f32[64,4,128]{2,1,0:T(4,128)S(1)} all-to-all(f32[64,4,128]{2,1,0:T(4,128)S(1)} %copy.39), channel_id=1, replica_groups=mesh['ctx'=64,'ch'=4] {'ctx'}, dimensions={0} | all-to-all | bytes 262144 | tf_op jit(solution)/shard_map/all_to_all | solution.py:138
  57.9 0.1 copy.41
  58.0 0.1 copy.42
  58.2 0.7 copy.43
  58.9 10.7 %psum.7 = f32[32,128]{1,0:T(8,128)} all-reduce(f32[32,128]{1,0:T(8,128)S(1)} %reduce_sum.39), channel_id=1, replica_groups=mesh['ctx'=64,'ch'=4] {'ch'}, use_global_device_ids=true, to_apply=%region_4.5 | all-reduce | flops 4096 | bytes 32768 | tf_op jit(solution)/shard_map/psum | solution.py:142
  69.7 0.6 slice.107
  (20 shorter events, 0.3 us)
Async XLA Ops:
  0.6 0.8 %copy-start.1 = (bf16[32,4,128]{2,1,0:T(4,128)(2,1)S(1)}, bf16[32,4,128]{2,1,0:T(4,128)(2,1)}, u32[]{:S(2)}) copy-start(bf16[32,4,128]{2,1,0:T(4,128)(2,1)} %param.7) | copy-start | bytes 98308
  1.4 0.8 %copy-start = (bf16[32,4,128]{2,1,0:T(4,128)(2,1)S(1)}, bf16[32,4,128]{2,1,0:T(4,128)(2,1)}, u32[]{:S(2)}) copy-start(bf16[32,4,128]{2,1,0:T(4,128)(2,1)} %param.4) | copy-start | bytes 98308
  2.9 26.3 %all-to-all-start = ((bf16[64,5,128]{2,1,0:T(8,128)(2,1)}), bf16[64,5,128]{2,1,0:T(8,128)(2,1)S(1)}, u32[]{:S(2)}, u32[]{:S(2)}) async-start(bf16[64,5,128]{2,1,0:T(8,128)(2,1)} %pad_maximum_fusion), calls=%async_computation | async-start | bytes 262144 | tf_op jit(solution)/shard_map/all_to_all | solution.py:94
  16.5 0.7 copy-start.2
where the time goes:
time: 71.1 us; the launch traced here: 70.3 us
  blocking collectives  27.4 us (39%)
  starting transfers between devices  13.7 us (19%)
  waiting for transfers between devices  11.7 us (16%)
  Pallas kernels  10.1 us (14%)
  local copies, waits for them, and re-layouts  4.94 us (7%)
  other arithmetic  1.74 us (2%)
  between operations  0.85 us (1%)
    all_to_all x1, blocking collectives, per_device(): got = lax.all_to_all(back, 'ctx', 0, 0, tiled=True)  16.7 us
    all_to_all x1, starting transfers between devices, per_device(): recv = lax.all_to_all(send, 'ctx', 0, 0, tiled=True)  13.7 us
    all_to_all x1, waiting for transfers between devices, per_device(): recv = lax.all_to_all(send, 'ctx', 0, 0, tiled=True)  11.7 us
    psum x1, blocking collectives, per_device(): grad_long_out = lax.psum(long_part, 'ch')  10.7 us
    pallas_call x1, Pallas kernels, correlate_all(): pl.pallas_call(conv_kernel, out_shape=(jax.ShapeDtypeStruct((chans, block...  10.1 us
    unnamed x12, local copies, waits for them, and re-layouts  2.33 us
  transfers between devices with their start and end apart: 1, of which 1 were waited for; matrix products, arithmetic and copies ran while one was open for 0% of the time, Pallas kernels for 0%

commit v1 on v0

--- a/solution.py
+++ b/solution.py
@@ -3,7 +3,21 @@
 from jax import lax
 from jax.experimental import pallas as pl
 from jax.experimental.pallas import tpu as pltpu
+from jax.sharding import Mesh
 from jax.sharding import PartitionSpec as P
+
+INNER = "z"
+OUTER = ("x", "yh")
+CTX = OUTER + (INNER,)
+
+
+def exchange(chunks):
+    inner = lax.axis_size(INNER)
+    rest = chunks.shape[1:]
+    split = chunks.reshape((chunks.shape[0] // inner, inner) + rest)
+    split = lax.all_to_all(split, INNER, 1, 1, tiled=True)
+    split = lax.all_to_all(split, OUTER, 0, 0, tiled=True)
+    return split.reshape(chunks.shape)
 
 
 def delayed(values, by, length):
@@ -75,8 +89,8 @@
 def per_device(inputs, short_filter, long_filter, grad_out):
     tap_count = short_filter.shape[0]
     filter_count, chan_count, shard_len = inputs.shape
-    ctx_count = lax.axis_size("ctx")
-    my_index = lax.axis_index("ctx")
+    ctx_count = lax.axis_size(CTX)
+    my_index = lax.axis_index(CTX)
     total_len = shard_len * ctx_count
     per_dev = filter_count * chan_count // ctx_count
     per_filter = chan_count // per_dev
@@ -91,7 +105,7 @@
         ],
         axis=1,
     )
-    recv = lax.all_to_all(send, "ctx", 0, 0, tiled=True)
+    recv = exchange(send)
     seqs = recv.transpose(1, 0, 2).reshape(2 * per_dev + 1, total_len)
     grad_seq = seqs[:per_dev]
     in_seq = seqs[per_dev : 2 * per_dev].astype(jnp.float32)
@@ -135,7 +149,7 @@
         ],
         axis=1,
     )
-    got = lax.all_to_all(back, "ctx", 0, 0, tiled=True)
+    got = exchange(back)
     grad_in_out = got[:, :per_dev].reshape(filter_count, chan_count, shard_len)
     grad_in_out = grad_in_out.astype(jnp.bfloat16)
     long_part = got[:, per_dev].reshape(filter_count, per_filter, shard_len).sum(axis=1)
@@ -146,8 +160,13 @@
 
 
 def solution(mesh):
-    in_specs = (P(None, "ch", "ctx"), P(None, None, "ch"), P(None, "ctx"), P(None, "ch", "ctx"))
-    out_specs = (P(None, "ch", "ctx"), P(None, "ctx"), P(None, None, "ch"))
+    ctx_count = mesh.shape["ctx"]
+    inner = 8
+    outer = ctx_count // inner
+    devices = mesh.devices.reshape(outer // 2, 2, inner, mesh.shape["ch"])
+    split_mesh = Mesh(devices, ("x", "yh", "z", "ch"))
+    in_specs = (P(None, "ch", CTX), P(None, None, "ch"), P(None, CTX), P(None, "ch", CTX))
+    out_specs = (P(None, "ch", CTX), P(None, CTX), P(None, None, "ch"))
     return jax.shard_map(
-        per_device, mesh=mesh, in_specs=in_specs, out_specs=out_specs, check_vma=False
+        per_device, mesh=split_mesh, in_specs=in_specs, out_specs=out_specs, check_vma=False
     )

time: 71.1 us -> 81.6 us (1.15)
  blocking collectives: 27.4 us -> 32.6 us
  waiting for transfers between devices: 11.7 us -> 15.3 us
  local copies, waits for them, and re-layouts: 4.94 us -> 6.25 us
    all_to_all x1 -> x2, blocking collectives: 16.7 us -> 21.9 us  [the longest x1 11.5 us: exchange(): split = lax.all_to_all(split, INNER, 1, 1, tiled=True)]
    all_to_all x1 -> x2, waiting for transfers between devices: 11.7 us -> 15.3 us  [the longest x1 7.73 us: exchange(): split = lax.all_to_all(split, INNER, 1, 1, tiled=True)]
    all_to_all x1 -> x2, starting transfers between devices: 13.7 us -> 14.5 us  [the longest x1 8.47 us: exchange(): split = lax.all_to_all(split, INNER, 1, 1, tiled=True)]
  transfers between devices with their start and end apart: 1 -> 2, of which waited for: 1 -> 2; matrix products, arithmetic and copies ran while one was open for 0% -> 0% of each run, Pallas kernels for 0% -> 0%
where the time goes in v1:
time: 81.6 us; the launch traced here: 80.7 us
  blocking collectives  32.6 us (40%)
  waiting for transfers between devices  15.3 us (19%)
  starting transfers between devices  14.5 us (18%)
  Pallas kernels  10.1 us (12%)
  local copies, waits for them, and re-layouts  6.25 us (8%)
  other arithmetic  1.11 us (1%)
  between operations  0.85 us (1%)
    all_to_all x1, blocking collectives, exchange(): split = lax.all_to_all(split, INNER, 1, 1, tiled=True)  11.5 us
    psum x1, blocking collectives, per_device(): grad_long_out = lax.psum(long_part, 'ch')  10.7 us
    all_to_all x1, blocking collectives, exchange(): split = lax.all_to_all(split, OUTER, 0, 0, tiled=True)  10.5 us
    pallas_call x1, Pallas kernels, correlate_all(): pl.pallas_call(conv_kernel, out_shape=(jax.ShapeDtypeStruct((chans, block...  10.1 us
    all_to_all x1, starting transfers between devices, exchange(): split = lax.all_to_all(split, INNER, 1, 1, tiled=True)  8.47 us
    all_to_all x1, waiting for transfers between devices, exchange(): split = lax.all_to_all(split, INNER, 1, 1, tiled=True)  7.73 us
    all_to_all x1, waiting for transfers between devices, exchange(): split = lax.all_to_all(split, OUTER, 0, 0, tiled=True)  7.6 us
    all_to_all x1, starting transfers between devices, exchange(): split = lax.all_to_all(split, OUTER, 0, 0, tiled=True)  6.03 us
  transfers between devices with their start and end apart: 2, of which 2 were waited for; matrix products, arithmetic and copies ran while one was open for 0% of the time, Pallas kernels for 0%

profile of v1, /device:TPU:8, one launch (start us, length us, event | category | flops | bytes accessed | tf_op | source)
XLA Modules:
  0.0 80.7 jit_solution(13017343187876280251)
XLA Ops:
  0.6 0.0 copy-start.1
  0.6 0.7 broadcast_in_dim.11
  1.4 0.0 copy-start
  1.4 0.0 copy-done.1
  1.4 0.7 copy-done
  2.1 0.1 pad_maximum_fusion
  2.2 0.7 copy.44
  2.9 8.5 %all-to-all-start = ((bf16[8,8,5,128]{3,0,2,1:T(8,128)(2,1)}), bf16[8,8,5,128]{3,0,2,1:T(8,128)(2,1)S(1)}, u32[]{:S(2)}, u32[]{:S(2)}) async-start(bf16[8,8,5,128]{3,0,2,1:T(8,128)(2,1)} %copy.44), calls=%async_computation | async-start | bytes 163840 | tf_op jit(solution)/shard_map/all_to_all | solution.py:18
  11.4 0.7 copy-done.2
  12.1 0.1 copy.42
  12.2 7.7 %all-to-all-done = bf16[8,8,5,128]{3,0,2,1:T(8,128)(2,1)S(1)} async-done(((bf16[8,8,5,128]{3,0,2,1:T(8,128)(2,1)}), bf16[8,8,5,128]{3,0,2,1:T(8,128)(2,1)S(1)}, u32[]{:S(2)}, u32[]{:S(2)}) %all-to-all-start) | async-done | bytes 81952 | tf_op jit(solution)/shard_map/all_to_all | solution.py:18
  19.9 0.6 copy.45
  20.6 6.0 %all-to-all-start.1 = ((bf16[8,8,5,128]{3,1,2,0:T(8,128)(2,1)}), bf16[8,8,5,128]{3,1,2,0:T(8,128)(2,1)S(1)}, u32[]{:S(2)}, u32[]{:S(2)}) async-start(bf16[8,8,5,128]{3,1,2,0:T(8,128)(2,1)} %copy.45), calls=%async_computation.1 | async-start | bytes 163840 | tf_op jit(solution)/shard_map/all_to_all | solution.py:19
  26.6 0.2 slice_reduce_fusion.2
  26.8 7.6 %all-to-all-done.1 = bf16[8,8,5,128]{3,1,2,0:T(8,128)(2,1)S(1)} async-done(((bf16[8,8,5,128]{3,1,2,0:T(8,128)(2,1)}), bf16[8,8,5,128]{3,1,2,0:T(8,128)(2,1)S(1)}, u32[]{:S(2)}, u32[]{:S(2)}) %all-to-all-start.1) | async-done | bytes 81952 | tf_op jit(solution)/shard_map/all_to_all | solution.py:19
  34.4 0.1 copy.72
  34.5 0.2 fusion.5
  34.8 0.5 rev.3
  35.4 10.1 %shard_map.67 = (f32[2,64,128]{2,1,0:T(8,128)S(1)}, f32[64,128]{1,0:T(8,128)S(1)}) custom-call(f32[2,128,128]{2,1,0:T(8,128)S(1)} %pad_convert_fusion.grad_ref, f32[3,65,256]{2,1,0:T(8,128)S(1)} %convert_element_type.42.rev_ref), custom_call_target="tpu_custom_call" | custom-call | tf_op jit(solution)/shard_map/pallas_call | solution.py:74
  45.5 0.1 fusion.3
  45.6 0.1 copy.71
  45.6 0.3 multiply_reduce_fusion.1
  46.0 0.2 convert_bitcast_fusion.1
  46.2 0.1 reshape.72
  46.4 11.5 %all_to_all.20 = f32[8,8,4,128]{3,0,2,1:T(8,128)S(1)} all-to-all(f32[8,8,4,128]{3,0,2,1:T(8,128)S(1)} %copy.47), channel_id=1, replica_groups=mesh['x'=4,'yh'=2,'z'=8,'ch'=4] {'z'}, dimensions={1} | all-to-all | bytes 262144 | tf_op jit(solution)/shard_map/all_to_all | solution.py:18
  57.8 0.1 copy.48
  57.9 10.5 %all_to_all.21 = f32[8,8,4,128]{3,1,2,0:T(8,128)S(1)} all-to-all(f32[8,8,4,128]{3,1,2,0:T(8,128)S(1)} %copy.48), channel_id=1, replica_groups=mesh['x'=4,'yh'=2,'z'=8,'ch'=4] {'x','yh'}, dimensions={0} | all-to-all | bytes 262144 | tf_op jit(solution)/shard_map/all_to_all | solution.py:19
  68.4 0.1 copy.51
  68.5 0.1 copy.52
  68.6 0.7 copy.53
  69.3 0.6 copy.50
  70.0 10.7 %psum.7 = f32[32,128]{1,0:T(8,128)} all-reduce(f32[32,128]{1,0:T(8,128)S(1)} %reduce_sum.39), channel_id=1, replica_groups=mesh['x'=4,'yh'=2,'z'=8,'ch'=4] {'ch'}, use_global_device_ids=true, to_apply=%region_4.5 | all-reduce | flops 4096 | bytes 32768 | tf_op jit(solution)/shard_map/psum | solution.py:156
  (24 shorter events, 0.3 us)
Async XLA Ops:
  0.6 0.8 copy-start.1
  1.4 0.8 copy-start
  2.9 17.0 %all-to-all-start = ((bf16[8,8,5,128]{3,0,2,1:T(8,128)(2,1)}), bf16[8,8,5,128]{3,0,2,1:T(8,128)(2,1)S(1)}, u32[]{:S(2)}, u32[]{:S(2)}) async-start(bf16[8,8,5,128]{3,0,2,1:T(8,128)(2,1)} %copy.44), calls=%async_computation | async-start | bytes 163840 | tf_op jit(solution)/shard_map/all_to_all | solution.py:18
  11.4 0.7 copy-start.2
  20.6 13.8 %all-to-all-start.1 = ((bf16[8,8,5,128]{3,1,2,0:T(8,128)(2,1)}), bf16[8,8,5,128]{3,1,2,0:T(8,128)(2,1)S(1)}, u32[]{:S(2)}, u32[]{:S(2)}) async-start(bf16[8,8,5,128]{3,1,2,0:T(8,128)(2,1)} %copy.45), calls=%async_computation.1 | async-start | bytes 163840 | tf_op jit(solution)/shard_map/all_to_all | solution.py:19

commit v2 on v0

--- a/solution.py
+++ b/solution.py
@@ -72,6 +72,64 @@
     return hidden.reshape(chans, total_len), long.reshape(total_len)
 
 
+def swap_kernel(send_ref, out_ref, landed, local_sem, send_sem, recv_sem):
+    count = send_ref.shape[0]
+    me = lax.axis_index("ctx")
+    mine = lax.axis_index("ch")
+    barrier = pltpu.get_barrier_semaphore()
+    for step in range(1, count):
+        peer = lax.rem(me + step, count)
+        pl.semaphore_signal(
+            barrier, 1, device_id=(peer, mine), device_id_type=pl.DeviceIdType.MESH
+        )
+    pl.semaphore_wait(barrier, count - 1)
+    local = pltpu.make_async_copy(send_ref.at[me], landed.at[me], local_sem)
+    local.start()
+    copies = []
+    for step in range(1, count):
+        peer = lax.rem(me + step, count)
+        copy = pltpu.make_async_remote_copy(
+            src_ref=send_ref.at[peer],
+            dst_ref=landed.at[me],
+            send_sem=send_sem.at[peer],
+            recv_sem=recv_sem.at[me],
+            device_id=(peer, mine),
+            device_id_type=pl.DeviceIdType.MESH,
+        )
+        copy.start()
+        copies.append(copy)
+    local.wait()
+    for copy in copies:
+        copy.wait_send()
+    for step in range(1, count):
+        source = lax.rem(me + step, count)
+        pltpu.make_async_remote_copy(
+            src_ref=send_ref.at[source],
+            dst_ref=landed.at[source],
+            send_sem=send_sem.at[source],
+            recv_sem=recv_sem.at[source],
+            device_id=(source, mine),
+            device_id_type=pl.DeviceIdType.MESH,
+        ).wait_recv()
+    out_ref[...] = landed[...]
+
+
+def swap(chunks, collective_id):
+    return pl.pallas_call(
+        swap_kernel,
+        out_shape=jax.ShapeDtypeStruct(chunks.shape, chunks.dtype),
+        in_specs=[pl.BlockSpec(memory_space=pltpu.VMEM)],
+        out_specs=pl.BlockSpec(memory_space=pltpu.VMEM),
+        scratch_shapes=[
+            pltpu.VMEM(chunks.shape, chunks.dtype),
+            pltpu.SemaphoreType.DMA,
+            pltpu.SemaphoreType.DMA((chunks.shape[0],)),
+            pltpu.SemaphoreType.DMA((chunks.shape[0],)),
+        ],
+        compiler_params=pltpu.CompilerParams(collective_id=collective_id, has_side_effects=True),
+    )(chunks)
+
+
 def per_device(inputs, short_filter, long_filter, grad_out):
     tap_count = short_filter.shape[0]
     filter_count, chan_count, shard_len = inputs.shape
@@ -91,7 +149,7 @@
         ],
         axis=1,
     )
-    recv = lax.all_to_all(send, "ctx", 0, 0, tiled=True)
+    recv = swap(send, 0)
     seqs = recv.transpose(1, 0, 2).reshape(2 * per_dev + 1, total_len)
     grad_seq = seqs[:per_dev]
     in_seq = seqs[per_dev : 2 * per_dev].astype(jnp.float32)
@@ -135,7 +193,7 @@
         ],
         axis=1,
     )
-    got = lax.all_to_all(back, "ctx", 0, 0, tiled=True)
+    got = swap(back, 1)
     grad_in_out = got[:, :per_dev].reshape(filter_count, chan_count, shard_len)
     grad_in_out = grad_in_out.astype(jnp.bfloat16)
     long_part = got[:, per_dev].reshape(filter_count, per_filter, shard_len).sum(axis=1)

time: 71.1 us -> 68.2 us (0.959)
  Pallas kernels: 10.1 us -> 46.7 us
  blocking collectives: 27.4 us -> 10.7 us
  starting transfers between devices: 13.7 us -> 0 us
  waiting for transfers between devices: 11.7 us -> 0 us
  local copies, waits for them, and re-layouts: 4.94 us -> 6.54 us
    pallas_call x0 -> x2, Pallas kernels: none -> 36.6 us  [swap(): pl.pallas_call(swap_kernel, out_shape=jax.ShapeDtypeStruct(chunks.shape,...]
    all_to_all x1 -> x0, blocking collectives: 16.7 us -> none  [per_device(): got = lax.all_to_all(back, 'ctx', 0, 0, tiled=True)]
    all_to_all x1 -> x0, starting transfers between devices: 13.7 us -> none  [per_device(): recv = lax.all_to_all(send, 'ctx', 0, 0, tiled=True)]
    all_to_all x1 -> x0, waiting for transfers between devices: 11.7 us -> none  [per_device(): recv = lax.all_to_all(send, 'ctx', 0, 0, tiled=True)]
    slice x2, local copies, waits for them, and re-layouts: 0.11 us -> 1.08 us  [per_device(): got[:, per_dev + 1, :tap_count * per_dev]]
    pallas_call x0 -> x1, local copies, waits for them, and re-layouts: none -> 0.92 us  [swap(): pl.pallas_call(swap_kernel, out_shape=jax.ShapeDtypeStruct(chunks.shape,...]
    concatenate x1, other arithmetic: 0.01 us -> 0.73 us  [per_device(): jnp.concatenate([grad_in.astype(jnp.float32).reshape(per_dev, ctx_count,...]
    unnamed x12 -> x15, local copies, waits for them, and re-layouts: 2.33 us -> 2.82 us
  transfers between devices with their start and end apart: 1 -> 0, of which waited for: 1 -> 0; matrix products, arithmetic and copies ran while one was open for 0% -> 0% of each run, Pallas kernels for 0% -> 0%
where the time goes in v2:
time: 68.2 us; the launch traced here: 67.2 us
  Pallas kernels  46.7 us (68%)
  blocking collectives  10.7 us (16%)
  local copies, waits for them, and re-layouts  6.54 us (10%)
  other arithmetic  2.45 us (4%)
  between operations  0.84 us (1%)
    pallas_call x2, Pallas kernels, swap(): pl.pallas_call(swap_kernel, out_shape=jax.ShapeDtypeStruct(chunks.shape,...  36.6 us
    psum x1, blocking collectives, per_device(): grad_long_out = lax.psum(long_part, 'ch')  10.7 us
    pallas_call x1, Pallas kernels, correlate_all(): pl.pallas_call(conv_kernel, out_shape=(jax.ShapeDtypeStruct((chans, block...  10.1 us
    unnamed x15, local copies, waits for them, and re-layouts  2.82 us

profile of v2, /device:TPU:8, one launch (start us, length us, event | category | flops | bytes accessed | tf_op | source)
XLA Modules:
  0.0 67.2 jit_solution(4752106588643079437)
XLA Ops:
  0.6 0.0 copy-start.4
  0.6 0.7 %copy-done.4 = f32[3,32,4]{1,2,0:T(4,128)S(1)} copy-done((f32[3,32,4]{1,2,0:T(4,128)S(1)}, f32[3,32,4]{1,2,0:T(4,128)}, u32[]{:S(2)}) %copy-start.4) | copy-done | bytes 1560
  1.3 0.1 copy.14
  1.4 0.0 copy-start.3
  1.5 0.2 slice_reduce_fusion.2
  1.6 0.5 copy-done.3
  2.1 0.0 copy-start.2
  2.2 0.0 copy-start.1
  2.2 0.7 %copy-done.2 = bf16[32,4,128]{2,1,0:T(4,128)(2,1)S(1)} copy-done((bf16[32,4,128]{2,1,0:T(4,128)(2,1)S(1)}, bf16[32,4,128]{2,1,0:T(4,128)(2,1)}, u32[]{:S(2)}) %copy-start.2) | copy-done | bytes 32792
  2.9 0.0 copy-done.1
  2.9 0.8 %pad_maximum_fusion.send_ref = bf16[64,5,128]{2,1,0:T(8,128)(2,1)} fusion(bf16[64,1,128]{2,1,0:T(2,128)(2,1)S(1)} %copy.15, bf16[64,2,128]{2,1,0:T(2,128)(2,1)S(1)} %bitcast.56, bf16[64,2,128]{2,1,0:T(2,128)(2,1)S(1)} %bitcast.57), kind=kLoop, calls=%fused_computation.2 | loop fusion | flops 245760 | bytes 163840 | tf_op jit(solution)/shard_map/concatenate | solution.py:144
  3.7 20.2 %shard_map.67 = bf16[64,5,128]{2,1,0:T(8,128)(2,1)} custom-call(bf16[64,5,128]{2,1,0:T(8,128)(2,1)} %pad_maximum_fusion.send_ref), custom_call_target="tpu_custom_call" | custom-call | tf_op jit(solution)/shard_map/pallas_call | solution.py:118
  23.9 0.9 %copy.31 = bf16[64,5,128]{2,0,1:T(8,128)(2,1)S(1)} copy(bf16[64,5,128]{2,1,0:T(8,128)(2,1)} %shard_map.67) | data formatting | bytes 163840 | tf_op jit(solution)/shard_map/pallas_call | solution.py:118
  24.8 0.1 copy.33
  24.9 0.2 fusion.5
  25.2 0.5 rev.3
  25.8 10.1 %shard_map.68 = (f32[2,64,128]{2,1,0:T(8,128)S(1)}, f32[64,128]{1,0:T(8,128)S(1)}) custom-call(f32[2,128,128]{2,1,0:T(8,128)S(1)} %pad_convert_fusion.grad_ref, f32[3,65,256]{2,1,0:T(8,128)S(1)} %convert_element_type.42.rev_ref), custom_call_target="tpu_custom_call" | custom-call | tf_op jit(solution)/shard_map/pallas_call | solution.py:60
  35.9 0.1 copy.32
  35.9 0.2 convert_bitcast_fusion.1
  36.2 0.3 multiply_reduce_fusion.1
  36.5 0.1 fusion.3
  36.6 0.1 reshape.58
  36.7 0.7 %pad_maximum_fusion.1.send_ref = f32[64,4,128]{2,1,0:T(4,128)} fusion(f32[64,1,128]{2,1,0:T(1,128)S(1)} %broadcast_in_dim.13, f32[64,1,128]{2,1,0:T(1,128)S(1)} %bitcast.44, f32[64,2,128]{2,1,0:T(2,128)S(1)} %convert_bitcast_fusion.1), kind=kLoop, calls=%fused_computation.3 | loop fusion | flops 65536 | bytes 262144 | tf_op jit(solution)/shard_map/concatenate | solution.py:188
  37.4 16.4 %shard_map.69 = f32[64,4,128]{2,1,0:T(4,128)} custom-call(f32[64,4,128]{2,1,0:T(4,128)} %pad_maximum_fusion.1.send_ref), custom_call_target="tpu_custom_call" | custom-call | tf_op jit(solution)/shard_map/pallas_call | solution.py:118
  53.8 0.0 copy-start
  53.8 1.0 %slice.72 = f32[64,1,6]{2,1,0:T(1,128)S(1)} slice(f32[64,4,128]{2,1,0:T(4,128)} %shard_map.69), slice={[0:64], [3:4], [0:6]} | slice | bytes 3072 | tf_op jit(solution)/shard_map/slice | solution.py:201
  54.9 0.1 copy.17
  54.9 0.1 copy.18
  55.1 0.7 %copy.19 = f32[3,32,4]{1,2,0:T(4,128)} copy(f32[3,32,4]{0,2,1:T(4,128)S(1)} %bitcast.51) | data formatting | bytes 3072
  55.8 0.0 copy-done
  55.9 10.7 %psum.7 = f32[32,128]{1,0:T(8,128)} all-reduce(f32[32,128]{1,0:T(8,128)S(1)} %reduce_sum.39), channel_id=1, replica_groups=mesh['ctx'=64,'ch'=4] {'ch'}, use_global_device_ids=true, to_apply=%region_4.5 | all-reduce | flops 4096 | bytes 32768 | tf_op jit(solution)/shard_map/psum | solution.py:200
  66.6 0.6 slice.105
  (17 shorter events, 0.3 us)
Async XLA Ops:
  0.6 0.7 %copy-start.4 = (f32[3,32,4]{1,2,0:T(4,128)S(1)}, f32[3,32,4]{1,2,0:T(4,128)}, u32[]{:S(2)}) copy-start(f32[3,32,4]{1,2,0:T(4,128)} %param.5) | copy-start | bytes 4612
  1.4 0.7 %copy-start.3 = (bf16[32,128]{1,0:T(8,128)(2,1)S(1)}, bf16[32,128]{1,0:T(8,128)(2,1)}, u32[]{:S(2)}) copy-start(bf16[32,128]{1,0:T(8,128)(2,1)} %param.6) | copy-start | bytes 24580
  2.1 0.8 %copy-start.2 = (bf16[32,4,128]{2,1,0:T(4,128)(2,1)S(1)}, bf16[32,4,128]{2,1,0:T(4,128)(2,1)}, u32[]{:S(2)}) copy-start(bf16[32,4,128]{2,1,0:T(4,128)(2,1)} %param.7) | copy-start | bytes 98308
  2.2 0.8 %copy-start.1 = (bf16[32,4,128]{2,1,0:T(4,128)(2,1)S(1)}, bf16[32,4,128]{2,1,0:T(4,128)(2,1)}, u32[]{:S(2)}) copy-start(bf16[32,4,128]{2,1,0:T(4,128)(2,1)} %param.4) | copy-start | bytes 98308
  53.8 1.9 %copy-start = (f32[64,4,128]{2,1,0:T(4,128)S(1)}, f32[64,4,128]{2,1,0:T(4,128)}, u32[]{:S(2)}) copy-start(f32[64,4,128]{2,1,0:T(4,128)} %shard_map.69) | copy-start | bytes 393220

commit v3 on v2

--- a/solution.py
+++ b/solution.py
@@ -130,6 +130,103 @@
     )(chunks)
 
 
+def gather_kernel(
+    rows_ref, long_ref, rows_out, long_out, rows_in, long_in, local_sems,
+    rows_send, rows_recv, long_send, long_recv,
+):
+    count = rows_ref.shape[0]
+    groups = lax.axis_size("ch")
+    me = lax.axis_index("ctx")
+    mine = lax.axis_index("ch")
+    mesh_id = pl.DeviceIdType.MESH
+    peers = [(c, h) for c in range(count) for h in range(groups) if (c, h) != (0, 0)]
+    barrier = pltpu.get_barrier_semaphore()
+    for step_c, step_h in peers:
+        peer, other = lax.rem(me + step_c, count), lax.rem(mine + step_h, groups)
+        pl.semaphore_signal(barrier, 1, device_id=(peer, other), device_id_type=mesh_id)
+    pl.semaphore_wait(barrier, len(peers))
+    local_rows = pltpu.make_async_copy(rows_ref.at[me], rows_in.at[me], local_sems.at[0])
+    local_long = pltpu.make_async_copy(long_ref.at[me], long_in.at[me, mine], local_sems.at[1])
+    local_rows.start()
+    local_long.start()
+    copies = []
+    for step in range(1, count):
+        peer = lax.rem(me + step, count)
+        copy = pltpu.make_async_remote_copy(
+            src_ref=rows_ref.at[peer],
+            dst_ref=rows_in.at[me],
+            send_sem=rows_send.at[peer],
+            recv_sem=rows_recv.at[me],
+            device_id=(peer, mine),
+            device_id_type=mesh_id,
+        )
+        copy.start()
+        copies.append(copy)
+    for step_c, step_h in peers:
+        peer, other = lax.rem(me + step_c, count), lax.rem(mine + step_h, groups)
+        copy = pltpu.make_async_remote_copy(
+            src_ref=long_ref.at[peer],
+            dst_ref=long_in.at[me, mine],
+            send_sem=long_send.at[peer * groups + other],
+            recv_sem=long_recv.at[me * groups + mine],
+            device_id=(peer, other),
+            device_id_type=mesh_id,
+        )
+        copy.start()
+        copies.append(copy)
+    local_rows.wait()
+    local_long.wait()
+    for copy in copies:
+        copy.wait_send()
+    for step in range(1, count):
+        source = lax.rem(me + step, count)
+        pltpu.make_async_remote_copy(
+            src_ref=rows_ref.at[source],
+            dst_ref=rows_in.at[source],
+            send_sem=rows_send.at[source],
+            recv_sem=rows_recv.at[source],
+            device_id=(source, mine),
+            device_id_type=mesh_id,
+        ).wait_recv()
+    for step_c, step_h in peers:
+        source, other = lax.rem(me + step_c, count), lax.rem(mine + step_h, groups)
+        pltpu.make_async_remote_copy(
+            src_ref=long_ref.at[source],
+            dst_ref=long_in.at[source, other],
+            send_sem=long_send.at[source * groups + other],
+            recv_sem=long_recv.at[source * groups + other],
+            device_id=(source, other),
+            device_id_type=mesh_id,
+        ).wait_recv()
+    rows_out[...] = rows_in[...]
+    long_out[...] = long_in[...]
+
+
+def gather(rows, longs, groups, collective_id):
+    count = rows.shape[0]
+    long_shape = (count, groups) + longs.shape[1:]
+    vmem = pl.BlockSpec(memory_space=pltpu.VMEM)
+    return pl.pallas_call(
+        gather_kernel,
+        out_shape=(
+            jax.ShapeDtypeStruct(rows.shape, rows.dtype),
+            jax.ShapeDtypeStruct(long_shape, longs.dtype),
+        ),
+        in_specs=[vmem, vmem],
+        out_specs=(vmem, vmem),
+        scratch_shapes=[
+            pltpu.VMEM(rows.shape, rows.dtype),
+            pltpu.VMEM(long_shape, longs.dtype),
+            pltpu.SemaphoreType.DMA((2,)),
+            pltpu.SemaphoreType.DMA((count,)),
+            pltpu.SemaphoreType.DMA((count,)),
+            pltpu.SemaphoreType.DMA((count * groups,)),
+            pltpu.SemaphoreType.DMA((count * groups,)),
+        ],
+        compiler_params=pltpu.CompilerParams(collective_id=collective_id, has_side_effects=True),
+    )(rows, longs)
+
+
 def per_device(inputs, short_filter, long_filter, grad_out):
     tap_count = short_filter.shape[0]
     filter_count, chan_count, shard_len = inputs.shape
@@ -188,17 +285,16 @@
     back = jnp.concatenate(
         [
             grad_in.astype(jnp.float32).reshape(per_dev, ctx_count, shard_len).transpose(1, 0, 2),
-            grad_long.reshape(ctx_count, 1, shard_len),
             jnp.broadcast_to(short_row[None], (ctx_count, 1, shard_len)),
         ],
         axis=1,
     )
-    got = swap(back, 1)
+    groups = lax.axis_size("ch")
+    got, got_long = gather(back, grad_long.reshape(ctx_count, 1, shard_len), groups, 1)
     grad_in_out = got[:, :per_dev].reshape(filter_count, chan_count, shard_len)
     grad_in_out = grad_in_out.astype(jnp.bfloat16)
-    long_part = got[:, per_dev].reshape(filter_count, per_filter, shard_len).sum(axis=1)
-    grad_long_out = lax.psum(long_part, "ch")
-    short_all = got[:, per_dev + 1, : tap_count * per_dev].reshape(ctx_count, tap_count, per_dev)
+    grad_long_out = got_long.reshape(filter_count, per_filter * groups, shard_len).sum(axis=1)
+    short_all = got[:, per_dev, : tap_count * per_dev].reshape(ctx_count, tap_count, per_dev)
     grad_short_out = short_all.transpose(1, 0, 2).reshape(tap_count, filter_count, chan_count)
     return (grad_in_out, grad_long_out, grad_short_out)
 

time: 68.2 us -> 69 us (1.012)
  the two profiles are of different devices: /device:TPU:8 before, /device:TPU:1 now
where the time goes in v3:
time: 69 us; the launch traced here: 68.7 us
  Pallas kernels  56.8 us (82%)
  local copies, waits for them, and re-layouts  7.92 us (11%)
  other arithmetic  3.16 us (5%)
  between operations  0.84 us (1%)
    pallas_call x1, Pallas kernels, gather(): pl.pallas_call(gather_kernel, out_shape=(jax.ShapeDtypeStruct(rows.shape,...  26.2 us
    pallas_call x1, Pallas kernels, swap(): pl.pallas_call(swap_kernel, out_shape=jax.ShapeDtypeStruct(chunks.shape,...  20.5 us
    pallas_call x1, Pallas kernels, correlate_all(): pl.pallas_call(conv_kernel, out_shape=(jax.ShapeDtypeStruct((chans, block...  10.1 us
    unnamed x17, local copies, waits for them, and re-layouts  3.37 us
    slice x1, local copies, waits for them, and re-layouts, per_device(): grad_in_out = got[:, :per_dev].reshape(filter_count, chan_count, shard_len)  1.54 us

profile of v3, /device:TPU:1, one launch (start us, length us, event | category | flops | bytes accessed | tf_op | source)
XLA Modules:
  0.0 68.7 jit_solution(14235005585962785246)
XLA Ops:
  0.6 0.0 copy-start.5
  0.6 0.7 copy-done.5
  1.3 0.1 copy.26
  1.5 0.2 slice_reduce_fusion.2
  1.6 0.5 copy-done.4
  2.2 0.0 copy-start.2
  2.2 0.7 %copy-done.3 = bf16[32,4,128]{2,1,0:T(4,128)(2,1)S(1)} copy-done((bf16[32,4,128]{2,1,0:T(4,128)(2,1)S(1)}, bf16[32,4,128]{2,1,0:T(4,128)(2,1)}, u32[]{:S(2)}) %copy-start.3) | copy-done | bytes 32792
  2.9 0.0 copy-done.2
  2.9 0.8 %pad_maximum_fusion.send_ref = bf16[64,5,128]{2,1,0:T(8,128)(2,1)} fusion(bf16[64,1,128]{2,1,0:T(2,128)(2,1)S(1)} %copy.27, bf16[64,2,128]{2,1,0:T(2,128)(2,1)S(1)} %bitcast.56, bf16[64,2,128]{2,1,0:T(2,128)(2,1)S(1)} %bitcast.57), kind=kLoop, calls=%fused_computation.2 | loop fusion | flops 245760 | bytes 163840 | tf_op jit(solution)/shard_map/concatenate | solution.py:241
  3.7 20.5 %shard_map.67 = bf16[64,5,128]{2,1,0:T(8,128)(2,1)} custom-call(bf16[64,5,128]{2,1,0:T(8,128)(2,1)} %pad_maximum_fusion.send_ref), custom_call_target="tpu_custom_call" | custom-call | tf_op jit(solution)/shard_map/pallas_call | solution.py:118
  24.2 0.9 %copy.45 = bf16[64,5,128]{2,0,1:T(8,128)(2,1)S(1)} copy(bf16[64,5,128]{2,1,0:T(8,128)(2,1)} %shard_map.67) | data formatting | bytes 163840 | tf_op jit(solution)/shard_map/pallas_call | solution.py:118
  25.1 0.1 copy.47
  25.2 0.2 fusion.5
  25.5 0.5 rev.3
  26.1 10.1 %shard_map.68 = (f32[2,64,128]{2,1,0:T(8,128)S(1)}, f32[64,128]{1,0:T(8,128)S(1)}) custom-call(f32[2,128,128]{2,1,0:T(8,128)S(1)} %pad_convert_fusion.grad_ref, f32[3,65,256]{2,1,0:T(8,128)S(1)} %convert_element_type.42.rev_ref), custom_call_target="tpu_custom_call" | custom-call | tf_op jit(solution)/shard_map/pallas_call | solution.py:60
  36.2 0.0 copy-start
  36.2 0.1 copy.46
  36.3 0.5 copy-done
  36.8 0.2 convert_bitcast_fusion.1
  37.0 0.3 multiply_reduce_fusion.1
  37.3 0.1 fusion.3
  37.5 0.1 reshape.60
  37.6 0.7 %pad_maximum_fusion.1.rows_ref = f32[64,3,128]{2,1,0:T(4,128)} fusion(f32[64,1,128]{2,1,0:T(1,128)S(1)} %broadcast_in_dim.13, f32[64,2,128]{2,1,0:T(2,128)S(1)} %convert_bitcast_fusion.1), kind=kLoop, calls=%fused_computation.3 | loop fusion | flops 24576 | bytes 196608 | tf_op jit(solution)/shard_map/concatenate | solution.py:285
  38.3 26.2 %shard_map.69 = (f32[64,3,128]{2,1,0:T(4,128)}, f32[64,4,1,128]{3,2,1,0:T(1,128)}) custom-call(f32[64,3,128]{2,1,0:T(4,128)} %pad_maximum_fusion.1.rows_ref, f32[64,1,128]{2,1,0:T(1,128)} %bitcast.44), custom_call_target="tpu_custom_call" | custom-call | tf_op jit(solution)/shard_map/pallas_call | solution.py:209
  64.5 0.0 copy-start.1
  64.5 1.0 %slice.68 = f32[64,1,6]{2,1,0:T(1,128)S(1)} slice(f32[64,3,128]{2,1,0:T(4,128)} %get-tuple-element.9), slice={[0:64], [2:3], [0:6]} | slice | bytes 3072 | tf_op jit(solution)/shard_map/slice | solution.py:297
  65.5 0.1 copy.30
  65.6 0.1 copy.31
  65.7 0.7 %copy.32 = f32[3,32,4]{1,2,0:T(4,128)} copy(f32[3,32,4]{0,2,1:T(4,128)S(1)} %bitcast.51) | data formatting | bytes 3072
  66.4 0.1 reduce_sum.46
  66.5 0.6 reduce_sum.48
  67.2 1.5 %slice.101 = bf16[64,2,128]{2,1,0:T(2,128)(2,1)} slice(f32[64,3,128]{2,1,0:T(4,128)} %get-tuple-element.9), slice={[0:64], [0:2], [0:128]} | slice | bytes 65536 | tf_op jit(solution)/shard_map/slice | solution.py:294
  (18 shorter events, 0.2 us)
Async XLA Ops:
  0.6 0.7 %copy-start.5 = (f32[3,32,4]{1,2,0:T(4,128)S(1)}, f32[3,32,4]{1,2,0:T(4,128)}, u32[]{:S(2)}) copy-start(f32[3,32,4]{1,2,0:T(4,128)} %param.5) | copy-start | bytes 4612
  1.4 0.7 %copy-start.4 = (bf16[32,128]{1,0:T(8,128)(2,1)S(1)}, bf16[32,128]{1,0:T(8,128)(2,1)}, u32[]{:S(2)}) copy-start(bf16[32,128]{1,0:T(8,128)(2,1)} %param.6) | copy-start | bytes 24580
  2.1 0.8 %copy-start.3 = (bf16[32,4,128]{2,1,0:T(4,128)(2,1)S(1)}, bf16[32,4,128]{2,1,0:T(4,128)(2,1)}, u32[]{:S(2)}) copy-start(bf16[32,4,128]{2,1,0:T(4,128)(2,1)} %param.7) | copy-start | bytes 98308
  2.2 0.8 %copy-start.2 = (bf16[32,4,128]{2,1,0:T(4,128)(2,1)S(1)}, bf16[32,4,128]{2,1,0:T(4,128)(2,1)}, u32[]{:S(2)}) copy-start(bf16[32,4,128]{2,1,0:T(4,128)(2,1)} %param.4) | copy-start | bytes 98308
  36.2 0.6 copy-start
  64.5 1.9 %copy-start.1 = (f32[64,4,1,128]{3,2,1,0:T(1,128)S(1)}, f32[64,4,1,128]{3,2,1,0:T(1,128)}, u32[]{:S(2)}) copy-start(f32[64,4,1,128]{3,2,1,0:T(1,128)} %get-tuple-element.10) | copy-start | bytes 393220

commit v4 on v3

--- a/solution.py
+++ b/solution.py
@@ -227,6 +227,187 @@
     )(rows, longs)
 
 
+def fused_kernel(
+    grad_ref, rev_ref, in_ref, taps_ref, rows_out, long_out,
+    hankel, toeplitz, grad_buf, rows_buf, long_buf, rows_in, long_in, local_sems,
+    rows_send, rows_recv, long_send, long_recv,
+):
+    count = rows_buf.shape[0]
+    chans, _, block_len = grad_ref.shape
+    block_count = count
+    sources, lags, _ = rev_ref.shape
+    tap_count = taps_ref.shape[0]
+    groups = lax.axis_size("ch")
+    me = lax.axis_index("ctx")
+    mine = lax.axis_index("ch")
+    mesh_id = pl.DeviceIdType.MESH
+    peers = [(c, h) for c in range(count) for h in range(groups) if (c, h) != (0, 0)]
+    barrier = pltpu.get_barrier_semaphore()
+    for step_c, step_h in peers:
+        peer, other = lax.rem(me + step_c, count), lax.rem(mine + step_h, groups)
+        pl.semaphore_signal(barrier, 1, device_id=(peer, other), device_id_type=mesh_id)
+
+    def fill_hankel(lag, carry):
+        col = pl.multiple_of(lag * block_len, block_len)
+        for g in range(chans):
+            hankel[g, :, pl.ds(col, block_len)] = grad_ref[g, pl.ds(lag, block_count), :].astype(
+                hankel.dtype
+            )
+        return carry
+
+    lax.fori_loop(0, lags, fill_hankel, 0)
+
+    def fill_toeplitz(lag, carry):
+        row = pl.multiple_of(lag * block_len, block_len)
+        for s in range(sources):
+            line = rev_ref[s, pl.ds(lag, 1), :]
+            tiled = jnp.broadcast_to(line, (block_len, 2 * block_len))
+            skewed = pltpu.roll(tiled, block_len + 1, 1, stride=1, stride_axis=0)
+            toeplitz[s, pl.ds(row, block_len), :] = skewed[:, :block_len].astype(toeplitz.dtype)
+        return carry
+
+    lax.fori_loop(0, lags, fill_toeplitz, 0)
+
+    acc = jnp.dot(hankel[0], toeplitz[1], preferred_element_type=jnp.float32)
+    for g in range(1, chans):
+        acc = acc + jnp.dot(hankel[g], toeplitz[1 + g], preferred_element_type=jnp.float32)
+    long_buf[:, 0, :] = acc
+
+    lane = lax.broadcasted_iota(jnp.int32, (block_count, block_len), 1)
+    short_row = jnp.zeros((block_count, block_len), jnp.float32)
+    grad_buf[...] = jnp.zeros_like(grad_buf)
+    for g in range(chans):
+        hidden_grad = jnp.dot(hankel[g], toeplitz[0], preferred_element_type=jnp.float32)
+        grad_buf[g, pl.ds(0, block_count), :] = hidden_grad
+        following = grad_buf[g, pl.ds(1, block_count), :]
+        total = taps_ref[0, g] * hidden_grad
+        for offset in range(1, tap_count):
+            here = pltpu.roll(hidden_grad, block_len - offset, 1)
+            there = pltpu.roll(following, block_len - offset, 1)
+            total = total + taps_ref[offset, g] * jnp.where(
+                lane >= block_len - offset, there, here
+            )
+        rows_buf[:, g, :] = total.astype(jnp.bfloat16).astype(jnp.float32)
+        current = in_ref[g, pl.ds(1, block_count), :]
+        previous = in_ref[g, pl.ds(0, block_count), :]
+        for offset in range(tap_count):
+            if offset == 0:
+                delayed_in = current
+            else:
+                delayed_in = jnp.where(
+                    lane < offset,
+                    pltpu.roll(previous, offset, 1),
+                    pltpu.roll(current, offset, 1),
+                )
+            value = jnp.sum(hidden_grad * delayed_in)
+            short_row = jnp.where(lane == offset * chans + g, value, short_row)
+    rows_buf[:, chans, :] = short_row
+
+    pl.semaphore_wait(barrier, len(peers))
+    local_rows = pltpu.make_async_copy(rows_buf.at[me], rows_in.at[me], local_sems.at[0])
+    local_long = pltpu.make_async_copy(long_buf.at[me], long_in.at[me, mine], local_sems.at[1])
+    local_rows.start()
+    local_long.start()
+    copies = []
+    for step in range(1, count):
+        peer = lax.rem(me + step, count)
+        copy = pltpu.make_async_remote_copy(
+            src_ref=rows_buf.at[peer],
+            dst_ref=rows_in.at[me],
+            send_sem=rows_send.at[peer],
+            recv_sem=rows_recv.at[me],
+            device_id=(peer, mine),
+            device_id_type=mesh_id,
+        )
+        copy.start()
+        copies.append(copy)
+    for step_c, step_h in peers:
+        peer, other = lax.rem(me + step_c, count), lax.rem(mine + step_h, groups)
+        copy = pltpu.make_async_remote_copy(
+            src_ref=long_buf.at[peer],
+            dst_ref=long_in.at[me, mine],
+            send_sem=long_send.at[peer * groups + other],
+            recv_sem=long_recv.at[me * groups + mine],
+            device_id=(peer, other),
+            device_id_type=mesh_id,
+        )
+        copy.start()
+        copies.append(copy)
+    local_rows.wait()
+    local_long.wait()
+    for copy in copies:
+        copy.wait_send()
+    for step in range(1, count):
+        source = lax.rem(me + step, count)
+        pltpu.make_async_remote_copy(
+            src_ref=rows_buf.at[source],
+            dst_ref=rows_in.at[source],
+            send_sem=rows_send.at[source],
+            recv_sem=rows_recv.at[source],
+            device_id=(source, mine),
+            device_id_type=mesh_id,
+        ).wait_recv()
+    for step_c, step_h in peers:
+        source, other = lax.rem(me + step_c, count), lax.rem(mine + step_h, groups)
+        pltpu.make_async_remote_copy(
+            src_ref=long_buf.at[source],
+            dst_ref=long_in.at[source, other],
+            send_sem=long_send.at[source * groups + other],
+            recv_sem=long_recv.at[source * groups + other],
+            device_id=(source, other),
+            device_id_type=mesh_id,
+        ).wait_recv()
+    rows_out[...] = rows_in[...]
+    long_out[...] = long_in[...]
+
+
+def fused(grad_seq, sources, in_seq, taps, groups, block_len, collective_id):
+    chans, total_len = grad_seq.shape
+    count = sources.shape[0]
+    block_count = total_len // block_len
+    grad_pad = jnp.pad(
+        grad_seq.astype(jnp.float32).reshape(chans, block_count, block_len),
+        ((0, 0), (0, block_count), (0, 0)),
+    )
+    blocks = sources.reshape(count, block_count, block_len)
+    padded = jnp.pad(blocks, ((0, 0), (1, 1), (0, 0)))
+    pairs = jnp.concatenate([padded[:, :-1], padded[:, 1:]], axis=2)
+    rev = pairs[..., ::-1].astype(jnp.float32)
+    in_pad = jnp.pad(in_seq.reshape(chans, block_count, block_len), ((0, 0), (1, 0), (0, 0)))
+    lags = block_count + 1
+    rows_shape = (block_count, chans + 1, block_len)
+    long_shape = (block_count, groups, 1, block_len)
+    vmem = pl.BlockSpec(memory_space=pltpu.VMEM)
+    return pl.pallas_call(
+        fused_kernel,
+        out_shape=(
+            jax.ShapeDtypeStruct(rows_shape, jnp.float32),
+            jax.ShapeDtypeStruct(long_shape, jnp.float32),
+        ),
+        in_specs=[vmem, vmem, vmem, pl.BlockSpec(memory_space=pltpu.SMEM)],
+        out_specs=(vmem, vmem),
+        scratch_shapes=[
+            pltpu.VMEM((chans, block_count, lags * block_len), jnp.bfloat16),
+            pltpu.VMEM((count, lags * block_len, block_len), jnp.bfloat16),
+            pltpu.VMEM((chans, block_count + 8, block_len), jnp.float32),
+            pltpu.VMEM(rows_shape, jnp.float32),
+            pltpu.VMEM((block_count, 1, block_len), jnp.float32),
+            pltpu.VMEM(rows_shape, jnp.float32),
+            pltpu.VMEM(long_shape, jnp.float32),
+            pltpu.SemaphoreType.DMA((2,)),
+            pltpu.SemaphoreType.DMA((block_count,)),
+            pltpu.SemaphoreType.DMA((block_count,)),
+            pltpu.SemaphoreType.DMA((block_count * groups,)),
+            pltpu.SemaphoreType.DMA((block_count * groups,)),
+        ],
+        compiler_params=pltpu.CompilerParams(
+            collective_id=collective_id,
+            has_side_effects=True,
+            vmem_limit_bytes=48 * 1024 * 1024,
+        ),
+    )(grad_pad, rev, in_pad, taps)
+
+
 def per_device(inputs, short_filter, long_filter, grad_out):
     tap_count = short_filter.shape[0]
     filter_count, chan_count, shard_len = inputs.shape
@@ -259,38 +440,16 @@
     )
     hidden = hidden.astype(jnp.bfloat16)
 
-    grad_hidden, grad_long = correlate_all(
-        grad_seq, jnp.concatenate([filt_seq, hidden], axis=0), block_len
-    )
-
-    padded_grad = jnp.pad(grad_hidden, ((0, 0), (0, tap_count - 1)))
-    grad_in = sum(
-        (
-            taps[offset][:, None] * padded_grad[:, offset : offset + total_len]
-            for offset in range(tap_count)
-        )
-    )
-    grad_in = grad_in.astype(jnp.bfloat16)
-    grad_short = jnp.stack(
-        [
-            jnp.sum(grad_hidden * delayed(in_seq, offset, total_len), axis=1)
-            for offset in range(tap_count)
-        ]
-    )
-
-    short_row = jnp.pad(
-        grad_short.reshape(1, tap_count * per_dev),
-        ((0, 0), (0, shard_len - tap_count * per_dev)),
-    )
-    back = jnp.concatenate(
-        [
-            grad_in.astype(jnp.float32).reshape(per_dev, ctx_count, shard_len).transpose(1, 0, 2),
-            jnp.broadcast_to(short_row[None], (ctx_count, 1, shard_len)),
-        ],
-        axis=1,
-    )
     groups = lax.axis_size("ch")
-    got, got_long = gather(back, grad_long.reshape(ctx_count, 1, shard_len), groups, 1)
+    got, got_long = fused(
+        grad_seq,
+        jnp.concatenate([filt_seq, hidden], axis=0),
+        in_seq,
+        taps,
+        groups,
+        block_len,
+        1,
+    )
     grad_in_out = got[:, :per_dev].reshape(filter_count, chan_count, shard_len)
     grad_in_out = grad_in_out.astype(jnp.bfloat16)
     grad_long_out = got_long.reshape(filter_count, per_filter * groups, shard_len).sum(axis=1)

time: 69 us -> 60.3 us (0.87)
  Pallas kernels: 56.8 us -> 52.1 us
  local copies, waits for them, and re-layouts: 7.92 us -> 5.25 us
  other arithmetic: 3.16 us -> 1.84 us
    pallas_call x2 -> x1, Pallas kernels: 36.3 us -> 31.6 us  [fused(): pl.pallas_call(fused_kernel, out_shape=(jax.ShapeDtypeStruct(rows_shape,...]
    slice x2, local copies, waits for them, and re-layouts: 1.05 us -> 0.11 us  [per_device(): got[:, per_dev, :tap_count * per_dev].reshape(ctx_count, tap_count, per_dev)]
    slice x1, local copies, waits for them, and re-layouts: 1.54 us -> 0.64 us  [per_device(): grad_in_out = got[:, :per_dev].reshape(filter_count, chan_count, shard_len)]
    unnamed x17 -> x12, local copies, waits for them, and re-layouts: 3.37 us -> 2.56 us
    concatenate x2 -> x1, other arithmetic: 0.72 us -> 0.02 us  [fused(): pairs = jnp.concatenate([padded[:, :-1], padded[:, 1:]], axis=2)]
where the time goes in v4:
time: 60.3 us; the launch traced here: 60 us
  Pallas kernels  52.1 us (86%)
  local copies, waits for them, and re-layouts  5.25 us (9%)
  other arithmetic  1.84 us (3%)
  between operations  0.8 us (1%)
    pallas_call x1, Pallas kernels, fused(): pl.pallas_call(fused_kernel, out_shape=(jax.ShapeDtypeStruct(rows_shape,...  31.6 us
    pallas_call x1, Pallas kernels, swap(): pl.pallas_call(swap_kernel, out_shape=jax.ShapeDtypeStruct(chunks.shape,...  20.5 us
    unnamed x12, local copies, waits for them, and re-layouts  2.56 us

profile of v4, /device:TPU:1, one launch (start us, length us, event | category | flops | bytes accessed | tf_op | source)
XLA Modules:
  0.0 60.0 jit_solution(4699783313355090157)
XLA Ops:
  0.6 0.0 copy-start.2
  0.6 0.7 %copy-done.2 = bf16[32,128]{1,0:T(8,128)(2,1)S(1)} copy-done((bf16[32,128]{1,0:T(8,128)(2,1)S(1)}, bf16[32,128]{1,0:T(8,128)(2,1)}, u32[]{:S(2)}) %copy-start.2) | copy-done | bytes 8216
  1.3 0.0 copy-start.3
  1.4 0.6 %copy-done.3 = f32[3,32,4]{1,2,0:T(4,128)S(1)} copy-done((f32[3,32,4]{1,2,0:T(4,128)S(1)}, f32[3,32,4]{1,2,0:T(4,128)}, u32[]{:S(2)}) %copy-start.3) | copy-done | bytes 1560
  2.0 0.0 copy-start
  2.0 0.0 copy-start.1
  2.0 0.1 copy.25
  2.2 0.2 slice_reduce_fusion.2
  2.4 0.1 copy.26.taps_ref
  2.5 0.3 copy-done
  2.8 0.0 copy-done.1
  2.8 0.8 %pad_maximum_fusion.send_ref = bf16[64,5,128]{2,1,0:T(8,128)(2,1)} fusion(bf16[64,1,128]{2,1,0:T(2,128)(2,1)S(1)} %copy.23, bf16[64,2,128]{2,1,0:T(2,128)(2,1)S(1)} %bitcast.34, bf16[64,2,128]{2,1,0:T(2,128)(2,1)S(1)} %bitcast.35), kind=kLoop, calls=%fused_computation.2 | loop fusion | flops 245760 | bytes 163840 | tf_op jit(solution)/shard_map/concatenate | solution.py:422
  3.6 20.5 %shard_map.67 = bf16[64,5,128]{2,1,0:T(8,128)(2,1)} custom-call(bf16[64,5,128]{2,1,0:T(8,128)(2,1)} %pad_maximum_fusion.send_ref), custom_call_target="tpu_custom_call" | custom-call | tf_op jit(solution)/shard_map/pallas_call | solution.py:118
  24.1 0.9 %copy.37 = bf16[64,5,128]{2,0,1:T(8,128)(2,1)S(1)} copy(bf16[64,5,128]{2,1,0:T(8,128)(2,1)} %shard_map.67) | data formatting | bytes 163840 | tf_op jit(solution)/shard_map/pallas_call | solution.py:118
  25.1 0.1 copy.38
  25.1 0.2 fusion.9
  25.4 0.5 rev.3
  26.0 31.6 %shard_map.68 = (f32[64,3,128]{2,1,0:T(4,128)S(1)}, f32[64,4,1,128]{3,2,1,0:T(1,128)S(1)}) custom-call(f32[2,128,128]{2,1,0:T(8,128)S(1)} %pad_convert_fusion.grad_ref, f32[3,65,256]{2,1,0:T(8,128)S(1)} %convert_element_type.32.rev_ref, f32[2,65,128]{2,1,0:T(8,128)S(1)} %pad_convert_fusion.1.in_ref, f32[3,2]{1,0:T(4,128)S(1)} %copy.26.taps_ref), custom_call_target="tpu_custom_call" | custom-call | tf_op jit(solution)/shard_map/pallas_call | solution.py:381
  57.6 0.1 reduce_sum.10
  57.8 0.6 %reduce_sum.18 = f32[32,128]{1,0:T(8,128)} reduce(f32[32,2,128]{2,1,0:T(2,128)S(1)} %bitcast.30, f32[]{:T(128)} %constant.18.clone.1), dimensions={1}, to_apply=%region_1.2 | reduce | flops 4096 | bytes 49156 | tf_op jit(solution)/shard_map/reduce_sum | solution.py:455
  58.4 0.6 %slice.86 = bf16[64,2,128]{2,1,0:T(2,128)(2,1)} slice(f32[64,3,128]{2,1,0:T(4,128)S(1)} %get-tuple-element.5), slice={[0:64], [0:2], [0:128]} | slice | bytes 65536 | tf_op jit(solution)/shard_map/slice | solution.py:453
  59.1 0.1 copy.28
  59.2 0.1 copy.29
  59.3 0.7 %copy.30 = f32[3,32,4]{1,2,0:T(4,128)} copy(f32[3,32,4]{0,2,1:T(4,128)S(1)} %bitcast.28) | data formatting | bytes 3072
  (15 shorter events, 0.2 us)
Async XLA Ops:
  0.6 0.7 %copy-start.2 = (bf16[32,128]{1,0:T(8,128)(2,1)S(1)}, bf16[32,128]{1,0:T(8,128)(2,1)}, u32[]{:S(2)}) copy-start(bf16[32,128]{1,0:T(8,128)(2,1)} %param.6) | copy-start | bytes 24580
  1.3 0.7 %copy-start.3 = (f32[3,32,4]{1,2,0:T(4,128)S(1)}, f32[3,32,4]{1,2,0:T(4,128)}, u32[]{:S(2)}) copy-start(f32[3,32,4]{1,2,0:T(4,128)} %param.5) | copy-start | bytes 4612
  2.0 0.8 %copy-start = (bf16[32,4,128]{2,1,0:T(4,128)(2,1)S(1)}, bf16[32,4,128]{2,1,0:T(4,128)(2,1)}, u32[]{:S(2)}) copy-start(bf16[32,4,128]{2,1,0:T(4,128)(2,1)} %param.4) | copy-start | bytes 98308
  2.0 0.8 %copy-start.1 = (bf16[32,4,128]{2,1,0:T(4,128)(2,1)S(1)}, bf16[32,4,128]{2,1,0:T(4,128)(2,1)}, u32[]{:S(2)}) copy-start(bf16[32,4,128]{2,1,0:T(4,128)(2,1)} %param.7) | copy-start | bytes 98308

commit v5 on v4

--- a/solution.py
+++ b/solution.py
@@ -228,9 +228,9 @@
 
 
 def fused_kernel(
-    grad_ref, rev_ref, in_ref, taps_ref, rows_out, long_out,
-    hankel, toeplitz, grad_buf, rows_buf, long_buf, rows_in, long_in, local_sems,
-    rows_send, rows_recv, long_send, long_recv,
+    grad_ref, rev_ref, in_ref, taps_ref, rows_out,
+    hankel, toeplitz, grad_buf, rows_buf, ch_in, rows_in, local_sems,
+    rows_send, rows_recv, ch_send, ch_recv,
 ):
     count = rows_buf.shape[0]
     chans, _, block_len = grad_ref.shape
@@ -241,7 +241,7 @@
     me = lax.axis_index("ctx")
     mine = lax.axis_index("ch")
     mesh_id = pl.DeviceIdType.MESH
-    peers = [(c, h) for c in range(count) for h in range(groups) if (c, h) != (0, 0)]
+    peers = [(c, 0) for c in range(1, count)] + [(0, h) for h in range(1, groups)]
     barrier = pltpu.get_barrier_semaphore()
     for step_c, step_h in peers:
         peer, other = lax.rem(me + step_c, count), lax.rem(mine + step_h, groups)
@@ -271,7 +271,7 @@
     acc = jnp.dot(hankel[0], toeplitz[1], preferred_element_type=jnp.float32)
     for g in range(1, chans):
         acc = acc + jnp.dot(hankel[g], toeplitz[1 + g], preferred_element_type=jnp.float32)
-    long_buf[:, 0, :] = acc
+    ch_in[mine] = acc
 
     lane = lax.broadcasted_iota(jnp.int32, (block_count, block_len), 1)
     short_row = jnp.zeros((block_count, block_len), jnp.float32)
@@ -304,10 +304,38 @@
     rows_buf[:, chans, :] = short_row
 
     pl.semaphore_wait(barrier, len(peers))
+    partials = []
+    for step in range(1, groups):
+        other = lax.rem(mine + step, groups)
+        copy = pltpu.make_async_remote_copy(
+            src_ref=ch_in.at[mine],
+            dst_ref=ch_in.at[mine],
+            send_sem=ch_send.at[other],
+            recv_sem=ch_recv.at[mine],
+            device_id=(me, other),
+            device_id_type=mesh_id,
+        )
+        copy.start()
+        partials.append(copy)
+    for copy in partials:
+        copy.wait_send()
+    for step in range(1, groups):
+        source = lax.rem(mine + step, groups)
+        pltpu.make_async_remote_copy(
+            src_ref=ch_in.at[source],
+            dst_ref=ch_in.at[source],
+            send_sem=ch_send.at[source],
+            recv_sem=ch_recv.at[source],
+            device_id=(me, source),
+            device_id_type=mesh_id,
+        ).wait_recv()
+    summed = ch_in[0]
+    for h in range(1, groups):
+        summed = summed + ch_in[h]
+    rows_buf[:, chans + 1, :] = summed
+
     local_rows = pltpu.make_async_copy(rows_buf.at[me], rows_in.at[me], local_sems.at[0])
-    local_long = pltpu.make_async_copy(long_buf.at[me], long_in.at[me, mine], local_sems.at[1])
     local_rows.start()
-    local_long.start()
     copies = []
     for step in range(1, count):
         peer = lax.rem(me + step, count)
@@ -321,20 +349,7 @@
         )
         copy.start()
         copies.append(copy)
-    for step_c, step_h in peers:
-        peer, other = lax.rem(me + step_c, count), lax.rem(mine + step_h, groups)
-        copy = pltpu.make_async_remote_copy(
-            src_ref=long_buf.at[peer],
-            dst_ref=long_in.at[me, mine],
-            send_sem=long_send.at[peer * groups + other],
-            recv_sem=long_recv.at[me * groups + mine],
-            device_id=(peer, other),
-            device_id_type=mesh_id,
-        )
-        copy.start()
-        copies.append(copy)
     local_rows.wait()
-    local_long.wait()
     for copy in copies:
         copy.wait_send()
     for step in range(1, count):
@@ -347,18 +362,7 @@
             device_id=(source, mine),
             device_id_type=mesh_id,
         ).wait_recv()
-    for step_c, step_h in peers:
-        source, other = lax.rem(me + step_c, count), lax.rem(mine + step_h, groups)
-        pltpu.make_async_remote_copy(
-            src_ref=long_buf.at[source],
-            dst_ref=long_in.at[source, other],
-            send_sem=long_send.at[source * groups + other],
-            recv_sem=long_recv.at[source * groups + other],
-            device_id=(source, other),
-            device_id_type=mesh_id,
-        ).wait_recv()
     rows_out[...] = rows_in[...]
-    long_out[...] = long_in[...]
 
 
 def fused(grad_seq, sources, in_seq, taps, groups, block_len, collective_id):
@@ -375,30 +379,25 @@
     rev = pairs[..., ::-1].astype(jnp.float32)
     in_pad = jnp.pad(in_seq.reshape(chans, block_count, block_len), ((0, 0), (1, 0), (0, 0)))
     lags = block_count + 1
-    rows_shape = (block_count, chans + 1, block_len)
-    long_shape = (block_count, groups, 1, block_len)
+    rows_shape = (block_count, chans + 2, block_len)
     vmem = pl.BlockSpec(memory_space=pltpu.VMEM)
     return pl.pallas_call(
         fused_kernel,
-        out_shape=(
-            jax.ShapeDtypeStruct(rows_shape, jnp.float32),
-            jax.ShapeDtypeStruct(long_shape, jnp.float32),
-        ),
+        out_shape=jax.ShapeDtypeStruct(rows_shape, jnp.float32),
         in_specs=[vmem, vmem, vmem, pl.BlockSpec(memory_space=pltpu.SMEM)],
-        out_specs=(vmem, vmem),
+        out_specs=vmem,
         scratch_shapes=[
             pltpu.VMEM((chans, block_count, lags * block_len), jnp.bfloat16),
             pltpu.VMEM((count, lags * block_len, block_len), jnp.bfloat16),
             pltpu.VMEM((chans, block_count + 8, block_len), jnp.float32),
             pltpu.VMEM(rows_shape, jnp.float32),
-            pltpu.VMEM((block_count, 1, block_len), jnp.float32),
+            pltpu.VMEM((groups, block_count, block_len), jnp.float32),
             pltpu.VMEM(rows_shape, jnp.float32),
-            pltpu.VMEM(long_shape, jnp.float32),
-            pltpu.SemaphoreType.DMA((2,)),
+            pltpu.SemaphoreType.DMA((1,)),
             pltpu.SemaphoreType.DMA((block_count,)),
             pltpu.SemaphoreType.DMA((block_count,)),
-            pltpu.SemaphoreType.DMA((block_count * groups,)),
-            pltpu.SemaphoreType.DMA((block_count * groups,)),
+            pltpu.SemaphoreType.DMA((groups,)),
+            pltpu.SemaphoreType.DMA((groups,)),
         ],
         compiler_params=pltpu.CompilerParams(
             collective_id=collective_id,
@@ -441,7 +440,7 @@
     hidden = hidden.astype(jnp.bfloat16)
 
     groups = lax.axis_size("ch")
-    got, got_long = fused(
+    got = fused(
         grad_seq,
         jnp.concatenate([filt_seq, hidden], axis=0),
         in_seq,
@@ -452,7 +451,7 @@
     )
     grad_in_out = got[:, :per_dev].reshape(filter_count, chan_count, shard_len)
     grad_in_out = grad_in_out.astype(jnp.bfloat16)
-    grad_long_out = got_long.reshape(filter_count, per_filter * groups, shard_len).sum(axis=1)
+    grad_long_out = got[:, per_dev + 1].reshape(filter_count, per_filter, shard_len).sum(axis=1)
     short_all = got[:, per_dev, : tap_count * per_dev].reshape(ctx_count, tap_count, per_dev)
     grad_short_out = short_all.transpose(1, 0, 2).reshape(tap_count, filter_count, chan_count)
     return (grad_in_out, grad_long_out, grad_short_out)

time: 60.3 us -> 56.1 us (0.930)
  Pallas kernels: 52.1 us -> 48 us
    pallas_call x1, Pallas kernels: 31.6 us -> 27.5 us  [fused(): pl.pallas_call(fused_kernel, out_shape=jax.ShapeDtypeStruct(rows_shape, j...]
where the time goes in v5:
time: 56.1 us; the launch traced here: 55.8 us
  Pallas kernels  48 us (86%)
  local copies, waits for them, and re-layouts  5.28 us (9%)
  other arithmetic  1.7 us (3%)
  between operations  0.81 us (1%)
    pallas_call x1, Pallas kernels, fused(): pl.pallas_call(fused_kernel, out_shape=jax.ShapeDtypeStruct(rows_shape, j...  27.5 us
    pallas_call x1, Pallas kernels, swap(): pl.pallas_call(swap_kernel, out_shape=jax.ShapeDtypeStruct(chunks.shape,...  20.5 us
    unnamed x12, local copies, waits for them, and re-layouts  2.56 us

profile of v5, /device:TPU:1, one launch (start us, length us, event | category | flops | bytes accessed | tf_op | source)
XLA Modules:
  0.0 55.8 jit_solution(15170850365228015887)
XLA Ops:
  0.6 0.0 copy-start.2
  0.6 0.7 %copy-done.2 = bf16[32,128]{1,0:T(8,128)(2,1)S(1)} copy-done((bf16[32,128]{1,0:T(8,128)(2,1)S(1)}, bf16[32,128]{1,0:T(8,128)(2,1)}, u32[]{:S(2)}) %copy-start.2) | copy-done | bytes 8216
  1.3 0.0 copy-start.3
  1.4 0.6 %copy-done.3 = f32[3,32,4]{1,2,0:T(4,128)S(1)} copy-done((f32[3,32,4]{1,2,0:T(4,128)S(1)}, f32[3,32,4]{1,2,0:T(4,128)}, u32[]{:S(2)}) %copy-start.3) | copy-done | bytes 1560
  2.0 0.0 copy-start
  2.0 0.0 copy-start.1
  2.0 0.1 copy.11
  2.2 0.2 slice_reduce_fusion.2
  2.4 0.1 copy.12.taps_ref
  2.5 0.3 copy-done
  2.8 0.0 copy-done.1
  2.8 0.8 %pad_maximum_fusion.send_ref = bf16[64,5,128]{2,1,0:T(8,128)(2,1)} fusion(bf16[64,1,128]{2,1,0:T(2,128)(2,1)S(1)} %copy.9, bf16[64,2,128]{2,1,0:T(2,128)(2,1)S(1)} %bitcast.34, bf16[64,2,128]{2,1,0:T(2,128)(2,1)S(1)} %bitcast.35), kind=kLoop, calls=%fused_computation.2 | loop fusion | flops 245760 | bytes 163840 | tf_op jit(solution)/shard_map/concatenate | solution.py:421
  3.6 20.5 %shard_map.67 = bf16[64,5,128]{2,1,0:T(8,128)(2,1)} custom-call(bf16[64,5,128]{2,1,0:T(8,128)(2,1)} %pad_maximum_fusion.send_ref), custom_call_target="tpu_custom_call" | custom-call | tf_op jit(solution)/shard_map/pallas_call | solution.py:118
  24.1 0.9 %copy.21 = bf16[64,5,128]{2,0,1:T(8,128)(2,1)S(1)} copy(bf16[64,5,128]{2,1,0:T(8,128)(2,1)} %shard_map.67) | data formatting | bytes 163840 | tf_op jit(solution)/shard_map/pallas_call | solution.py:118
  25.1 0.1 copy.22
  25.1 0.2 fusion.9
  25.4 0.5 rev.3
  26.0 27.5 %shard_map.68 = f32[64,4,128]{2,1,0:T(4,128)S(1)} custom-call(f32[2,128,128]{2,1,0:T(8,128)S(1)} %pad_convert_fusion.grad_ref, f32[3,65,256]{2,1,0:T(8,128)S(1)} %convert_element_type.32.rev_ref, f32[2,65,128]{2,1,0:T(8,128)S(1)} %pad_convert_fusion.1.in_ref, f32[3,2]{1,0:T(4,128)S(1)} %copy.12.taps_ref), custom_call_target="tpu_custom_call" | custom-call | tf_op jit(solution)/shard_map/pallas_call | solution.py:384
  53.6 0.1 copy.13
  53.7 0.6 %slice.90 = bf16[64,2,128]{2,1,0:T(2,128)(2,1)} slice(f32[64,4,128]{2,1,0:T(4,128)S(1)} %shard_map.68), slice={[0:64], [0:2], [0:128]} | slice | bytes 65536 | tf_op jit(solution)/shard_map/slice | solution.py:452
  54.4 0.6 %reduce_sum.9 = f32[32,128]{1,0:T(8,128)} reduce(f32[32,2,128]{2,1,0:T(2,128)S(1)} %bitcast.30, f32[]{:T(128)} %constant.18.clone.1), dimensions={1}, to_apply=%region_0.1 | reduce | flops 4096 | bytes 49156 | tf_op jit(solution)/shard_map/reduce_sum | solution.py:454
  55.0 0.1 copy.14
  55.1 0.7 %copy.15 = f32[3,32,4]{1,2,0:T(4,128)} copy(f32[3,32,4]{0,2,1:T(4,128)S(1)} %bitcast.28) | data formatting | bytes 3072
  (16 shorter events, 0.3 us)
Async XLA Ops:
  0.6 0.7 %copy-start.2 = (bf16[32,128]{1,0:T(8,128)(2,1)S(1)}, bf16[32,128]{1,0:T(8,128)(2,1)}, u32[]{:S(2)}) copy-start(bf16[32,128]{1,0:T(8,128)(2,1)} %param.6) | copy-start | bytes 24580
  1.3 0.7 %copy-start.3 = (f32[3,32,4]{1,2,0:T(4,128)S(1)}, f32[3,32,4]{1,2,0:T(4,128)}, u32[]{:S(2)}) copy-start(f32[3,32,4]{1,2,0:T(4,128)} %param.5) | copy-start | bytes 4612
  2.0 0.8 %copy-start = (bf16[32,4,128]{2,1,0:T(4,128)(2,1)S(1)}, bf16[32,4,128]{2,1,0:T(4,128)(2,1)}, u32[]{:S(2)}) copy-start(bf16[32,4,128]{2,1,0:T(4,128)(2,1)} %param.4) | copy-start | bytes 98308
  2.0 0.8 %copy-start.1 = (bf16[32,4,128]{2,1,0:T(4,128)(2,1)S(1)}, bf16[32,4,128]{2,1,0:T(4,128)(2,1)}, u32[]{:S(2)}) copy-start(bf16[32,4,128]{2,1,0:T(4,128)(2,1)} %param.7) | copy-start | bytes 98308

commit v6 on v5

--- a/solution.py
+++ b/solution.py
@@ -257,21 +257,41 @@
 
     lax.fori_loop(0, lags, fill_hankel, 0)
 
-    def fill_toeplitz(lag, carry):
-        row = pl.multiple_of(lag * block_len, block_len)
-        for s in range(sources):
-            line = rev_ref[s, pl.ds(lag, 1), :]
-            tiled = jnp.broadcast_to(line, (block_len, 2 * block_len))
-            skewed = pltpu.roll(tiled, block_len + 1, 1, stride=1, stride_axis=0)
-            toeplitz[s, pl.ds(row, block_len), :] = skewed[:, :block_len].astype(toeplitz.dtype)
-        return carry
-
-    lax.fori_loop(0, lags, fill_toeplitz, 0)
+    def fill_toeplitz(picked):
+        def fill(lag, carry):
+            row = pl.multiple_of(lag * block_len, block_len)
+            for s in picked:
+                line = rev_ref[s, pl.ds(lag, 1), :]
+                tiled = jnp.broadcast_to(line, (block_len, 2 * block_len))
+                skewed = pltpu.roll(tiled, block_len + 1, 1, stride=1, stride_axis=0)
+                toeplitz[s, pl.ds(row, block_len), :] = skewed[:, :block_len].astype(
+                    toeplitz.dtype
+                )
+            return carry
+
+        lax.fori_loop(0, lags, fill, 0)
+
+    fill_toeplitz(range(1, sources))
 
     acc = jnp.dot(hankel[0], toeplitz[1], preferred_element_type=jnp.float32)
     for g in range(1, chans):
         acc = acc + jnp.dot(hankel[g], toeplitz[1 + g], preferred_element_type=jnp.float32)
     ch_in[mine] = acc
+    pl.semaphore_wait(barrier, len(peers))
+    partials = []
+    for step in range(1, groups):
+        other = lax.rem(mine + step, groups)
+        copy = pltpu.make_async_remote_copy(
+            src_ref=ch_in.at[mine],
+            dst_ref=ch_in.at[mine],
+            send_sem=ch_send.at[other],
+            recv_sem=ch_recv.at[mine],
+            device_id=(me, other),
+            device_id_type=mesh_id,
+        )
+        copy.start()
+        partials.append(copy)
+    fill_toeplitz(range(1))
 
     lane = lax.broadcasted_iota(jnp.int32, (block_count, block_len), 1)
     short_row = jnp.zeros((block_count, block_len), jnp.float32)
@@ -303,20 +323,6 @@
             short_row = jnp.where(lane == offset * chans + g, value, short_row)
     rows_buf[:, chans, :] = short_row
 
-    pl.semaphore_wait(barrier, len(peers))
-    partials = []
-    for step in range(1, groups):
-        other = lax.rem(mine + step, groups)
-        copy = pltpu.make_async_remote_copy(
-            src_ref=ch_in.at[mine],
-            dst_ref=ch_in.at[mine],
-            send_sem=ch_send.at[other],
-            recv_sem=ch_recv.at[mine],
-            device_id=(me, other),
-            device_id_type=mesh_id,
-        )
-        copy.start()
-        partials.append(copy)
     for copy in partials:
         copy.wait_send()
     for step in range(1, groups):

time: 56.1 us -> 56.1 us (level)
  the two profiles are of different devices: /device:TPU:1 before, /device:TPU:8 now
where the time goes in v6:
time: 56.1 us; the launch traced here: 55.5 us
  Pallas kernels  47.7 us (85%)
  local copies, waits for them, and re-layouts  5.28 us (9%)
  other arithmetic  1.7 us (3%)
  between operations  0.81 us (1%)
    pallas_call x1, Pallas kernels, fused(): pl.pallas_call(fused_kernel, out_shape=jax.ShapeDtypeStruct(rows_shape, j...  27.5 us
    pallas_call x1, Pallas kernels, swap(): pl.pallas_call(swap_kernel, out_shape=jax.ShapeDtypeStruct(chunks.shape,...  20.2 us
    unnamed x12, local copies, waits for them, and re-layouts  2.56 us

profile of v6, /device:TPU:8, one launch (start us, length us, event | category | flops | bytes accessed | tf_op | source)
XLA Modules:
  0.0 55.5 jit_solution(4424234319832738448)
XLA Ops:
  0.6 0.0 copy-start.2
  0.6 0.7 %copy-done.2 = bf16[32,128]{1,0:T(8,128)(2,1)S(1)} copy-done((bf16[32,128]{1,0:T(8,128)(2,1)S(1)}, bf16[32,128]{1,0:T(8,128)(2,1)}, u32[]{:S(2)}) %copy-start.2) | copy-done | bytes 8216
  1.3 0.0 copy-start.3
  1.4 0.6 %copy-done.3 = f32[3,32,4]{1,2,0:T(4,128)S(1)} copy-done((f32[3,32,4]{1,2,0:T(4,128)S(1)}, f32[3,32,4]{1,2,0:T(4,128)}, u32[]{:S(2)}) %copy-start.3) | copy-done | bytes 1560
  2.0 0.0 copy-start
  2.0 0.0 copy-start.1
  2.0 0.1 copy.11
  2.2 0.2 slice_reduce_fusion.2
  2.4 0.1 copy.12.taps_ref
  2.5 0.3 copy-done
  2.8 0.0 copy-done.1
  2.8 0.8 %pad_maximum_fusion.send_ref = bf16[64,5,128]{2,1,0:T(8,128)(2,1)} fusion(bf16[64,1,128]{2,1,0:T(2,128)(2,1)S(1)} %copy.9, bf16[64,2,128]{2,1,0:T(2,128)(2,1)S(1)} %bitcast.34, bf16[64,2,128]{2,1,0:T(2,128)(2,1)S(1)} %bitcast.35), kind=kLoop, calls=%fused_computation.2 | loop fusion | flops 245760 | bytes 163840 | tf_op jit(solution)/shard_map/concatenate | solution.py:427
  3.6 20.2 %shard_map.67 = bf16[64,5,128]{2,1,0:T(8,128)(2,1)} custom-call(bf16[64,5,128]{2,1,0:T(8,128)(2,1)} %pad_maximum_fusion.send_ref), custom_call_target="tpu_custom_call" | custom-call | tf_op jit(solution)/shard_map/pallas_call | solution.py:118
  23.8 0.9 %copy.21 = bf16[64,5,128]{2,0,1:T(8,128)(2,1)S(1)} copy(bf16[64,5,128]{2,1,0:T(8,128)(2,1)} %shard_map.67) | data formatting | bytes 163840 | tf_op jit(solution)/shard_map/pallas_call | solution.py:118
  24.8 0.1 copy.22
  24.8 0.2 fusion.9
  25.1 0.5 rev.3
  25.7 27.5 %shard_map.68 = f32[64,4,128]{2,1,0:T(4,128)S(1)} custom-call(f32[2,128,128]{2,1,0:T(8,128)S(1)} %pad_convert_fusion.grad_ref, f32[3,65,256]{2,1,0:T(8,128)S(1)} %convert_element_type.32.rev_ref, f32[2,65,128]{2,1,0:T(8,128)S(1)} %pad_convert_fusion.1.in_ref, f32[3,2]{1,0:T(4,128)S(1)} %copy.12.taps_ref), custom_call_target="tpu_custom_call" | custom-call | tf_op jit(solution)/shard_map/pallas_call | solution.py:390
  53.3 0.1 copy.13
  53.4 0.6 %slice.90 = bf16[64,2,128]{2,1,0:T(2,128)(2,1)} slice(f32[64,4,128]{2,1,0:T(4,128)S(1)} %shard_map.68), slice={[0:64], [0:2], [0:128]} | slice | bytes 65536 | tf_op jit(solution)/shard_map/slice | solution.py:458
  54.1 0.6 %reduce_sum.9 = f32[32,128]{1,0:T(8,128)} reduce(f32[32,2,128]{2,1,0:T(2,128)S(1)} %bitcast.30, f32[]{:T(128)} %constant.18.clone.1), dimensions={1}, to_apply=%region_0.1 | reduce | flops 4096 | bytes 49156 | tf_op jit(solution)/shard_map/reduce_sum | solution.py:460
  54.7 0.1 copy.14
  54.8 0.7 %copy.15 = f32[3,32,4]{1,2,0:T(4,128)} copy(f32[3,32,4]{0,2,1:T(4,128)S(1)} %bitcast.28) | data formatting | bytes 3072
  (16 shorter events, 0.3 us)
Async XLA Ops:
  0.6 0.7 %copy-start.2 = (bf16[32,128]{1,0:T(8,128)(2,1)S(1)}, bf16[32,128]{1,0:T(8,128)(2,1)}, u32[]{:S(2)}) copy-start(bf16[32,128]{1,0:T(8,128)(2,1)} %param.6) | copy-start | bytes 24580
  1.3 0.7 %copy-start.3 = (f32[3,32,4]{1,2,0:T(4,128)S(1)}, f32[3,32,4]{1,2,0:T(4,128)}, u32[]{:S(2)}) copy-start(f32[3,32,4]{1,2,0:T(4,128)} %param.5) | copy-start | bytes 4612
  2.0 0.8 %copy-start = (bf16[32,4,128]{2,1,0:T(4,128)(2,1)S(1)}, bf16[32,4,128]{2,1,0:T(4,128)(2,1)}, u32[]{:S(2)}) copy-start(bf16[32,4,128]{2,1,0:T(4,128)(2,1)} %param.4) | copy-start | bytes 98308
  2.0 0.8 %copy-start.1 = (bf16[32,4,128]{2,1,0:T(4,128)(2,1)S(1)}, bf16[32,4,128]{2,1,0:T(4,128)(2,1)}, u32[]{:S(2)}) copy-start(bf16[32,4,128]{2,1,0:T(4,128)(2,1)} %param.7) | copy-start | bytes 98308

commit v7 on v6

--- a/solution.py
+++ b/solution.py
@@ -413,6 +413,104 @@
     )(grad_pad, rev, in_pad, taps)
 
 
+def relay_kernel(send_ref, out_ref, middle, landed, local_sems, first_send, first_recv, second_send, second_recv):
+    inner, outer = send_ref.shape[0], send_ref.shape[1]
+    me = lax.axis_index("ctx")
+    mine = lax.axis_index("ch")
+    row, col = me // inner, lax.rem(me, inner)
+    mesh_id = pl.DeviceIdType.MESH
+    barrier = pltpu.get_barrier_semaphore()
+    for step in range(1, inner):
+        peer = row * inner + lax.rem(col + step, inner)
+        pl.semaphore_signal(barrier, 1, device_id=(peer, mine), device_id_type=mesh_id)
+    for step in range(1, outer):
+        peer = lax.rem(row + step, outer) * inner + col
+        pl.semaphore_signal(barrier, 1, device_id=(peer, mine), device_id_type=mesh_id)
+    pl.semaphore_wait(barrier, inner - 1 + outer - 1)
+    local = pltpu.make_async_copy(send_ref.at[col], middle.at[:, col], local_sems.at[0])
+    local.start()
+    copies = []
+    for step in range(1, inner):
+        target = lax.rem(col + step, inner)
+        copy = pltpu.make_async_remote_copy(
+            src_ref=send_ref.at[target],
+            dst_ref=middle.at[:, col],
+            send_sem=first_send.at[target],
+            recv_sem=first_recv.at[col],
+            device_id=(row * inner + target, mine),
+            device_id_type=mesh_id,
+        )
+        copy.start()
+        copies.append(copy)
+    local.wait()
+    for copy in copies:
+        copy.wait_send()
+    for step in range(1, inner):
+        source = lax.rem(col + step, inner)
+        pltpu.make_async_remote_copy(
+            src_ref=send_ref.at[source],
+            dst_ref=middle.at[:, source],
+            send_sem=first_send.at[source],
+            recv_sem=first_recv.at[source],
+            device_id=(row * inner + source, mine),
+            device_id_type=mesh_id,
+        ).wait_recv()
+    local = pltpu.make_async_copy(middle.at[row], landed.at[row], local_sems.at[1])
+    local.start()
+    copies = []
+    for step in range(1, outer):
+        target = lax.rem(row + step, outer)
+        copy = pltpu.make_async_remote_copy(
+            src_ref=middle.at[target],
+            dst_ref=landed.at[row],
+            send_sem=second_send.at[target],
+            recv_sem=second_recv.at[row],
+            device_id=(target * inner + col, mine),
+            device_id_type=mesh_id,
+        )
+        copy.start()
+        copies.append(copy)
+    local.wait()
+    for copy in copies:
+        copy.wait_send()
+    for step in range(1, outer):
+        source = lax.rem(row + step, outer)
+        pltpu.make_async_remote_copy(
+            src_ref=middle.at[source],
+            dst_ref=landed.at[source],
+            send_sem=second_send.at[source],
+            recv_sem=second_recv.at[source],
+            device_id=(source * inner + col, mine),
+            device_id_type=mesh_id,
+        ).wait_recv()
+    out_ref[...] = landed[...]
+
+
+def relay(chunks, inner, collective_id):
+    count = chunks.shape[0]
+    outer = count // inner
+    rest = chunks.shape[1:]
+    by_inner = chunks.reshape((outer, inner) + rest).swapaxes(0, 1)
+    grid_shape = (outer, inner) + rest
+    landed = pl.pallas_call(
+        relay_kernel,
+        out_shape=jax.ShapeDtypeStruct(grid_shape, chunks.dtype),
+        in_specs=[pl.BlockSpec(memory_space=pltpu.VMEM)],
+        out_specs=pl.BlockSpec(memory_space=pltpu.VMEM),
+        scratch_shapes=[
+            pltpu.VMEM(grid_shape, chunks.dtype),
+            pltpu.VMEM(grid_shape, chunks.dtype),
+            pltpu.SemaphoreType.DMA((2,)),
+            pltpu.SemaphoreType.DMA((inner,)),
+            pltpu.SemaphoreType.DMA((inner,)),
+            pltpu.SemaphoreType.DMA((outer,)),
+            pltpu.SemaphoreType.DMA((outer,)),
+        ],
+        compiler_params=pltpu.CompilerParams(collective_id=collective_id, has_side_effects=True),
+    )(by_inner)
+    return landed.reshape(chunks.shape)
+
+
 def per_device(inputs, short_filter, long_filter, grad_out):
     tap_count = short_filter.shape[0]
     filter_count, chan_count, shard_len = inputs.shape
@@ -432,7 +530,7 @@
         ],
         axis=1,
     )
-    recv = swap(send, 0)
+    recv = relay(send, 8, 0)
     seqs = recv.transpose(1, 0, 2).reshape(2 * per_dev + 1, total_len)
     grad_seq = seqs[:per_dev]
     in_seq = seqs[per_dev : 2 * per_dev].astype(jnp.float32)

time: 56.1 us -> 54.4 us (0.970)
  Pallas kernels: 47.7 us -> 46 us
    pallas_call x1, Pallas kernels: 27.5 us -> 25.4 us  [fused(): pl.pallas_call(fused_kernel, out_shape=jax.ShapeDtypeStruct(rows_shape, j...]
    concatenate x1 -> x0, other arithmetic: 0.75 us -> none  [per_device(): jnp.concatenate([grad_out.reshape(ctx_count, per_dev, shard_len), inputs....]
    transpose x0 -> x1, other arithmetic: none -> 0.75 us  [relay(): by_inner = chunks.reshape((outer, inner) + rest).swapaxes(0, 1)]
where the time goes in v7:
time: 54.4 us; the launch traced here: 53.8 us
  Pallas kernels  46 us (85%)
  local copies, waits for them, and re-layouts  5.28 us (10%)
  other arithmetic  1.7 us (3%)
  between operations  0.81 us (1%)
    pallas_call x1, Pallas kernels, fused(): pl.pallas_call(fused_kernel, out_shape=jax.ShapeDtypeStruct(rows_shape, j...  25.4 us
    pallas_call x1, Pallas kernels, relay(): pl.pallas_call(relay_kernel, out_shape=jax.ShapeDtypeStruct(grid_shape, c...  20.5 us
    unnamed x12, local copies, waits for them, and re-layouts  2.56 us

profile of v7, /device:TPU:8, one launch (start us, length us, event | category | flops | bytes accessed | tf_op | source)
XLA Modules:
  0.0 53.8 jit_solution(6380484733038186933)
XLA Ops:
  0.6 0.0 copy-start.2
  0.6 0.7 %copy-done.2 = bf16[32,128]{1,0:T(8,128)(2,1)S(1)} copy-done((bf16[32,128]{1,0:T(8,128)(2,1)S(1)}, bf16[32,128]{1,0:T(8,128)(2,1)}, u32[]{:S(2)}) %copy-start.2) | copy-done | bytes 8216
  1.3 0.0 copy-start.3
  1.4 0.6 %copy-done.3 = f32[3,32,4]{1,2,0:T(4,128)S(1)} copy-done((f32[3,32,4]{1,2,0:T(4,128)S(1)}, f32[3,32,4]{1,2,0:T(4,128)}, u32[]{:S(2)}) %copy-start.3) | copy-done | bytes 1560
  2.0 0.0 copy-start
  2.0 0.0 copy-start.1
  2.0 0.1 copy.13
  2.2 0.2 slice_reduce_fusion.2
  2.4 0.1 copy.14.taps_ref
  2.5 0.3 copy-done
  2.8 0.0 copy-done.1
  2.8 0.8 %maximum_bitcast_fusion.send_ref = bf16[8,8,5,128]{3,2,1,0:T(8,128)(2,1)} fusion(bf16[8,8,1,128]{3,2,0,1:T(2,128)(2,1)S(1)} %copy.11, bf16[8,8,2,128]{3,2,1,0:T(2,128)(2,1)S(1)} %bitcast.38, bf16[8,8,2,128]{3,2,1,0:T(2,128)(2,1)S(1)} %bitcast.39), kind=kLoop, calls=%fused_computation.2 | loop fusion | flops 245760 | bytes 163840 | tf_op jit(solution)/shard_map/transpose | solution.py:493
  3.6 20.5 %shard_map.67 = bf16[8,8,5,128]{3,2,1,0:T(8,128)(2,1)} custom-call(bf16[8,8,5,128]{3,2,1,0:T(8,128)(2,1)} %maximum_bitcast_fusion.send_ref), custom_call_target="tpu_custom_call" | custom-call | tf_op jit(solution)/shard_map/pallas_call | solution.py:495
  24.1 0.9 %copy.27 = bf16[8,8,5,128]{3,1,0,2:T(8,128)(2,1)S(1)} copy(bf16[8,8,5,128]{3,2,1,0:T(8,128)(2,1)} %shard_map.67) | data formatting | bytes 163840 | tf_op jit(solution)/shard_map/pallas_call | solution.py:495
  25.1 0.1 copy.28
  25.1 0.2 fusion.9
  25.5 0.5 rev.3
  26.0 25.4 %shard_map.68 = f32[64,4,128]{2,1,0:T(4,128)S(1)} custom-call(f32[2,128,128]{2,1,0:T(8,128)S(1)} %pad_convert_fusion.grad_ref, f32[3,65,256]{2,1,0:T(8,128)S(1)} %convert_element_type.32.rev_ref, f32[2,65,128]{2,1,0:T(8,128)S(1)} %pad_convert_fusion.1.in_ref, f32[3,2]{1,0:T(4,128)S(1)} %copy.14.taps_ref), custom_call_target="tpu_custom_call" | custom-call | tf_op jit(solution)/shard_map/pallas_call | solution.py:390
  51.5 0.1 copy.15
  51.7 0.6 %slice.90 = bf16[64,2,128]{2,1,0:T(2,128)(2,1)} slice(f32[64,4,128]{2,1,0:T(4,128)S(1)} %shard_map.68), slice={[0:64], [0:2], [0:128]} | slice | bytes 65536 | tf_op jit(solution)/shard_map/slice | solution.py:556
  52.3 0.6 %reduce_sum.9 = f32[32,128]{1,0:T(8,128)} reduce(f32[32,2,128]{2,1,0:T(2,128)S(1)} %bitcast.34, f32[]{:T(128)} %constant.18.clone.1), dimensions={1}, to_apply=%region_0.1 | reduce | flops 4096 | bytes 49156 | tf_op jit(solution)/shard_map/reduce_sum | solution.py:558
  52.9 0.1 copy.16
  53.1 0.7 %copy.17 = f32[3,32,4]{1,2,0:T(4,128)} copy(f32[3,32,4]{0,2,1:T(4,128)S(1)} %bitcast.32) | data formatting | bytes 3072
  (16 shorter events, 0.3 us)
Async XLA Ops:
  0.6 0.7 %copy-start.2 = (bf16[32,128]{1,0:T(8,128)(2,1)S(1)}, bf16[32,128]{1,0:T(8,128)(2,1)}, u32[]{:S(2)}) copy-start(bf16[32,128]{1,0:T(8,128)(2,1)} %param.6) | copy-start | bytes 24580
  1.3 0.7 %copy-start.3 = (f32[3,32,4]{1,2,0:T(4,128)S(1)}, f32[3,32,4]{1,2,0:T(4,128)}, u32[]{:S(2)}) copy-start(f32[3,32,4]{1,2,0:T(4,128)} %param.5) | copy-start | bytes 4612
  2.0 0.8 %copy-start = (bf16[32,4,128]{2,1,0:T(4,128)(2,1)S(1)}, bf16[32,4,128]{2,1,0:T(4,128)(2,1)}, u32[]{:S(2)}) copy-start(bf16[32,4,128]{2,1,0:T(4,128)(2,1)} %param.7) | copy-start | bytes 98308
  2.0 0.8 %copy-start.1 = (bf16[32,4,128]{2,1,0:T(4,128)(2,1)S(1)}, bf16[32,4,128]{2,1,0:T(4,128)(2,1)}, u32[]{:S(2)}) copy-start(bf16[32,4,128]{2,1,0:T(4,128)(2,1)} %param.4) | copy-start | bytes 98308

commit v8 on v7

--- a/solution.py
+++ b/solution.py
@@ -229,10 +229,11 @@
 
 def fused_kernel(
     grad_ref, rev_ref, in_ref, taps_ref, rows_out,
-    hankel, toeplitz, grad_buf, rows_buf, ch_in, rows_in, local_sems,
-    rows_send, rows_recv, ch_send, ch_recv,
+    hankel, toeplitz, grad_buf, rows_buf, ch_in, middle, rows_in, local_sems,
+    first_send, first_recv, second_send, second_recv, ch_send, ch_recv,
 ):
-    count = rows_buf.shape[0]
+    outer, inner = rows_buf.shape[0], rows_buf.shape[1]
+    count = outer * inner
     chans, _, block_len = grad_ref.shape
     block_count = count
     sources, lags, _ = rev_ref.shape
@@ -241,10 +242,12 @@
     me = lax.axis_index("ctx")
     mine = lax.axis_index("ch")
     mesh_id = pl.DeviceIdType.MESH
-    peers = [(c, 0) for c in range(1, count)] + [(0, h) for h in range(1, groups)]
+    row, col = me // inner, lax.rem(me, inner)
+    peers = [(row * inner + lax.rem(col + step, inner), mine) for step in range(1, inner)]
+    peers += [(lax.rem(row + step, outer) * inner + col, mine) for step in range(1, outer)]
+    peers += [(me, lax.rem(mine + step, groups)) for step in range(1, groups)]
     barrier = pltpu.get_barrier_semaphore()
-    for step_c, step_h in peers:
-        peer, other = lax.rem(me + step_c, count), lax.rem(mine + step_h, groups)
+    for peer, other in peers:
         pl.semaphore_signal(barrier, 1, device_id=(peer, other), device_id_type=mesh_id)
 
     def fill_hankel(lag, carry):
@@ -307,7 +310,9 @@
             total = total + taps_ref[offset, g] * jnp.where(
                 lane >= block_len - offset, there, here
             )
-        rows_buf[:, g, :] = total.astype(jnp.bfloat16).astype(jnp.float32)
+        rows_buf[:, :, g, :] = (
+            total.astype(jnp.bfloat16).astype(jnp.float32).reshape(outer, inner, block_len)
+        )
         current = in_ref[g, pl.ds(1, block_count), :]
         previous = in_ref[g, pl.ds(0, block_count), :]
         for offset in range(tap_count):
@@ -321,7 +326,7 @@
                 )
             value = jnp.sum(hidden_grad * delayed_in)
             short_row = jnp.where(lane == offset * chans + g, value, short_row)
-    rows_buf[:, chans, :] = short_row
+    rows_buf[:, :, chans, :] = short_row.reshape(outer, inner, block_len)
 
     for copy in partials:
         copy.wait_send()
@@ -338,40 +343,68 @@
     summed = ch_in[0]
     for h in range(1, groups):
         summed = summed + ch_in[h]
-    rows_buf[:, chans + 1, :] = summed
-
-    local_rows = pltpu.make_async_copy(rows_buf.at[me], rows_in.at[me], local_sems.at[0])
-    local_rows.start()
+    rows_buf[:, :, chans + 1, :] = summed.reshape(outer, inner, block_len)
+
+    local = pltpu.make_async_copy(rows_buf.at[:, col], middle.at[:, col], local_sems.at[0])
+    local.start()
     copies = []
-    for step in range(1, count):
-        peer = lax.rem(me + step, count)
-        copy = pltpu.make_async_remote_copy(
-            src_ref=rows_buf.at[peer],
-            dst_ref=rows_in.at[me],
-            send_sem=rows_send.at[peer],
-            recv_sem=rows_recv.at[me],
-            device_id=(peer, mine),
+    for step in range(1, inner):
+        target = lax.rem(col + step, inner)
+        copy = pltpu.make_async_remote_copy(
+            src_ref=rows_buf.at[:, target],
+            dst_ref=middle.at[:, col],
+            send_sem=first_send.at[target],
+            recv_sem=first_recv.at[col],
+            device_id=(row * inner + target, mine),
             device_id_type=mesh_id,
         )
         copy.start()
         copies.append(copy)
-    local_rows.wait()
+    local.wait()
     for copy in copies:
         copy.wait_send()
-    for step in range(1, count):
-        source = lax.rem(me + step, count)
-        pltpu.make_async_remote_copy(
-            src_ref=rows_buf.at[source],
+    for step in range(1, inner):
+        source = lax.rem(col + step, inner)
+        pltpu.make_async_remote_copy(
+            src_ref=rows_buf.at[:, source],
+            dst_ref=middle.at[:, source],
+            send_sem=first_send.at[source],
+            recv_sem=first_recv.at[source],
+            device_id=(row * inner + source, mine),
+            device_id_type=mesh_id,
+        ).wait_recv()
+    local = pltpu.make_async_copy(middle.at[row], rows_in.at[row], local_sems.at[1])
+    local.start()
+    copies = []
+    for step in range(1, outer):
+        target = lax.rem(row + step, outer)
+        copy = pltpu.make_async_remote_copy(
+            src_ref=middle.at[target],
+            dst_ref=rows_in.at[row],
+            send_sem=second_send.at[target],
+            recv_sem=second_recv.at[row],
+            device_id=(target * inner + col, mine),
+            device_id_type=mesh_id,
+        )
+        copy.start()
+        copies.append(copy)
+    local.wait()
+    for copy in copies:
+        copy.wait_send()
+    for step in range(1, outer):
+        source = lax.rem(row + step, outer)
+        pltpu.make_async_remote_copy(
+            src_ref=middle.at[source],
             dst_ref=rows_in.at[source],
-            send_sem=rows_send.at[source],
-            recv_sem=rows_recv.at[source],
-            device_id=(source, mine),
+            send_sem=second_send.at[source],
+            recv_sem=second_recv.at[source],
+            device_id=(source * inner + col, mine),
             device_id_type=mesh_id,
         ).wait_recv()
     rows_out[...] = rows_in[...]
 
 
-def fused(grad_seq, sources, in_seq, taps, groups, block_len, collective_id):
+def fused(grad_seq, sources, in_seq, taps, groups, inner, block_len, collective_id):
     chans, total_len = grad_seq.shape
     count = sources.shape[0]
     block_count = total_len // block_len
@@ -385,7 +418,8 @@
     rev = pairs[..., ::-1].astype(jnp.float32)
     in_pad = jnp.pad(in_seq.reshape(chans, block_count, block_len), ((0, 0), (1, 0), (0, 0)))
     lags = block_count + 1
-    rows_shape = (block_count, chans + 2, block_len)
+    outer = block_count // inner
+    rows_shape = (outer, inner, chans + 2, block_len)
     vmem = pl.BlockSpec(memory_space=pltpu.VMEM)
     return pl.pallas_call(
         fused_kernel,
@@ -399,9 +433,12 @@
             pltpu.VMEM(rows_shape, jnp.float32),
             pltpu.VMEM((groups, block_count, block_len), jnp.float32),
             pltpu.VMEM(rows_shape, jnp.float32),
-            pltpu.SemaphoreType.DMA((1,)),
-            pltpu.SemaphoreType.DMA((block_count,)),
-            pltpu.SemaphoreType.DMA((block_count,)),
+            pltpu.VMEM(rows_shape, jnp.float32),
+            pltpu.SemaphoreType.DMA((2,)),
+            pltpu.SemaphoreType.DMA((inner,)),
+            pltpu.SemaphoreType.DMA((inner,)),
+            pltpu.SemaphoreType.DMA((outer,)),
+            pltpu.SemaphoreType.DMA((outer,)),
             pltpu.SemaphoreType.DMA((groups,)),
             pltpu.SemaphoreType.DMA((groups,)),
         ],
@@ -410,7 +447,7 @@
             has_side_effects=True,
             vmem_limit_bytes=48 * 1024 * 1024,
         ),
-    )(grad_pad, rev, in_pad, taps)
+    )(grad_pad, rev, in_pad, taps).reshape((block_count,) + rows_shape[2:])
 
 
 def relay_kernel(send_ref, out_ref, middle, landed, local_sems, first_send, first_recv, second_send, second_recv):
@@ -550,6 +587,7 @@
         in_seq,
         taps,
         groups,
+        8,
         block_len,
         1,
     )

time: 54.4 us -> 56.5 us (1.039)
  Pallas kernels: 46 us -> 47.9 us
    pallas_call x1, Pallas kernels: 25.4 us -> 27.4 us  [fused(): pl.pallas_call(fused_kernel, out_shape=jax.ShapeDtypeStruct(rows_shape, j...]
    unnamed x12 -> x13, local copies, waits for them, and re-layouts: 2.56 us -> 2.63 us
where the time goes in v8:
time: 56.5 us; the launch traced here: 55.7 us
  Pallas kernels  47.9 us (85%)
  local copies, waits for them, and re-layouts  5.28 us (9%)
  other arithmetic  1.7 us (3%)
  between operations  0.81 us (1%)
    pallas_call x1, Pallas kernels, fused(): pl.pallas_call(fused_kernel, out_shape=jax.ShapeDtypeStruct(rows_shape, j...  27.4 us
    pallas_call x1, Pallas kernels, relay(): pl.pallas_call(relay_kernel, out_shape=jax.ShapeDtypeStruct(grid_shape, c...  20.5 us
    unnamed x13, local copies, waits for them, and re-layouts  2.63 us

profile of v8, /device:TPU:8, one launch (start us, length us, event | category | flops | bytes accessed | tf_op | source)
XLA Modules:
  0.0 55.7 jit_solution(8924796888841691927)
XLA Ops:
  0.6 0.0 copy-start.2
  0.6 0.7 %copy-done.2 = bf16[32,128]{1,0:T(8,128)(2,1)S(1)} copy-done((bf16[32,128]{1,0:T(8,128)(2,1)S(1)}, bf16[32,128]{1,0:T(8,128)(2,1)}, u32[]{:S(2)}) %copy-start.2) | copy-done | bytes 8216
  1.3 0.0 copy-start.3
  1.4 0.6 %copy-done.3 = f32[3,32,4]{1,2,0:T(4,128)S(1)} copy-done((f32[3,32,4]{1,2,0:T(4,128)S(1)}, f32[3,32,4]{1,2,0:T(4,128)}, u32[]{:S(2)}) %copy-start.3) | copy-done | bytes 1560
  2.0 0.0 copy-start
  2.0 0.0 copy-start.1
  2.0 0.1 copy.13
  2.2 0.2 slice_reduce_fusion.2
  2.4 0.1 copy.14.taps_ref
  2.5 0.3 copy-done
  2.8 0.0 copy-done.1
  2.8 0.8 %maximum_bitcast_fusion.send_ref = bf16[8,8,5,128]{3,2,1,0:T(8,128)(2,1)} fusion(bf16[8,8,1,128]{3,2,0,1:T(2,128)(2,1)S(1)} %copy.11, bf16[8,8,2,128]{3,2,1,0:T(2,128)(2,1)S(1)} %bitcast.42, bf16[8,8,2,128]{3,2,1,0:T(2,128)(2,1)S(1)} %bitcast.43), kind=kLoop, calls=%fused_computation.2 | loop fusion | flops 245760 | bytes 163840 | tf_op jit(solution)/shard_map/transpose | solution.py:530
  3.6 20.5 %shard_map.67 = bf16[8,8,5,128]{3,2,1,0:T(8,128)(2,1)} custom-call(bf16[8,8,5,128]{3,2,1,0:T(8,128)(2,1)} %maximum_bitcast_fusion.send_ref), custom_call_target="tpu_custom_call" | custom-call | tf_op jit(solution)/shard_map/pallas_call | solution.py:532
  24.1 0.9 %copy.28 = bf16[8,8,5,128]{3,1,0,2:T(8,128)(2,1)S(1)} copy(bf16[8,8,5,128]{3,2,1,0:T(8,128)(2,1)} %shard_map.67) | data formatting | bytes 163840 | tf_op jit(solution)/shard_map/pallas_call | solution.py:532
  25.1 0.1 copy.29
  25.1 0.2 fusion.9
  25.5 0.5 rev.3
  26.0 27.4 %shard_map.68 = f32[8,8,4,128]{3,2,1,0:T(4,128)S(1)} custom-call(f32[2,128,128]{2,1,0:T(8,128)S(1)} %pad_convert_fusion.grad_ref, f32[3,65,256]{2,1,0:T(8,128)S(1)} %convert_element_type.32.rev_ref, f32[2,65,128]{2,1,0:T(8,128)S(1)} %pad_convert_fusion.1.in_ref, f32[3,2]{1,0:T(4,128)S(1)} %copy.14.taps_ref), custom_call_target="tpu_custom_call" | custom-call | tf_op jit(solution)/shard_map/pallas_call | solution.py:424
  53.5 0.1 copy.18
  53.6 0.6 %slice.92 = bf16[64,2,128]{2,1,0:T(2,128)(2,1)} slice(f32[64,4,128]{2,1,0:T(4,128)S(1)} %bitcast.32), slice={[0:64], [0:2], [0:128]} | slice | bytes 65536 | tf_op jit(solution)/shard_map/slice | solution.py:594
  54.3 0.6 %reduce_sum.9 = f32[32,128]{1,0:T(8,128)} reduce(f32[32,2,128]{2,1,0:T(2,128)S(1)} %bitcast.38, f32[]{:T(128)} %constant.18.clone.1), dimensions={1}, to_apply=%region_0.1 | reduce | flops 4096 | bytes 49156 | tf_op jit(solution)/shard_map/reduce_sum | solution.py:596
  54.9 0.1 copy.16
  55.0 0.7 %copy.17 = f32[3,32,4]{1,2,0:T(4,128)} copy(f32[3,32,4]{0,2,1:T(4,128)S(1)} %bitcast.36) | data formatting | bytes 3072
  (16 shorter events, 0.3 us)
Async XLA Ops:
  0.6 0.7 %copy-start.2 = (bf16[32,128]{1,0:T(8,128)(2,1)S(1)}, bf16[32,128]{1,0:T(8,128)(2,1)}, u32[]{:S(2)}) copy-start(bf16[32,128]{1,0:T(8,128)(2,1)} %param.6) | copy-start | bytes 24580
  1.3 0.7 %copy-start.3 = (f32[3,32,4]{1,2,0:T(4,128)S(1)}, f32[3,32,4]{1,2,0:T(4,128)}, u32[]{:S(2)}) copy-start(f32[3,32,4]{1,2,0:T(4,128)} %param.5) | copy-start | bytes 4612
  2.0 0.8 %copy-start = (bf16[32,4,128]{2,1,0:T(4,128)(2,1)S(1)}, bf16[32,4,128]{2,1,0:T(4,128)(2,1)}, u32[]{:S(2)}) copy-start(bf16[32,4,128]{2,1,0:T(4,128)(2,1)} %param.7) | copy-start | bytes 98308
  2.0 0.8 %copy-start.1 = (bf16[32,4,128]{2,1,0:T(4,128)(2,1)S(1)}, bf16[32,4,128]{2,1,0:T(4,128)(2,1)}, u32[]{:S(2)}) copy-start(bf16[32,4,128]{2,1,0:T(4,128)(2,1)} %param.4) | copy-start | bytes 98308

commit v9 on v7

--- a/solution.py
+++ b/solution.py
@@ -530,7 +530,7 @@
         ],
         axis=1,
     )
-    recv = relay(send, 8, 0)
+    recv = relay(send, 16, 0)
     seqs = recv.transpose(1, 0, 2).reshape(2 * per_dev + 1, total_len)
     grad_seq = seqs[:per_dev]
     in_seq = seqs[per_dev : 2 * per_dev].astype(jnp.float32)

time: 54.4 us -> 56.8 us (1.044)
  Pallas kernels: 46 us -> 48.3 us
    pallas_call x1, Pallas kernels: 25.4 us -> 27.2 us  [fused(): pl.pallas_call(fused_kernel, out_shape=jax.ShapeDtypeStruct(rows_shape, j...]
where the time goes in v9:
time: 56.8 us; the launch traced here: 56.1 us
  Pallas kernels  48.3 us (85%)
  local copies, waits for them, and re-layouts  5.28 us (9%)
  other arithmetic  1.7 us (3%)
  between operations  0.81 us (1%)
    pallas_call x1, Pallas kernels, fused(): pl.pallas_call(fused_kernel, out_shape=jax.ShapeDtypeStruct(rows_shape, j...  27.2 us
    pallas_call x1, Pallas kernels, relay(): pl.pallas_call(relay_kernel, out_shape=jax.ShapeDtypeStruct(grid_shape, c...  21.1 us
    unnamed x12, local copies, waits for them, and re-layouts  2.56 us

profile of v9, /device:TPU:8, one launch (start us, length us, event | category | flops | bytes accessed | tf_op | source)
XLA Modules:
  0.0 56.1 jit_solution(14745371499656867637)
XLA Ops:
  0.6 0.0 copy-start.2
  0.6 0.7 %copy-done.2 = bf16[32,128]{1,0:T(8,128)(2,1)S(1)} copy-done((bf16[32,128]{1,0:T(8,128)(2,1)S(1)}, bf16[32,128]{1,0:T(8,128)(2,1)}, u32[]{:S(2)}) %copy-start.2) | copy-done | bytes 8216
  1.3 0.0 copy-start.3
  1.4 0.6 %copy-done.3 = f32[3,32,4]{1,2,0:T(4,128)S(1)} copy-done((f32[3,32,4]{1,2,0:T(4,128)S(1)}, f32[3,32,4]{1,2,0:T(4,128)}, u32[]{:S(2)}) %copy-start.3) | copy-done | bytes 1560
  2.0 0.0 copy-start
  2.0 0.0 copy-start.1
  2.0 0.1 copy.13
  2.2 0.2 slice_reduce_fusion.2
  2.4 0.1 copy.14.taps_ref
  2.5 0.3 copy-done
  2.8 0.0 copy-done.1
  2.8 0.8 %maximum_bitcast_fusion.send_ref = bf16[16,4,5,128]{3,2,1,0:T(8,128)(2,1)} fusion(bf16[4,16,1,128]{3,2,0,1:T(2,128)(2,1)S(1)} %copy.11, bf16[4,16,2,128]{3,2,1,0:T(2,128)(2,1)S(1)} %bitcast.36, bf16[4,16,2,128]{3,2,1,0:T(2,128)(2,1)S(1)} %bitcast.37), kind=kLoop, calls=%fused_computation.2 | loop fusion | flops 245760 | bytes 163840 | tf_op jit(solution)/shard_map/transpose | solution.py:493
  3.6 21.1 %shard_map.67 = bf16[4,16,5,128]{3,2,1,0:T(8,128)(2,1)} custom-call(bf16[16,4,5,128]{3,2,1,0:T(8,128)(2,1)} %maximum_bitcast_fusion.send_ref), custom_call_target="tpu_custom_call" | custom-call | tf_op jit(solution)/shard_map/pallas_call | solution.py:495
  24.7 0.9 %copy.12 = bf16[4,16,5,128]{3,1,0,2:T(8,128)(2,1)S(1)} copy(bf16[4,16,5,128]{3,2,1,0:T(8,128)(2,1)} %shard_map.67) | data formatting | bytes 163840 | tf_op jit(solution)/shard_map/pallas_call | solution.py:495
  25.7 0.1 copy.26
  25.7 0.2 fusion.9
  26.0 0.5 rev.3
  26.6 27.2 %shard_map.68 = f32[64,4,128]{2,1,0:T(4,128)S(1)} custom-call(f32[2,128,128]{2,1,0:T(8,128)S(1)} %pad_convert_fusion.grad_ref, f32[3,65,256]{2,1,0:T(8,128)S(1)} %convert_element_type.32.rev_ref, f32[2,65,128]{2,1,0:T(8,128)S(1)} %pad_convert_fusion.1.in_ref, f32[3,2]{1,0:T(4,128)S(1)} %copy.14.taps_ref), custom_call_target="tpu_custom_call" | custom-call | tf_op jit(solution)/shard_map/pallas_call | solution.py:390
  53.9 0.1 copy.15
  54.0 0.6 %slice.90 = bf16[64,2,128]{2,1,0:T(2,128)(2,1)} slice(f32[64,4,128]{2,1,0:T(4,128)S(1)} %shard_map.68), slice={[0:64], [0:2], [0:128]} | slice | bytes 65536 | tf_op jit(solution)/shard_map/slice | solution.py:556
  54.7 0.6 %reduce_sum.9 = f32[32,128]{1,0:T(8,128)} reduce(f32[32,2,128]{2,1,0:T(2,128)S(1)} %bitcast.32, f32[]{:T(128)} %constant.18.clone.1), dimensions={1}, to_apply=%region_0.1 | reduce | flops 4096 | bytes 49156 | tf_op jit(solution)/shard_map/reduce_sum | solution.py:558
  55.3 0.1 copy.16
  55.4 0.7 %copy.17 = f32[3,32,4]{1,2,0:T(4,128)} copy(f32[3,32,4]{0,2,1:T(4,128)S(1)} %bitcast.30) | data formatting | bytes 3072
  (16 shorter events, 0.3 us)
Async XLA Ops:
  0.6 0.7 %copy-start.2 = (bf16[32,128]{1,0:T(8,128)(2,1)S(1)}, bf16[32,128]{1,0:T(8,128)(2,1)}, u32[]{:S(2)}) copy-start(bf16[32,128]{1,0:T(8,128)(2,1)} %param.6) | copy-start | bytes 24580
  1.3 0.7 %copy-start.3 = (f32[3,32,4]{1,2,0:T(4,128)S(1)}, f32[3,32,4]{1,2,0:T(4,128)}, u32[]{:S(2)}) copy-start(f32[3,32,4]{1,2,0:T(4,128)} %param.5) | copy-start | bytes 4612
  2.0 0.8 %copy-start = (bf16[32,4,128]{2,1,0:T(4,128)(2,1)S(1)}, bf16[32,4,128]{2,1,0:T(4,128)(2,1)}, u32[]{:S(2)}) copy-start(bf16[32,4,128]{2,1,0:T(4,128)(2,1)} %param.7) | copy-start | bytes 98308
  2.0 0.8 %copy-start.1 = (bf16[32,4,128]{2,1,0:T(4,128)(2,1)S(1)}, bf16[32,4,128]{2,1,0:T(4,128)(2,1)}, u32[]{:S(2)}) copy-start(bf16[32,4,128]{2,1,0:T(4,128)(2,1)} %param.4) | copy-start | bytes 98308

commit v10 on v7

--- a/solution.py
+++ b/solution.py
@@ -414,30 +414,34 @@
 
 
 def relay_kernel(send_ref, out_ref, middle, landed, local_sems, first_send, first_recv, second_send, second_recv):
-    inner, outer = send_ref.shape[0], send_ref.shape[1]
+    firsts, seconds = send_ref.shape[0], send_ref.shape[1]
     me = lax.axis_index("ctx")
     mine = lax.axis_index("ch")
-    row, col = me // inner, lax.rem(me, inner)
+    first, second = me // seconds, lax.rem(me, seconds)
     mesh_id = pl.DeviceIdType.MESH
+
+    def place(f, s):
+        return f * seconds + s
+
     barrier = pltpu.get_barrier_semaphore()
-    for step in range(1, inner):
-        peer = row * inner + lax.rem(col + step, inner)
+    for step in range(1, firsts):
+        peer = place(lax.rem(first + step, firsts), second)
         pl.semaphore_signal(barrier, 1, device_id=(peer, mine), device_id_type=mesh_id)
-    for step in range(1, outer):
-        peer = lax.rem(row + step, outer) * inner + col
+    for step in range(1, seconds):
+        peer = place(first, lax.rem(second + step, seconds))
         pl.semaphore_signal(barrier, 1, device_id=(peer, mine), device_id_type=mesh_id)
-    pl.semaphore_wait(barrier, inner - 1 + outer - 1)
-    local = pltpu.make_async_copy(send_ref.at[col], middle.at[:, col], local_sems.at[0])
+    pl.semaphore_wait(barrier, firsts - 1 + seconds - 1)
+    local = pltpu.make_async_copy(send_ref.at[first], middle.at[:, first], local_sems.at[0])
     local.start()
     copies = []
-    for step in range(1, inner):
-        target = lax.rem(col + step, inner)
+    for step in range(1, firsts):
+        target = lax.rem(first + step, firsts)
         copy = pltpu.make_async_remote_copy(
             src_ref=send_ref.at[target],
-            dst_ref=middle.at[:, col],
+            dst_ref=middle.at[:, first],
             send_sem=first_send.at[target],
-            recv_sem=first_recv.at[col],
-            device_id=(row * inner + target, mine),
+            recv_sem=first_recv.at[first],
+            device_id=(place(target, second), mine),
             device_id_type=mesh_id,
         )
         copy.start()
@@ -445,27 +449,27 @@
     local.wait()
     for copy in copies:
         copy.wait_send()
-    for step in range(1, inner):
-        source = lax.rem(col + step, inner)
+    for step in range(1, firsts):
+        source = lax.rem(first + step, firsts)
         pltpu.make_async_remote_copy(
             src_ref=send_ref.at[source],
             dst_ref=middle.at[:, source],
             send_sem=first_send.at[source],
             recv_sem=first_recv.at[source],
-            device_id=(row * inner + source, mine),
-            device_id_type=mesh_id,
-        ).wait_recv()
-    local = pltpu.make_async_copy(middle.at[row], landed.at[row], local_sems.at[1])
+            device_id=(place(source, second), mine),
+            device_id_type=mesh_id,
+        ).wait_recv()
+    local = pltpu.make_async_copy(middle.at[second], landed.at[second], local_sems.at[1])
     local.start()
     copies = []
-    for step in range(1, outer):
-        target = lax.rem(row + step, outer)
+    for step in range(1, seconds):
+        target = lax.rem(second + step, seconds)
         copy = pltpu.make_async_remote_copy(
             src_ref=middle.at[target],
-            dst_ref=landed.at[row],
+            dst_ref=landed.at[second],
             send_sem=second_send.at[target],
-            recv_sem=second_recv.at[row],
-            device_id=(target * inner + col, mine),
+            recv_sem=second_recv.at[second],
+            device_id=(place(first, target), mine),
             device_id_type=mesh_id,
         )
         copy.start()
@@ -473,14 +477,14 @@
     local.wait()
     for copy in copies:
         copy.wait_send()
-    for step in range(1, outer):
-        source = lax.rem(row + step, outer)
+    for step in range(1, seconds):
+        source = lax.rem(second + step, seconds)
         pltpu.make_async_remote_copy(
             src_ref=middle.at[source],
             dst_ref=landed.at[source],
             send_sem=second_send.at[source],
             recv_sem=second_recv.at[source],
-            device_id=(source * inner + col, mine),
+            device_id=(place(first, source), mine),
             device_id_type=mesh_id,
         ).wait_recv()
     out_ref[...] = landed[...]
@@ -490,25 +494,26 @@
     count = chunks.shape[0]
     outer = count // inner
     rest = chunks.shape[1:]
-    by_inner = chunks.reshape((outer, inner) + rest).swapaxes(0, 1)
-    grid_shape = (outer, inner) + rest
+    by_first = chunks.reshape((outer, inner) + rest)
+    first_shape = (outer, inner) + rest
+    second_shape = (inner, outer) + rest
     landed = pl.pallas_call(
         relay_kernel,
-        out_shape=jax.ShapeDtypeStruct(grid_shape, chunks.dtype),
+        out_shape=jax.ShapeDtypeStruct(second_shape, chunks.dtype),
         in_specs=[pl.BlockSpec(memory_space=pltpu.VMEM)],
         out_specs=pl.BlockSpec(memory_space=pltpu.VMEM),
         scratch_shapes=[
-            pltpu.VMEM(grid_shape, chunks.dtype),
-            pltpu.VMEM(grid_shape, chunks.dtype),
+            pltpu.VMEM(second_shape, chunks.dtype),
+            pltpu.VMEM(second_shape, chunks.dtype),
             pltpu.SemaphoreType.DMA((2,)),
+            pltpu.SemaphoreType.DMA((outer,)),
+            pltpu.SemaphoreType.DMA((outer,)),
             pltpu.SemaphoreType.DMA((inner,)),
             pltpu.SemaphoreType.DMA((inner,)),
-            pltpu.SemaphoreType.DMA((outer,)),
-            pltpu.SemaphoreType.DMA((outer,)),
         ],
         compiler_params=pltpu.CompilerParams(collective_id=collective_id, has_side_effects=True),
-    )(by_inner)
-    return landed.reshape(chunks.shape)
+    )(by_first)
+    return landed.swapaxes(0, 1).reshape(chunks.shape)
 
 
 def per_device(inputs, short_filter, long_filter, grad_out):

time: 54.4 us -> 54 us (level)
    transpose x0 -> x1, local copies, waits for them, and re-layouts: none -> 0.97 us  [relay(): return landed.swapaxes(0, 1).reshape(chunks.shape)]
    pallas_call x1 -> x0, local copies, waits for them, and re-layouts: 0.92 us -> none  [relay(): pl.pallas_call(relay_kernel, out_shape=jax.ShapeDtypeStruct(grid_shape, c...]
    concatenate x0 -> x1, other arithmetic: none -> 0.75 us  [per_device(): jnp.concatenate([grad_out.reshape(ctx_count, per_dev, shard_len), inputs....]
    transpose x1 -> x0, other arithmetic: 0.75 us -> none  [relay(): by_inner = chunks.reshape((outer, inner) + rest).swapaxes(0, 1)]
    pallas_call x1, Pallas kernels: 25.4 us -> 24.9 us  [fused(): pl.pallas_call(fused_kernel, out_shape=jax.ShapeDtypeStruct(rows_shape, j...]
where the time goes in v10:
time: 54 us; the launch traced here: 53.5 us
  Pallas kernels  45.7 us (85%)
  local copies, waits for them, and re-layouts  5.33 us (10%)
  other arithmetic  1.7 us (3%)
  between operations  0.81 us (2%)
    pallas_call x1, Pallas kernels, fused(): pl.pallas_call(fused_kernel, out_shape=jax.ShapeDtypeStruct(rows_shape, j...  24.9 us
    pallas_call x1, Pallas kernels, relay(): pl.pallas_call(relay_kernel, out_shape=jax.ShapeDtypeStruct(second_shape,...  20.8 us
    unnamed x12, local copies, waits for them, and re-layouts  2.56 us

profile of v10, /device:TPU:8, one launch (start us, length us, event | category | flops | bytes accessed | tf_op | source)
XLA Modules:
  0.0 53.5 jit_solution(17710756484641683565)
XLA Ops:
  0.6 0.0 copy-start.2
  0.6 0.7 %copy-done.2 = bf16[32,128]{1,0:T(8,128)(2,1)S(1)} copy-done((bf16[32,128]{1,0:T(8,128)(2,1)S(1)}, bf16[32,128]{1,0:T(8,128)(2,1)}, u32[]{:S(2)}) %copy-start.2) | copy-done | bytes 8216
  1.3 0.0 copy-start.3
  1.4 0.6 %copy-done.3 = f32[3,32,4]{1,2,0:T(4,128)S(1)} copy-done((f32[3,32,4]{1,2,0:T(4,128)S(1)}, f32[3,32,4]{1,2,0:T(4,128)}, u32[]{:S(2)}) %copy-start.3) | copy-done | bytes 1560
  2.0 0.0 copy-start
  2.0 0.0 copy-start.1
  2.0 0.1 copy.11
  2.2 0.2 slice_reduce_fusion.2
  2.4 0.1 copy.12.taps_ref
  2.5 0.3 copy-done
  2.8 0.0 copy-done.1
  2.8 0.8 %pad_maximum_fusion.send_ref = bf16[8,8,5,128]{3,2,1,0:T(8,128)(2,1)} fusion(bf16[8,8,1,128]{3,2,1,0:T(2,128)(2,1)S(1)} %copy.9, bf16[8,8,2,128]{3,2,1,0:T(2,128)(2,1)S(1)} %bitcast.38, bf16[8,8,2,128]{3,2,1,0:T(2,128)(2,1)S(1)} %bitcast.39), kind=kLoop, calls=%fused_computation.2 | loop fusion | flops 245760 | bytes 163840 | tf_op jit(solution)/shard_map/concatenate | solution.py:530
  3.6 20.8 %shard_map.67 = bf16[8,8,5,128]{3,2,1,0:T(8,128)(2,1)} custom-call(bf16[8,8,5,128]{3,2,1,0:T(8,128)(2,1)} %pad_maximum_fusion.send_ref), custom_call_target="tpu_custom_call" | custom-call | tf_op jit(solution)/shard_map/pallas_call | solution.py:500
  24.4 1.0 %copy.21 = bf16[8,8,5,128]{3,1,0,2:T(8,128)(2,1)S(1)} copy(bf16[8,8,5,128]{3,2,0,1:T(8,128)(2,1)} %bitcast.28) | data formatting | bytes 163840 | tf_op jit(solution)/shard_map/transpose | solution.py:516
  25.4 0.1 copy.22
  25.4 0.2 fusion.9
  25.8 0.5 %rev.3 = bf16[3,65,256]{2,1,0:T(8,128)(2,1)S(1)} reverse(bf16[3,65,256]{2,1,0:T(8,128)(2,1)S(1)} %pad_maximum_fusion.1), dimensions={2} | reverse | bytes 199680 | tf_op jit(solution)/shard_map/rev | solution.py:385
  26.3 24.9 %shard_map.68 = f32[64,4,128]{2,1,0:T(4,128)S(1)} custom-call(f32[2,128,128]{2,1,0:T(8,128)S(1)} %pad_convert_fusion.grad_ref, f32[3,65,256]{2,1,0:T(8,128)S(1)} %convert_element_type.32.rev_ref, f32[2,65,128]{2,1,0:T(8,128)S(1)} %pad_convert_fusion.1.in_ref, f32[3,2]{1,0:T(4,128)S(1)} %copy.12.taps_ref), custom_call_target="tpu_custom_call" | custom-call | tf_op jit(solution)/shard_map/pallas_call | solution.py:390
  51.3 0.1 copy.13
  51.4 0.6 %slice.90 = bf16[64,2,128]{2,1,0:T(2,128)(2,1)} slice(f32[64,4,128]{2,1,0:T(4,128)S(1)} %shard_map.68), slice={[0:64], [0:2], [0:128]} | slice | bytes 65536 | tf_op jit(solution)/shard_map/slice | solution.py:561
  52.0 0.6 %reduce_sum.9 = f32[32,128]{1,0:T(8,128)} reduce(f32[32,2,128]{2,1,0:T(2,128)S(1)} %bitcast.34, f32[]{:T(128)} %constant.18.clone.1), dimensions={1}, to_apply=%region_0.1 | reduce | flops 4096 | bytes 49156 | tf_op jit(solution)/shard_map/reduce_sum | solution.py:563
  52.7 0.1 copy.14
  52.8 0.7 %copy.15 = f32[3,32,4]{1,2,0:T(4,128)} copy(f32[3,32,4]{0,2,1:T(4,128)S(1)} %bitcast.32) | data formatting | bytes 3072
  (16 shorter events, 0.3 us)
Async XLA Ops:
  0.6 0.7 %copy-start.2 = (bf16[32,128]{1,0:T(8,128)(2,1)S(1)}, bf16[32,128]{1,0:T(8,128)(2,1)}, u32[]{:S(2)}) copy-start(bf16[32,128]{1,0:T(8,128)(2,1)} %param.6) | copy-start | bytes 24580
  1.3 0.7 %copy-start.3 = (f32[3,32,4]{1,2,0:T(4,128)S(1)}, f32[3,32,4]{1,2,0:T(4,128)}, u32[]{:S(2)}) copy-start(f32[3,32,4]{1,2,0:T(4,128)} %param.5) | copy-start | bytes 4612
  2.0 0.8 %copy-start = (bf16[32,4,128]{2,1,0:T(4,128)(2,1)S(1)}, bf16[32,4,128]{2,1,0:T(4,128)(2,1)}, u32[]{:S(2)}) copy-start(bf16[32,4,128]{2,1,0:T(4,128)(2,1)} %param.4) | copy-start | bytes 98308
  2.0 0.8 %copy-start.1 = (bf16[32,4,128]{2,1,0:T(4,128)(2,1)S(1)}, bf16[32,4,128]{2,1,0:T(4,128)(2,1)}, u32[]{:S(2)}) copy-start(bf16[32,4,128]{2,1,0:T(4,128)(2,1)} %param.7) | copy-start | bytes 98308

commit v11 on v10

--- a/solution.py
+++ b/solution.py
@@ -535,7 +535,7 @@
         ],
         axis=1,
     )
-    recv = relay(send, 8, 0)
+    recv = relay(send, 16, 0)
     seqs = recv.transpose(1, 0, 2).reshape(2 * per_dev + 1, total_len)
     grad_seq = seqs[:per_dev]
     in_seq = seqs[per_dev : 2 * per_dev].astype(jnp.float32)

time: 54 us -> 56.6 us (1.048)
  Pallas kernels: 45.7 us -> 47.9 us
    pallas_call x1, Pallas kernels: 24.9 us -> 26.9 us  [fused(): pl.pallas_call(fused_kernel, out_shape=jax.ShapeDtypeStruct(rows_shape, j...]
where the time goes in v11:
time: 56.6 us; the launch traced here: 55.7 us
  Pallas kernels  47.9 us (85%)
  local copies, waits for them, and re-layouts  5.31 us (9%)
  other arithmetic  1.7 us (3%)
  between operations  0.81 us (1%)
    pallas_call x1, Pallas kernels, fused(): pl.pallas_call(fused_kernel, out_shape=jax.ShapeDtypeStruct(rows_shape, j...  26.9 us
    pallas_call x1, Pallas kernels, relay(): pl.pallas_call(relay_kernel, out_shape=jax.ShapeDtypeStruct(second_shape,...  21 us
    unnamed x12, local copies, waits for them, and re-layouts  2.56 us

profile of v11, /device:TPU:8, one launch (start us, length us, event | category | flops | bytes accessed | tf_op | source)
XLA Modules:
  0.0 55.7 jit_solution(717105354533967861)
XLA Ops:
  0.6 0.0 copy-start.2
  0.6 0.7 %copy-done.2 = bf16[32,128]{1,0:T(8,128)(2,1)S(1)} copy-done((bf16[32,128]{1,0:T(8,128)(2,1)S(1)}, bf16[32,128]{1,0:T(8,128)(2,1)}, u32[]{:S(2)}) %copy-start.2) | copy-done | bytes 8216
  1.3 0.0 copy-start.3
  1.4 0.6 %copy-done.3 = f32[3,32,4]{1,2,0:T(4,128)S(1)} copy-done((f32[3,32,4]{1,2,0:T(4,128)S(1)}, f32[3,32,4]{1,2,0:T(4,128)}, u32[]{:S(2)}) %copy-start.3) | copy-done | bytes 1560
  2.0 0.0 copy-start
  2.0 0.0 copy-start.1
  2.0 0.1 copy.11
  2.2 0.2 slice_reduce_fusion.2
  2.4 0.1 copy.12.taps_ref
  2.5 0.3 copy-done
  2.8 0.0 copy-done.1
  2.8 0.8 %pad_maximum_fusion.send_ref = bf16[4,16,5,128]{3,2,1,0:T(8,128)(2,1)} fusion(bf16[4,16,1,128]{3,2,1,0:T(2,128)(2,1)S(1)} %copy.9, bf16[4,16,2,128]{3,2,1,0:T(2,128)(2,1)S(1)} %bitcast.36, bf16[4,16,2,128]{3,2,1,0:T(2,128)(2,1)S(1)} %bitcast.37), kind=kLoop, calls=%fused_computation.2 | loop fusion | flops 245760 | bytes 163840 | tf_op jit(solution)/shard_map/concatenate | solution.py:530
  3.6 21.0 %shard_map.67 = bf16[16,4,5,128]{3,2,1,0:T(8,128)(2,1)} custom-call(bf16[4,16,5,128]{3,2,1,0:T(8,128)(2,1)} %pad_maximum_fusion.send_ref), custom_call_target="tpu_custom_call" | custom-call | tf_op jit(solution)/shard_map/pallas_call | solution.py:500
  24.6 0.9 %copy.10 = bf16[4,16,5,128]{3,1,0,2:T(8,128)(2,1)S(1)} copy(bf16[4,16,5,128]{3,2,0,1:T(8,128)(2,1)} %bitcast.26) | data formatting | bytes 163840 | tf_op jit(solution)/shard_map/transpose | solution.py:516
  25.6 0.1 copy.20
  25.6 0.2 fusion.9
  25.9 0.5 rev.3
  26.5 26.9 %shard_map.68 = f32[64,4,128]{2,1,0:T(4,128)S(1)} custom-call(f32[2,128,128]{2,1,0:T(8,128)S(1)} %pad_convert_fusion.grad_ref, f32[3,65,256]{2,1,0:T(8,128)S(1)} %convert_element_type.32.rev_ref, f32[2,65,128]{2,1,0:T(8,128)S(1)} %pad_convert_fusion.1.in_ref, f32[3,2]{1,0:T(4,128)S(1)} %copy.12.taps_ref), custom_call_target="tpu_custom_call" | custom-call | tf_op jit(solution)/shard_map/pallas_call | solution.py:390
  53.5 0.1 copy.13
  53.6 0.6 %slice.90 = bf16[64,2,128]{2,1,0:T(2,128)(2,1)} slice(f32[64,4,128]{2,1,0:T(4,128)S(1)} %shard_map.68), slice={[0:64], [0:2], [0:128]} | slice | bytes 65536 | tf_op jit(solution)/shard_map/slice | solution.py:561
  54.3 0.6 %reduce_sum.9 = f32[32,128]{1,0:T(8,128)} reduce(f32[32,2,128]{2,1,0:T(2,128)S(1)} %bitcast.32, f32[]{:T(128)} %constant.18.clone.1), dimensions={1}, to_apply=%region_0.1 | reduce | flops 4096 | bytes 49156 | tf_op jit(solution)/shard_map/reduce_sum | solution.py:563
  54.9 0.1 copy.14
  55.0 0.7 %copy.15 = f32[3,32,4]{1,2,0:T(4,128)} copy(f32[3,32,4]{0,2,1:T(4,128)S(1)} %bitcast.30) | data formatting | bytes 3072
  (16 shorter events, 0.3 us)
Async XLA Ops:
  0.6 0.7 %copy-start.2 = (bf16[32,128]{1,0:T(8,128)(2,1)S(1)}, bf16[32,128]{1,0:T(8,128)(2,1)}, u32[]{:S(2)}) copy-start(bf16[32,128]{1,0:T(8,128)(2,1)} %param.6) | copy-start | bytes 24580
  1.3 0.7 %copy-start.3 = (f32[3,32,4]{1,2,0:T(4,128)S(1)}, f32[3,32,4]{1,2,0:T(4,128)}, u32[]{:S(2)}) copy-start(f32[3,32,4]{1,2,0:T(4,128)} %param.5) | copy-start | bytes 4612
  2.0 0.8 %copy-start = (bf16[32,4,128]{2,1,0:T(4,128)(2,1)S(1)}, bf16[32,4,128]{2,1,0:T(4,128)(2,1)}, u32[]{:S(2)}) copy-start(bf16[32,4,128]{2,1,0:T(4,128)(2,1)} %param.4) | copy-start | bytes 98308
  2.0 0.8 %copy-start.1 = (bf16[32,4,128]{2,1,0:T(4,128)(2,1)S(1)}, bf16[32,4,128]{2,1,0:T(4,128)(2,1)}, u32[]{:S(2)}) copy-start(bf16[32,4,128]{2,1,0:T(4,128)(2,1)} %param.7) | copy-start | bytes 98308

commit v12 on v10

--- a/solution.py
+++ b/solution.py
@@ -228,7 +228,7 @@
 
 
 def fused_kernel(
-    grad_ref, rev_ref, in_ref, taps_ref, rows_out,
+    grad_ref, rev_ref, in_ref, taps_ref, short_out, grad_in_out, long_out,
     hankel, toeplitz, grad_buf, rows_buf, ch_in, rows_in, local_sems,
     rows_send, rows_recv, ch_send, ch_recv,
 ):
@@ -340,14 +340,19 @@
         summed = summed + ch_in[h]
     rows_buf[:, chans + 1, :] = summed
 
-    local_rows = pltpu.make_async_copy(rows_buf.at[me], rows_in.at[me], local_sems.at[0])
+    pairs = rows_in.shape[1]
+
+    def landing(index):
+        return rows_in.at[index // pairs, lax.rem(index, pairs)]
+
+    local_rows = pltpu.make_async_copy(rows_buf.at[me], landing(me), local_sems.at[0])
     local_rows.start()
     copies = []
     for step in range(1, count):
         peer = lax.rem(me + step, count)
         copy = pltpu.make_async_remote_copy(
             src_ref=rows_buf.at[peer],
-            dst_ref=rows_in.at[me],
+            dst_ref=landing(me),
             send_sem=rows_send.at[peer],
             recv_sem=rows_recv.at[me],
             device_id=(peer, mine),
@@ -362,16 +367,23 @@
         source = lax.rem(me + step, count)
         pltpu.make_async_remote_copy(
             src_ref=rows_buf.at[source],
-            dst_ref=rows_in.at[source],
+            dst_ref=landing(source),
             send_sem=rows_send.at[source],
             recv_sem=rows_recv.at[source],
             device_id=(source, mine),
             device_id_type=mesh_id,
         ).wait_recv()
-    rows_out[...] = rows_in[...]
-
-
-def fused(grad_seq, sources, in_seq, taps, groups, block_len, collective_id):
+    for pair in range(pairs):
+        short_out[:, pair, :] = rows_in[:, pair, chans, :]
+        for g in range(chans):
+            grad_in_out[:, pair * chans + g, :] = rows_in[:, pair, g, :].astype(grad_in_out.dtype)
+    total = rows_in[:, 0, chans + 1, :]
+    for pair in range(1, pairs):
+        total = total + rows_in[:, pair, chans + 1, :]
+    long_out[...] = total
+
+
+def fused(grad_seq, sources, in_seq, taps, groups, filter_count, block_len, collective_id):
     chans, total_len = grad_seq.shape
     count = sources.shape[0]
     block_count = total_len // block_len
@@ -386,19 +398,25 @@
     in_pad = jnp.pad(in_seq.reshape(chans, block_count, block_len), ((0, 0), (1, 0), (0, 0)))
     lags = block_count + 1
     rows_shape = (block_count, chans + 2, block_len)
+    pairs = block_count // filter_count
+    landed_shape = (filter_count, pairs, chans + 2, block_len)
     vmem = pl.BlockSpec(memory_space=pltpu.VMEM)
     return pl.pallas_call(
         fused_kernel,
-        out_shape=jax.ShapeDtypeStruct(rows_shape, jnp.float32),
+        out_shape=(
+            jax.ShapeDtypeStruct((filter_count, pairs, block_len), jnp.float32),
+            jax.ShapeDtypeStruct((filter_count, pairs * chans, block_len), jnp.bfloat16),
+            jax.ShapeDtypeStruct((filter_count, block_len), jnp.float32),
+        ),
         in_specs=[vmem, vmem, vmem, pl.BlockSpec(memory_space=pltpu.SMEM)],
-        out_specs=vmem,
+        out_specs=(vmem, vmem, vmem),
         scratch_shapes=[
             pltpu.VMEM((chans, block_count, lags * block_len), jnp.bfloat16),
             pltpu.VMEM((count, lags * block_len, block_len), jnp.bfloat16),
             pltpu.VMEM((chans, block_count + 8, block_len), jnp.float32),
             pltpu.VMEM(rows_shape, jnp.float32),
             pltpu.VMEM((groups, block_count, block_len), jnp.float32),
-            pltpu.VMEM(rows_shape, jnp.float32),
+            pltpu.VMEM(landed_shape, jnp.float32),
             pltpu.SemaphoreType.DMA((1,)),
             pltpu.SemaphoreType.DMA((block_count,)),
             pltpu.SemaphoreType.DMA((block_count,)),
@@ -549,19 +567,18 @@
     hidden = hidden.astype(jnp.bfloat16)
 
     groups = lax.axis_size("ch")
-    got = fused(
+    short_rows, grad_in_out, grad_long_out = fused(
         grad_seq,
         jnp.concatenate([filt_seq, hidden], axis=0),
         in_seq,
         taps,
         groups,
+        filter_count,
         block_len,
         1,
     )
-    grad_in_out = got[:, :per_dev].reshape(filter_count, chan_count, shard_len)
-    grad_in_out = grad_in_out.astype(jnp.bfloat16)
-    grad_long_out = got[:, per_dev + 1].reshape(filter_count, per_filter, shard_len).sum(axis=1)
-    short_all = got[:, per_dev, : tap_count * per_dev].reshape(ctx_count, tap_count, per_dev)
+    short_all = short_rows.reshape(ctx_count, shard_len)[:, : tap_count * per_dev]
+    short_all = short_all.reshape(ctx_count, tap_count, per_dev)
     grad_short_out = short_all.transpose(1, 0, 2).reshape(tap_count, filter_count, chan_count)
     return (grad_in_out, grad_long_out, grad_short_out)
 

time: 54 us -> 54 us (level)
  other arithmetic: 1.7 us -> 1.06 us
    unnamed x12 -> x15, local copies, waits for them, and re-layouts: 2.56 us -> 3.85 us
    slice x4 -> x0, local copies, waits for them, and re-layouts: 0.79 us -> none  [the longest x1 0.64 us: per_device(): grad_in_out = got[:, :per_dev].reshape(filter_count, chan_count, shard_len)]
    reduce_sum x1 -> x0, other arithmetic: 0.64 us -> none  [per_device(): got[:, per_dev + 1].reshape(filter_count, per_filter, shard_len).sum(axis=1)]
where the time goes in v12:
time: 54 us; the launch traced here: 53.5 us
  Pallas kernels  45.8 us (85%)
  local copies, waits for them, and re-layouts  5.85 us (11%)
  other arithmetic  1.06 us (2%)
  between operations  0.79 us (1%)
    pallas_call x1, Pallas kernels, fused(): pl.pallas_call(fused_kernel, out_shape=(jax.ShapeDtypeStruct((filter_coun...  25 us
    pallas_call x1, Pallas kernels, relay(): pl.pallas_call(relay_kernel, out_shape=jax.ShapeDtypeStruct(second_shape,...  20.8 us
    unnamed x15, local copies, waits for them, and re-layouts  3.85 us

profile of v12, /device:TPU:8, one launch (start us, length us, event | category | flops | bytes accessed | tf_op | source)
XLA Modules:
  0.0 53.5 jit_solution(11835290777875656852)
XLA Ops:
  0.6 0.0 copy-start.2
  0.6 0.7 %copy-done.2 = bf16[32,128]{1,0:T(8,128)(2,1)S(1)} copy-done((bf16[32,128]{1,0:T(8,128)(2,1)S(1)}, bf16[32,128]{1,0:T(8,128)(2,1)}, u32[]{:S(2)}) %copy-start.2) | copy-done | bytes 8216
  1.3 0.0 copy-start.3
  1.4 0.6 %copy-done.3 = f32[3,32,4]{1,2,0:T(4,128)S(1)} copy-done((f32[3,32,4]{1,2,0:T(4,128)S(1)}, f32[3,32,4]{1,2,0:T(4,128)}, u32[]{:S(2)}) %copy-start.3) | copy-done | bytes 1560
  2.0 0.0 copy-start
  2.0 0.0 copy-start.1
  2.0 0.1 copy.11
  2.2 0.2 slice_reduce_fusion.2
  2.4 0.1 copy.12.taps_ref
  2.5 0.3 copy-done
  2.8 0.0 copy-done.1
  2.8 0.8 %pad_maximum_fusion.send_ref = bf16[8,8,5,128]{3,2,1,0:T(8,128)(2,1)} fusion(bf16[8,8,1,128]{3,2,1,0:T(2,128)(2,1)S(1)} %copy.9, bf16[8,8,2,128]{3,2,1,0:T(2,128)(2,1)S(1)} %bitcast.38, bf16[8,8,2,128]{3,2,1,0:T(2,128)(2,1)S(1)} %bitcast.39), kind=kLoop, calls=%fused_computation.2 | loop fusion | flops 245760 | bytes 163840 | tf_op jit(solution)/shard_map/concatenate | solution.py:548
  3.6 20.8 %shard_map.67 = bf16[8,8,5,128]{3,2,1,0:T(8,128)(2,1)} custom-call(bf16[8,8,5,128]{3,2,1,0:T(8,128)(2,1)} %pad_maximum_fusion.send_ref), custom_call_target="tpu_custom_call" | custom-call | tf_op jit(solution)/shard_map/pallas_call | solution.py:518
  24.4 1.0 %copy.22 = bf16[8,8,5,128]{3,1,0,2:T(8,128)(2,1)S(1)} copy(bf16[8,8,5,128]{3,2,0,1:T(8,128)(2,1)} %bitcast.29) | data formatting | bytes 163840 | tf_op jit(solution)/shard_map/transpose | solution.py:534
  25.4 0.1 copy.23
  25.5 0.2 fusion.9
  25.8 0.5 %rev.3 = bf16[3,65,256]{2,1,0:T(8,128)(2,1)S(1)} reverse(bf16[3,65,256]{2,1,0:T(8,128)(2,1)S(1)} %pad_maximum_fusion.1), dimensions={2} | reverse | bytes 199680 | tf_op jit(solution)/shard_map/rev | solution.py:397
  26.4 25.0 %shard_map.68 = (f32[32,2,128]{2,1,0:T(2,128)S(1)}, bf16[32,4,128]{2,1,0:T(4,128)(2,1)S(1)}, f32[32,128]{1,0:T(8,128)S(1)}) custom-call(f32[2,128,128]{2,1,0:T(8,128)S(1)} %pad_convert_fusion.grad_ref, f32[3,65,256]{2,1,0:T(8,128)S(1)} %convert_element_type.28.rev_ref, f32[2,65,128]{2,1,0:T(8,128)S(1)} %pad_convert_fusion.1.in_ref, f32[3,2]{1,0:T(4,128)S(1)} %copy.12.taps_ref), custom_call_target="tpu_custom_call" | custom-call | tf_op jit(solution)/shard_map/pallas_call | solution.py:404
  51.4 0.1 copy.16
  51.4 0.1 copy.14
  51.6 0.7 %copy.15 = f32[3,32,4]{1,2,0:T(4,128)} copy(f32[3,32,4]{0,2,1:T(4,128)S(1)} %bitcast.33) | data formatting | bytes 3072
  52.3 0.6 %copy.27 = bf16[32,4,128]{2,1,0:T(4,128)(2,1)} copy(bf16[32,4,128]{2,1,0:T(4,128)(2,1)S(1)} %get-tuple-element.23) | data formatting | bytes 65536
  52.9 0.6 %copy.28 = f32[32,128]{1,0:T(8,128)} copy(f32[32,128]{1,0:T(8,128)S(1)} %get-tuple-element.24) | data formatting | bytes 32768
  (14 shorter events, 0.2 us)
Async XLA Ops:
  0.6 0.7 %copy-start.2 = (bf16[32,128]{1,0:T(8,128)(2,1)S(1)}, bf16[32,128]{1,0:T(8,128)(2,1)}, u32[]{:S(2)}) copy-start(bf16[32,128]{1,0:T(8,128)(2,1)} %param.6) | copy-start | bytes 24580
  1.3 0.7 %copy-start.3 = (f32[3,32,4]{1,2,0:T(4,128)S(1)}, f32[3,32,4]{1,2,0:T(4,128)}, u32[]{:S(2)}) copy-start(f32[3,32,4]{1,2,0:T(4,128)} %param.5) | copy-start | bytes 4612
  2.0 0.8 %copy-start = (bf16[32,4,128]{2,1,0:T(4,128)(2,1)S(1)}, bf16[32,4,128]{2,1,0:T(4,128)(2,1)}, u32[]{:S(2)}) copy-start(bf16[32,4,128]{2,1,0:T(4,128)(2,1)} %param.4) | copy-start | bytes 98308
  2.0 0.8 %copy-start.1 = (bf16[32,4,128]{2,1,0:T(4,128)(2,1)S(1)}, bf16[32,4,128]{2,1,0:T(4,128)(2,1)}, u32[]{:S(2)}) copy-start(bf16[32,4,128]{2,1,0:T(4,128)(2,1)} %param.7) | copy-start | bytes 98308

commit v13 on v12

--- a/solution.py
+++ b/solution.py
@@ -296,8 +296,14 @@
     lane = lax.broadcasted_iota(jnp.int32, (block_count, block_len), 1)
     short_row = jnp.zeros((block_count, block_len), jnp.float32)
     grad_buf[...] = jnp.zeros_like(grad_buf)
+    window = hankel.shape[2]
+    hidden_all = jnp.dot(
+        hankel[...].reshape(chans * block_count, window),
+        toeplitz[0],
+        preferred_element_type=jnp.float32,
+    )
     for g in range(chans):
-        hidden_grad = jnp.dot(hankel[g], toeplitz[0], preferred_element_type=jnp.float32)
+        hidden_grad = hidden_all[g * block_count : (g + 1) * block_count]
         grad_buf[g, pl.ds(0, block_count), :] = hidden_grad
         following = grad_buf[g, pl.ds(1, block_count), :]
         total = taps_ref[0, g] * hidden_grad

time: 54 us -> 53.9 us (level)
  no operation moved by 1% of the time
where the time goes in v13:
time: 53.9 us; the launch traced here: 53.4 us
  Pallas kernels  45.7 us (85%)
  local copies, waits for them, and re-layouts  5.85 us (11%)
  other arithmetic  1.06 us (2%)
  between operations  0.79 us (1%)
    pallas_call x1, Pallas kernels, fused(): pl.pallas_call(fused_kernel, out_shape=(jax.ShapeDtypeStruct((filter_coun...  24.9 us
    pallas_call x1, Pallas kernels, relay(): pl.pallas_call(relay_kernel, out_shape=jax.ShapeDtypeStruct(second_shape,...  20.8 us
    unnamed x15, local copies, waits for them, and re-layouts  3.85 us

profile of v13, /device:TPU:8, one launch (start us, length us, event | category | flops | bytes accessed | tf_op | source)
XLA Modules:
  0.0 53.4 jit_solution(8434807518600119294)
XLA Ops:
  0.6 0.0 copy-start.2
  0.6 0.7 %copy-done.2 = bf16[32,128]{1,0:T(8,128)(2,1)S(1)} copy-done((bf16[32,128]{1,0:T(8,128)(2,1)S(1)}, bf16[32,128]{1,0:T(8,128)(2,1)}, u32[]{:S(2)}) %copy-start.2) | copy-done | bytes 8216
  1.3 0.0 copy-start.3
  1.4 0.6 %copy-done.3 = f32[3,32,4]{1,2,0:T(4,128)S(1)} copy-done((f32[3,32,4]{1,2,0:T(4,128)S(1)}, f32[3,32,4]{1,2,0:T(4,128)}, u32[]{:S(2)}) %copy-start.3) | copy-done | bytes 1560
  2.0 0.0 copy-start
  2.0 0.0 copy-start.1
  2.0 0.1 copy.11
  2.2 0.2 slice_reduce_fusion.2
  2.4 0.1 copy.12.taps_ref
  2.5 0.3 copy-done
  2.8 0.0 copy-done.1
  2.8 0.8 %pad_maximum_fusion.send_ref = bf16[8,8,5,128]{3,2,1,0:T(8,128)(2,1)} fusion(bf16[8,8,1,128]{3,2,1,0:T(2,128)(2,1)S(1)} %copy.9, bf16[8,8,2,128]{3,2,1,0:T(2,128)(2,1)S(1)} %bitcast.38, bf16[8,8,2,128]{3,2,1,0:T(2,128)(2,1)S(1)} %bitcast.39), kind=kLoop, calls=%fused_computation.2 | loop fusion | flops 245760 | bytes 163840 | tf_op jit(solution)/shard_map/concatenate | solution.py:554
  3.6 20.8 %shard_map.67 = bf16[8,8,5,128]{3,2,1,0:T(8,128)(2,1)} custom-call(bf16[8,8,5,128]{3,2,1,0:T(8,128)(2,1)} %pad_maximum_fusion.send_ref), custom_call_target="tpu_custom_call" | custom-call | tf_op jit(solution)/shard_map/pallas_call | solution.py:524
  24.4 1.0 %copy.22 = bf16[8,8,5,128]{3,1,0,2:T(8,128)(2,1)S(1)} copy(bf16[8,8,5,128]{3,2,0,1:T(8,128)(2,1)} %bitcast.29) | data formatting | bytes 163840 | tf_op jit(solution)/shard_map/transpose | solution.py:540
  25.4 0.1 copy.23
  25.5 0.2 fusion.9
  25.8 0.5 %rev.3 = bf16[3,65,256]{2,1,0:T(8,128)(2,1)S(1)} reverse(bf16[3,65,256]{2,1,0:T(8,128)(2,1)S(1)} %pad_maximum_fusion.1), dimensions={2} | reverse | bytes 199680 | tf_op jit(solution)/shard_map/rev | solution.py:403
  26.4 24.9 %shard_map.68 = (f32[32,2,128]{2,1,0:T(2,128)S(1)}, bf16[32,4,128]{2,1,0:T(4,128)(2,1)S(1)}, f32[32,128]{1,0:T(8,128)S(1)}) custom-call(f32[2,128,128]{2,1,0:T(8,128)S(1)} %pad_convert_fusion.grad_ref, f32[3,65,256]{2,1,0:T(8,128)S(1)} %convert_element_type.28.rev_ref, f32[2,65,128]{2,1,0:T(8,128)S(1)} %pad_convert_fusion.1.in_ref, f32[3,2]{1,0:T(4,128)S(1)} %copy.12.taps_ref), custom_call_target="tpu_custom_call" | custom-call | tf_op jit(solution)/shard_map/pallas_call | solution.py:410
  51.2 0.1 copy.16
  51.3 0.1 copy.14
  51.4 0.7 %copy.15 = f32[3,32,4]{1,2,0:T(4,128)} copy(f32[3,32,4]{0,2,1:T(4,128)S(1)} %bitcast.33) | data formatting | bytes 3072
  52.1 0.6 %copy.27 = bf16[32,4,128]{2,1,0:T(4,128)(2,1)} copy(bf16[32,4,128]{2,1,0:T(4,128)(2,1)S(1)} %get-tuple-element.23) | data formatting | bytes 65536
  52.8 0.6 %copy.28 = f32[32,128]{1,0:T(8,128)} copy(f32[32,128]{1,0:T(8,128)S(1)} %get-tuple-element.24) | data formatting | bytes 32768
  (14 shorter events, 0.2 us)
Async XLA Ops:
  0.6 0.7 %copy-start.2 = (bf16[32,128]{1,0:T(8,128)(2,1)S(1)}, bf16[32,128]{1,0:T(8,128)(2,1)}, u32[]{:S(2)}) copy-start(bf16[32,128]{1,0:T(8,128)(2,1)} %param.6) | copy-start | bytes 24580
  1.3 0.7 %copy-start.3 = (f32[3,32,4]{1,2,0:T(4,128)S(1)}, f32[3,32,4]{1,2,0:T(4,128)}, u32[]{:S(2)}) copy-start(f32[3,32,4]{1,2,0:T(4,128)} %param.5) | copy-start | bytes 4612
  2.0 0.8 %copy-start = (bf16[32,4,128]{2,1,0:T(4,128)(2,1)S(1)}, bf16[32,4,128]{2,1,0:T(4,128)(2,1)}, u32[]{:S(2)}) copy-start(bf16[32,4,128]{2,1,0:T(4,128)(2,1)} %param.4) | copy-start | bytes 98308
  2.0 0.8 %copy-start.1 = (bf16[32,4,128]{2,1,0:T(4,128)(2,1)S(1)}, bf16[32,4,128]{2,1,0:T(4,128)(2,1)}, u32[]{:S(2)}) copy-start(bf16[32,4,128]{2,1,0:T(4,128)(2,1)} %param.7) | copy-start | bytes 98308

commit v14 on v13

--- a/solution.py
+++ b/solution.py
@@ -264,18 +264,24 @@
                 line = rev_ref[s, pl.ds(lag, 1), :]
                 tiled = jnp.broadcast_to(line, (block_len, 2 * block_len))
                 skewed = pltpu.roll(tiled, block_len + 1, 1, stride=1, stride_axis=0)
-                toeplitz[s, pl.ds(row, block_len), :] = skewed[:, :block_len].astype(
-                    toeplitz.dtype
-                )
+                toeplitz[pl.ds(row, block_len), pl.ds(s * block_len, block_len)] = skewed[
+                    :, :block_len
+                ].astype(toeplitz.dtype)
             return carry
 
         lax.fori_loop(0, lags, fill, 0)
 
     fill_toeplitz(range(1, sources))
 
-    acc = jnp.dot(hankel[0], toeplitz[1], preferred_element_type=jnp.float32)
+    window = hankel.shape[2]
+    both = jnp.dot(
+        hankel[...].reshape(chans * block_count, window),
+        toeplitz[:, block_len:],
+        preferred_element_type=jnp.float32,
+    )
+    acc = both[:block_count, :block_len]
     for g in range(1, chans):
-        acc = acc + jnp.dot(hankel[g], toeplitz[1 + g], preferred_element_type=jnp.float32)
+        acc = acc + both[g * block_count : (g + 1) * block_count, g * block_len : (g + 1) * block_len]
     ch_in[mine] = acc
     pl.semaphore_wait(barrier, len(peers))
     partials = []
@@ -296,10 +302,9 @@
     lane = lax.broadcasted_iota(jnp.int32, (block_count, block_len), 1)
     short_row = jnp.zeros((block_count, block_len), jnp.float32)
     grad_buf[...] = jnp.zeros_like(grad_buf)
-    window = hankel.shape[2]
     hidden_all = jnp.dot(
         hankel[...].reshape(chans * block_count, window),
-        toeplitz[0],
+        toeplitz[:, :block_len],
         preferred_element_type=jnp.float32,
     )
     for g in range(chans):
@@ -418,7 +423,7 @@
         out_specs=(vmem, vmem, vmem),
         scratch_shapes=[
             pltpu.VMEM((chans, block_count, lags * block_len), jnp.bfloat16),
-            pltpu.VMEM((count, lags * block_len, block_len), jnp.bfloat16),
+            pltpu.VMEM((lags * block_len, count * block_len), jnp.bfloat16),
             pltpu.VMEM((chans, block_count + 8, block_len), jnp.float32),
             pltpu.VMEM(rows_shape, jnp.float32),
             pltpu.VMEM((groups, block_count, block_len), jnp.float32),

time: 53.9 us -> 54.8 us (1.017)
  Pallas kernels: 45.7 us -> 46.6 us
    pallas_call x1, Pallas kernels: 24.9 us -> 25.8 us  [fused(): pl.pallas_call(fused_kernel, out_shape=(jax.ShapeDtypeStruct((filter_coun...]
where the time goes in v14:
time: 54.8 us; the launch traced here: 54.3 us
  Pallas kernels  46.6 us (85%)
  local copies, waits for them, and re-layouts  5.85 us (11%)
  other arithmetic  1.06 us (2%)
  between operations  0.79 us (1%)
    pallas_call x1, Pallas kernels, fused(): pl.pallas_call(fused_kernel, out_shape=(jax.ShapeDtypeStruct((filter_coun...  25.8 us
    pallas_call x1, Pallas kernels, relay(): pl.pallas_call(relay_kernel, out_shape=jax.ShapeDtypeStruct(second_shape,...  20.8 us
    unnamed x15, local copies, waits for them, and re-layouts  3.85 us

profile of v14, /device:TPU:8, one launch (start us, length us, event | category | flops | bytes accessed | tf_op | source)
XLA Modules:
  0.0 54.3 jit_solution(12632923771061539994)
XLA Ops:
  0.6 0.0 copy-start.2
  0.6 0.7 %copy-done.2 = bf16[32,128]{1,0:T(8,128)(2,1)S(1)} copy-done((bf16[32,128]{1,0:T(8,128)(2,1)S(1)}, bf16[32,128]{1,0:T(8,128)(2,1)}, u32[]{:S(2)}) %copy-start.2) | copy-done | bytes 8216
  1.3 0.0 copy-start.3
  1.4 0.6 %copy-done.3 = f32[3,32,4]{1,2,0:T(4,128)S(1)} copy-done((f32[3,32,4]{1,2,0:T(4,128)S(1)}, f32[3,32,4]{1,2,0:T(4,128)}, u32[]{:S(2)}) %copy-start.3) | copy-done | bytes 1560
  2.0 0.0 copy-start
  2.0 0.0 copy-start.1
  2.0 0.1 copy.11
  2.2 0.2 slice_reduce_fusion.2
  2.4 0.1 copy.12.taps_ref
  2.5 0.3 copy-done
  2.8 0.0 copy-done.1
  2.8 0.8 %pad_maximum_fusion.send_ref = bf16[8,8,5,128]{3,2,1,0:T(8,128)(2,1)} fusion(bf16[8,8,1,128]{3,2,1,0:T(2,128)(2,1)S(1)} %copy.9, bf16[8,8,2,128]{3,2,1,0:T(2,128)(2,1)S(1)} %bitcast.38, bf16[8,8,2,128]{3,2,1,0:T(2,128)(2,1)S(1)} %bitcast.39), kind=kLoop, calls=%fused_computation.2 | loop fusion | flops 245760 | bytes 163840 | tf_op jit(solution)/shard_map/concatenate | solution.py:559
  3.6 20.8 %shard_map.67 = bf16[8,8,5,128]{3,2,1,0:T(8,128)(2,1)} custom-call(bf16[8,8,5,128]{3,2,1,0:T(8,128)(2,1)} %pad_maximum_fusion.send_ref), custom_call_target="tpu_custom_call" | custom-call | tf_op jit(solution)/shard_map/pallas_call | solution.py:529
  24.4 1.0 %copy.22 = bf16[8,8,5,128]{3,1,0,2:T(8,128)(2,1)S(1)} copy(bf16[8,8,5,128]{3,2,0,1:T(8,128)(2,1)} %bitcast.29) | data formatting | bytes 163840 | tf_op jit(solution)/shard_map/transpose | solution.py:545
  25.4 0.1 copy.23
  25.5 0.2 fusion.9
  25.8 0.5 rev.3
  26.4 25.8 %shard_map.68 = (f32[32,2,128]{2,1,0:T(2,128)S(1)}, bf16[32,4,128]{2,1,0:T(4,128)(2,1)S(1)}, f32[32,128]{1,0:T(8,128)S(1)}) custom-call(f32[2,128,128]{2,1,0:T(8,128)S(1)} %pad_convert_fusion.grad_ref, f32[3,65,256]{2,1,0:T(8,128)S(1)} %convert_element_type.28.rev_ref, f32[2,65,128]{2,1,0:T(8,128)S(1)} %pad_convert_fusion.1.in_ref, f32[3,2]{1,0:T(4,128)S(1)} %copy.12.taps_ref), custom_call_target="tpu_custom_call" | custom-call | tf_op jit(solution)/shard_map/pallas_call | solution.py:415
  52.1 0.1 copy.16
  52.2 0.1 copy.14
  52.3 0.7 %copy.15 = f32[3,32,4]{1,2,0:T(4,128)} copy(f32[3,32,4]{0,2,1:T(4,128)S(1)} %bitcast.33) | data formatting | bytes 3072
  53.0 0.6 %copy.27 = bf16[32,4,128]{2,1,0:T(4,128)(2,1)} copy(bf16[32,4,128]{2,1,0:T(4,128)(2,1)S(1)} %get-tuple-element.23) | data formatting | bytes 65536
  53.7 0.6 %copy.28 = f32[32,128]{1,0:T(8,128)} copy(f32[32,128]{1,0:T(8,128)S(1)} %get-tuple-element.24) | data formatting | bytes 32768
  (14 shorter events, 0.2 us)
Async XLA Ops:
  0.6 0.7 %copy-start.2 = (bf16[32,128]{1,0:T(8,128)(2,1)S(1)}, bf16[32,128]{1,0:T(8,128)(2,1)}, u32[]{:S(2)}) copy-start(bf16[32,128]{1,0:T(8,128)(2,1)} %param.6) | copy-start | bytes 24580
  1.3 0.7 %copy-start.3 = (f32[3,32,4]{1,2,0:T(4,128)S(1)}, f32[3,32,4]{1,2,0:T(4,128)}, u32[]{:S(2)}) copy-start(f32[3,32,4]{1,2,0:T(4,128)} %param.5) | copy-start | bytes 4612
  2.0 0.8 %copy-start = (bf16[32,4,128]{2,1,0:T(4,128)(2,1)S(1)}, bf16[32,4,128]{2,1,0:T(4,128)(2,1)}, u32[]{:S(2)}) copy-start(bf16[32,4,128]{2,1,0:T(4,128)(2,1)} %param.4) | copy-start | bytes 98308
  2.0 0.8 %copy-start.1 = (bf16[32,4,128]{2,1,0:T(4,128)(2,1)S(1)}, bf16[32,4,128]{2,1,0:T(4,128)(2,1)}, u32[]{:S(2)}) copy-start(bf16[32,4,128]{2,1,0:T(4,128)(2,1)} %param.7) | copy-start | bytes 98308

commit v15 on v13

--- a/solution.py
+++ b/solution.py
@@ -511,7 +511,9 @@
             device_id=(place(first, source), mine),
             device_id_type=mesh_id,
         ).wait_recv()
-    out_ref[...] = landed[...]
+    for r in range(send_ref.shape[2]):
+        for f in range(firsts):
+            out_ref[r, pl.ds(f * seconds, seconds), :] = landed[:, f, r, :]
 
 
 def relay(chunks, inner, collective_id):
@@ -523,7 +525,7 @@
     second_shape = (inner, outer) + rest
     landed = pl.pallas_call(
         relay_kernel,
-        out_shape=jax.ShapeDtypeStruct(second_shape, chunks.dtype),
+        out_shape=jax.ShapeDtypeStruct((rest[0], count) + rest[1:], chunks.dtype),
         in_specs=[pl.BlockSpec(memory_space=pltpu.VMEM)],
         out_specs=pl.BlockSpec(memory_space=pltpu.VMEM),
         scratch_shapes=[
@@ -537,7 +539,7 @@
         ],
         compiler_params=pltpu.CompilerParams(collective_id=collective_id, has_side_effects=True),
     )(by_first)
-    return landed.swapaxes(0, 1).reshape(chunks.shape)
+    return landed
 
 
 def per_device(inputs, short_filter, long_filter, grad_out):
@@ -559,11 +561,11 @@
         ],
         axis=1,
     )
-    recv = relay(send, 8, 0)
-    seqs = recv.transpose(1, 0, 2).reshape(2 * per_dev + 1, total_len)
+    recv = relay(send.astype(jnp.float32), 8, 0)
+    seqs = recv.reshape(2 * per_dev + 1, total_len)
     grad_seq = seqs[:per_dev]
-    in_seq = seqs[per_dev : 2 * per_dev].astype(jnp.float32)
-    filt_seq = seqs[2 * per_dev :]
+    in_seq = seqs[per_dev : 2 * per_dev]
+    filt_seq = seqs[2 * per_dev :].astype(jnp.bfloat16)
     taps = short_filter.reshape(tap_count, ctx_count, per_dev)
     taps = lax.dynamic_index_in_dim(taps, my_index, axis=1, keepdims=False)
 

time: 53.9 us -> 55.4 us (1.028)
  local copies, waits for them, and re-layouts: 5.85 us -> 6.75 us
  Pallas kernels: 45.7 us -> 46.4 us
    slice x1 -> x2, local copies, waits for them, and re-layouts: 0.01 us -> 1.65 us  [the longest x1 0.89 us: per_device(): in_seq = seqs[per_dev:2 * per_dev]]
    transpose x1 -> x0, local copies, waits for them, and re-layouts: 0.97 us -> none  [relay(): return landed.swapaxes(0, 1).reshape(chunks.shape)]
    convert_element_type x0 -> x1, other arithmetic: none -> 0.8 us  [per_device(): recv = relay(send.astype(jnp.float32), 8, 0)]
    concatenate x1 -> x0, other arithmetic: 0.75 us -> none  [per_device(): jnp.concatenate([grad_out.reshape(ctx_count, per_dev, shard_len), inputs....]
where the time goes in v15:
time: 55.4 us; the launch traced here: 55 us
  Pallas kernels  46.4 us (84%)
  local copies, waits for them, and re-layouts  6.75 us (12%)
  other arithmetic  1.07 us (2%)
  between operations  0.78 us (1%)
    pallas_call x1, Pallas kernels, fused(): pl.pallas_call(fused_kernel, out_shape=(jax.ShapeDtypeStruct((filter_coun...  25.2 us
    pallas_call x1, Pallas kernels, relay(): pl.pallas_call(relay_kernel, out_shape=jax.ShapeDtypeStruct((rest[0], cou...  21.3 us
    unnamed x15, local copies, waits for them, and re-layouts  4.06 us

profile of v15, /device:TPU:8, one launch (start us, length us, event | category | flops | bytes accessed | tf_op | source)
XLA Modules:
  0.0 55.0 jit_solution(3905699690038621291)
XLA Ops:
  0.6 0.0 copy-start.3
  0.6 0.7 %copy-done.3 = f32[3,32,4]{1,2,0:T(4,128)S(1)} copy-done((f32[3,32,4]{1,2,0:T(4,128)S(1)}, f32[3,32,4]{1,2,0:T(4,128)}, u32[]{:S(2)}) %copy-start.3) | copy-done | bytes 1560
  1.3 0.1 copy.9
  1.4 0.0 copy-start.2
  1.5 0.2 slice_reduce_fusion.2
  1.6 0.5 copy-done.2
  2.1 0.0 copy-start.1
  2.2 0.0 copy-start
  2.2 0.7 %copy-done.1 = bf16[32,4,128]{2,1,0:T(4,128)(2,1)S(1)} copy-done((bf16[32,4,128]{2,1,0:T(4,128)(2,1)S(1)}, bf16[32,4,128]{2,1,0:T(4,128)(2,1)}, u32[]{:S(2)}) %copy-start.1) | copy-done | bytes 32792
  2.9 0.0 copy-done
  2.9 0.8 %maximum_convert_fusion.send_ref = f32[8,8,5,128]{3,2,1,0:T(8,128)} fusion(bf16[8,8,1,128]{3,2,1,0:T(2,128)(2,1)S(1)} %copy.8, bf16[8,8,2,128]{3,2,1,0:T(2,128)(2,1)S(1)} %bitcast.29, bf16[8,8,2,128]{3,2,1,0:T(2,128)(2,1)S(1)} %bitcast.30), kind=kLoop, calls=%fused_computation.2 | loop fusion | flops 245760 | bytes 245760 | tf_op jit(solution)/shard_map/convert_element_type | solution.py:564
  3.7 21.3 %shard_map.67 = f32[5,64,128]{2,1,0:T(8,128)} custom-call(f32[8,8,5,128]{3,2,1,0:T(8,128)} %maximum_convert_fusion.send_ref), custom_call_target="tpu_custom_call" | custom-call | tf_op jit(solution)/shard_map/pallas_call | solution.py:526
  25.0 0.9 %fusion.10 = (f32[2,64,128]{2,1,0:T(8,128)S(1)}, f32[1,2,64,128]{3,2,1,0:T(8,128)S(1)}, f32[2,64,128]{2,1,0:T(8,128)S(1)}) fusion(f32[5,64,128]{2,1,0:T(8,128)} %shard_map.67), kind=kLoop, calls=%fused_computation.24 | loop fusion | bytes 327680 | tf_op jit(solution)/shard_map/slice | solution.py:567
  25.9 0.1 copy.19
  25.9 0.2 fusion.9
  26.2 0.8 %slice.83 = bf16[1,64,128]{2,1,0:T(8,128)(2,1)S(1)} slice(f32[5,64,128]{2,1,0:T(8,128)} %shard_map.67), slice={[4:5], [0:64], [0:128]} | slice | bytes 32768 | tf_op jit(solution)/shard_map/slice | solution.py:568
  27.0 0.5 rev.3
  27.6 0.1 copy.10.taps_ref
  27.7 25.2 %shard_map.68 = (f32[32,2,128]{2,1,0:T(2,128)S(1)}, bf16[32,4,128]{2,1,0:T(4,128)(2,1)S(1)}, f32[32,128]{1,0:T(8,128)S(1)}) custom-call(f32[2,128,128]{2,1,0:T(8,128)S(1)} %pad.20.grad_ref, f32[3,65,256]{2,1,0:T(8,128)S(1)} %convert_element_type.26.rev_ref, f32[2,65,128]{2,1,0:T(8,128)S(1)} %pad.24.in_ref, f32[3,2]{1,0:T(4,128)S(1)} %copy.10.taps_ref), custom_call_target="tpu_custom_call" | custom-call | tf_op jit(solution)/shard_map/pallas_call | solution.py:410
  52.9 0.1 copy.14
  53.0 0.1 copy.12
  53.1 0.7 %copy.13 = f32[3,32,4]{1,2,0:T(4,128)} copy(f32[3,32,4]{0,2,1:T(4,128)S(1)} %bitcast.24) | data formatting | bytes 3072
  53.8 0.6 %copy.23 = bf16[32,4,128]{2,1,0:T(4,128)(2,1)} copy(bf16[32,4,128]{2,1,0:T(4,128)(2,1)S(1)} %get-tuple-element.23) | data formatting | bytes 65536
  54.4 0.6 %copy.24 = f32[32,128]{1,0:T(8,128)} copy(f32[32,128]{1,0:T(8,128)S(1)} %get-tuple-element.24) | data formatting | bytes 32768
  (12 shorter events, 0.2 us)
Async XLA Ops:
  0.6 0.7 %copy-start.3 = (f32[3,32,4]{1,2,0:T(4,128)S(1)}, f32[3,32,4]{1,2,0:T(4,128)}, u32[]{:S(2)}) copy-start(f32[3,32,4]{1,2,0:T(4,128)} %param.5) | copy-start | bytes 4612
  1.4 0.7 %copy-start.2 = (bf16[32,128]{1,0:T(8,128)(2,1)S(1)}, bf16[32,128]{1,0:T(8,128)(2,1)}, u32[]{:S(2)}) copy-start(bf16[32,128]{1,0:T(8,128)(2,1)} %param.6) | copy-start | bytes 24580
  2.1 0.8 %copy-start.1 = (bf16[32,4,128]{2,1,0:T(4,128)(2,1)S(1)}, bf16[32,4,128]{2,1,0:T(4,128)(2,1)}, u32[]{:S(2)}) copy-start(bf16[32,4,128]{2,1,0:T(4,128)(2,1)} %param.7) | copy-start | bytes 98308
  2.2 0.8 %copy-start = (bf16[32,4,128]{2,1,0:T(4,128)(2,1)S(1)}, bf16[32,4,128]{2,1,0:T(4,128)(2,1)}, u32[]{:S(2)}) copy-start(bf16[32,4,128]{2,1,0:T(4,128)(2,1)} %param.4) | copy-start | bytes 98308

commit v16 on v15

--- a/solution.py
+++ b/solution.py
@@ -561,11 +561,11 @@
         ],
         axis=1,
     )
-    recv = relay(send.astype(jnp.float32), 8, 0)
+    recv = relay(send, 8, 0)
     seqs = recv.reshape(2 * per_dev + 1, total_len)
     grad_seq = seqs[:per_dev]
-    in_seq = seqs[per_dev : 2 * per_dev]
-    filt_seq = seqs[2 * per_dev :].astype(jnp.bfloat16)
+    in_seq = seqs[per_dev : 2 * per_dev].astype(jnp.float32)
+    filt_seq = seqs[2 * per_dev :]
     taps = short_filter.reshape(tap_count, ctx_count, per_dev)
     taps = lax.dynamic_index_in_dim(taps, my_index, axis=1, keepdims=False)
 

time: 55.4 us -> 54.5 us (0.984)
  local copies, waits for them, and re-layouts: 6.75 us -> 5.57 us
  other arithmetic: 1.07 us -> 1.83 us
  Pallas kernels: 46.4 us -> 45.7 us
    slice x2, local copies, waits for them, and re-layouts: 1.65 us -> 0.7 us  [per_device(): filt_seq = seqs[2 * per_dev:]]
    convert_element_type x1 -> x0, other arithmetic: 0.8 us -> none  [per_device(): recv = relay(send.astype(jnp.float32), 8, 0)]
    slice x0 -> x1, other arithmetic: none -> 0.79 us  [per_device(): in_seq = seqs[per_dev:2 * per_dev].astype(jnp.float32)]
    concatenate x0 -> x1, other arithmetic: none -> 0.75 us  [per_device(): jnp.concatenate([grad_out.reshape(ctx_count, per_dev, shard_len), inputs....]
where the time goes in v16:
time: 54.5 us; the launch traced here: 53.9 us
  Pallas kernels  45.7 us (84%)
  local copies, waits for them, and re-layouts  5.57 us (10%)
  other arithmetic  1.83 us (3%)
  between operations  0.78 us (1%)
    pallas_call x1, Pallas kernels, fused(): pl.pallas_call(fused_kernel, out_shape=(jax.ShapeDtypeStruct((filter_coun...  24.9 us
    pallas_call x1, Pallas kernels, relay(): pl.pallas_call(relay_kernel, out_shape=jax.ShapeDtypeStruct((rest[0], cou...  20.8 us
    unnamed x15, local copies, waits for them, and re-layouts  3.85 us

profile of v16, /device:TPU:8, one launch (start us, length us, event | category | flops | bytes accessed | tf_op | source)
XLA Modules:
  0.0 53.9 jit_solution(5896715301047394011)
XLA Ops:
  0.6 0.0 copy-start.2
  0.6 0.7 %copy-done.2 = bf16[32,128]{1,0:T(8,128)(2,1)S(1)} copy-done((bf16[32,128]{1,0:T(8,128)(2,1)S(1)}, bf16[32,128]{1,0:T(8,128)(2,1)}, u32[]{:S(2)}) %copy-start.2) | copy-done | bytes 8216
  1.3 0.0 copy-start.3
  1.4 0.6 %copy-done.3 = f32[3,32,4]{1,2,0:T(4,128)S(1)} copy-done((f32[3,32,4]{1,2,0:T(4,128)S(1)}, f32[3,32,4]{1,2,0:T(4,128)}, u32[]{:S(2)}) %copy-start.3) | copy-done | bytes 1560
  2.0 0.0 copy-start
  2.0 0.0 copy-start.1
  2.0 0.1 copy.9
  2.2 0.2 slice_reduce_fusion.2
  2.4 0.1 copy.10.taps_ref
  2.5 0.3 copy-done
  2.8 0.0 copy-done.1
  2.8 0.8 %pad_maximum_fusion.send_ref = bf16[8,8,5,128]{3,2,1,0:T(8,128)(2,1)} fusion(bf16[8,8,1,128]{3,2,1,0:T(2,128)(2,1)S(1)} %copy.8, bf16[8,8,2,128]{3,2,1,0:T(2,128)(2,1)S(1)} %bitcast.29, bf16[8,8,2,128]{3,2,1,0:T(2,128)(2,1)S(1)} %bitcast.30), kind=kLoop, calls=%fused_computation.2 | loop fusion | flops 245760 | bytes 163840 | tf_op jit(solution)/shard_map/concatenate | solution.py:556
  3.6 20.8 %shard_map.67 = bf16[5,64,128]{2,1,0:T(8,128)(2,1)} custom-call(bf16[8,8,5,128]{3,2,1,0:T(8,128)(2,1)} %pad_maximum_fusion.send_ref), custom_call_target="tpu_custom_call" | custom-call | tf_op jit(solution)/shard_map/pallas_call | solution.py:526
  24.4 0.8 %fusion.10 = (bf16[2,64,128]{2,1,0:T(8,128)(2,1)S(1)}, f32[1,2,64,128]{3,2,1,0:T(8,128)S(1)}, bf16[2,64,128]{2,1,0:T(8,128)(2,1)S(1)}) fusion(bf16[5,64,128]{2,1,0:T(8,128)(2,1)} %shard_map.67), kind=kLoop, calls=%fused_computation.25 | loop fusion | flops 16384 | bytes 196608 | tf_op jit(solution)/shard_map/slice | solution.py:567
  25.2 0.1 copy.19
  25.3 0.2 fusion.9
  25.5 0.0 slice-start
  25.5 0.7 %slice-done = bf16[1,64,128]{2,1,0:T(8,128)(2,1)S(1)} async-done(((bf16[5,64,128]{2,1,0:T(8,128)(2,1)}), bf16[1,64,128]{2,1,0:T(8,128)(2,1)S(1)}, s32[]{:S(2)}) %slice-start) | async-done | bytes 16408 | tf_op jit(solution)/shard_map/slice | solution.py:568
  26.3 0.5 rev.3
  26.9 24.9 %shard_map.68 = (f32[32,2,128]{2,1,0:T(2,128)S(1)}, bf16[32,4,128]{2,1,0:T(4,128)(2,1)S(1)}, f32[32,128]{1,0:T(8,128)S(1)}) custom-call(f32[2,128,128]{2,1,0:T(8,128)S(1)} %pad_convert_fusion.grad_ref, f32[3,65,256]{2,1,0:T(8,128)S(1)} %convert_element_type.28.rev_ref, f32[2,65,128]{2,1,0:T(8,128)S(1)} %pad_convert_fusion.1.in_ref, f32[3,2]{1,0:T(4,128)S(1)} %copy.10.taps_ref), custom_call_target="tpu_custom_call" | custom-call | tf_op jit(solution)/shard_map/pallas_call | solution.py:410
  51.8 0.1 copy.14
  51.8 0.1 copy.12
  52.0 0.7 %copy.13 = f32[3,32,4]{1,2,0:T(4,128)} copy(f32[3,32,4]{0,2,1:T(4,128)S(1)} %bitcast.24) | data formatting | bytes 3072
  52.7 0.6 %copy.23 = bf16[32,4,128]{2,1,0:T(4,128)(2,1)} copy(bf16[32,4,128]{2,1,0:T(4,128)(2,1)S(1)} %get-tuple-element.23) | data formatting | bytes 65536
  53.3 0.6 %copy.24 = f32[32,128]{1,0:T(8,128)} copy(f32[32,128]{1,0:T(8,128)S(1)} %get-tuple-element.24) | data formatting | bytes 32768
  (12 shorter events, 0.2 us)
Async XLA Ops:
  0.6 0.7 %copy-start.2 = (bf16[32,128]{1,0:T(8,128)(2,1)S(1)}, bf16[32,128]{1,0:T(8,128)(2,1)}, u32[]{:S(2)}) copy-start(bf16[32,128]{1,0:T(8,128)(2,1)} %param.6) | copy-start | bytes 24580
  1.3 0.7 %copy-start.3 = (f32[3,32,4]{1,2,0:T(4,128)S(1)}, f32[3,32,4]{1,2,0:T(4,128)}, u32[]{:S(2)}) copy-start(f32[3,32,4]{1,2,0:T(4,128)} %param.5) | copy-start | bytes 4612
  2.0 0.8 %copy-start = (bf16[32,4,128]{2,1,0:T(4,128)(2,1)S(1)}, bf16[32,4,128]{2,1,0:T(4,128)(2,1)}, u32[]{:S(2)}) copy-start(bf16[32,4,128]{2,1,0:T(4,128)(2,1)} %param.4) | copy-start | bytes 98308
  2.0 0.8 %copy-start.1 = (bf16[32,4,128]{2,1,0:T(4,128)(2,1)S(1)}, bf16[32,4,128]{2,1,0:T(4,128)(2,1)}, u32[]{:S(2)}) copy-start(bf16[32,4,128]{2,1,0:T(4,128)(2,1)} %param.7) | copy-start | bytes 98308
  25.5 0.7 %slice-start = ((bf16[5,64,128]{2,1,0:T(8,128)(2,1)}), bf16[1,64,128]{2,1,0:T(8,128)(2,1)S(1)}, s32[]{:S(2)}) async-start(bf16[5,64,128]{2,1,0:T(8,128)(2,1)} %shard_map.67), calls=%async_computation | async-start | bytes 32768 | tf_op jit(solution)/shard_map/slice | solution.py:568

commit v17 on v13

--- a/solution.py
+++ b/solution.py
@@ -255,7 +255,7 @@
             )
         return carry
 
-    lax.fori_loop(0, lags, fill_hankel, 0)
+    lax.fori_loop(0, lags, fill_hankel, 0, unroll=5)
 
     def fill_toeplitz(picked):
         def fill(lag, carry):
@@ -269,7 +269,7 @@
                 )
             return carry
 
-        lax.fori_loop(0, lags, fill, 0)
+        lax.fori_loop(0, lags, fill, 0, unroll=5)
 
     fill_toeplitz(range(1, sources))
 

time: 53.9 us -> 49.1 us (0.911)
  the two profiles are of different devices: /device:TPU:8 before, /device:TPU:1 now
where the time goes in v17:
time: 49.1 us; the launch traced here: 48.9 us
  Pallas kernels  41.2 us (84%)
  local copies, waits for them, and re-layouts  5.85 us (12%)
  other arithmetic  1.06 us (2%)
  between operations  0.79 us (2%)
    pallas_call x1, Pallas kernels, fused(): pl.pallas_call(fused_kernel, out_shape=(jax.ShapeDtypeStruct((filter_coun...  21.2 us
    pallas_call x1, Pallas kernels, relay(): pl.pallas_call(relay_kernel, out_shape=jax.ShapeDtypeStruct(second_shape,...  19.9 us
    unnamed x15, local copies, waits for them, and re-layouts  3.85 us

profile of v17, /device:TPU:1, one launch (start us, length us, event | category | flops | bytes accessed | tf_op | source)
XLA Modules:
  0.0 48.9 jit_solution(6738818285155479389)
XLA Ops:
  0.6 0.0 copy-start.2
  0.6 0.7 %copy-done.2 = bf16[32,128]{1,0:T(8,128)(2,1)S(1)} copy-done((bf16[32,128]{1,0:T(8,128)(2,1)S(1)}, bf16[32,128]{1,0:T(8,128)(2,1)}, u32[]{:S(2)}) %copy-start.2) | copy-done | bytes 8216
  1.3 0.0 copy-start.3
  1.4 0.6 %copy-done.3 = f32[3,32,4]{1,2,0:T(4,128)S(1)} copy-done((f32[3,32,4]{1,2,0:T(4,128)S(1)}, f32[3,32,4]{1,2,0:T(4,128)}, u32[]{:S(2)}) %copy-start.3) | copy-done | bytes 1560
  2.0 0.0 copy-start
  2.0 0.0 copy-start.1
  2.0 0.1 copy.11
  2.2 0.2 slice_reduce_fusion.2
  2.4 0.1 copy.12.taps_ref
  2.5 0.3 copy-done
  2.8 0.0 copy-done.1
  2.8 0.8 %pad_maximum_fusion.send_ref = bf16[8,8,5,128]{3,2,1,0:T(8,128)(2,1)} fusion(bf16[8,8,1,128]{3,2,1,0:T(2,128)(2,1)S(1)} %copy.9, bf16[8,8,2,128]{3,2,1,0:T(2,128)(2,1)S(1)} %bitcast.38, bf16[8,8,2,128]{3,2,1,0:T(2,128)(2,1)S(1)} %bitcast.39), kind=kLoop, calls=%fused_computation.2 | loop fusion | flops 245760 | bytes 163840 | tf_op jit(solution)/shard_map/concatenate | solution.py:554
  3.6 19.9 %shard_map.67 = bf16[8,8,5,128]{3,2,1,0:T(8,128)(2,1)} custom-call(bf16[8,8,5,128]{3,2,1,0:T(8,128)(2,1)} %pad_maximum_fusion.send_ref), custom_call_target="tpu_custom_call" | custom-call | tf_op jit(solution)/shard_map/pallas_call | solution.py:524
  23.5 1.0 %copy.22 = bf16[8,8,5,128]{3,1,0,2:T(8,128)(2,1)S(1)} copy(bf16[8,8,5,128]{3,2,0,1:T(8,128)(2,1)} %bitcast.29) | data formatting | bytes 163840 | tf_op jit(solution)/shard_map/transpose | solution.py:540
  24.5 0.1 copy.23
  24.6 0.2 fusion.9
  24.9 0.5 %rev.3 = bf16[3,65,256]{2,1,0:T(8,128)(2,1)S(1)} reverse(bf16[3,65,256]{2,1,0:T(8,128)(2,1)S(1)} %pad_maximum_fusion.1), dimensions={2} | reverse | bytes 199680 | tf_op jit(solution)/shard_map/rev | solution.py:403
  25.5 21.2 %shard_map.68 = (f32[32,2,128]{2,1,0:T(2,128)S(1)}, bf16[32,4,128]{2,1,0:T(4,128)(2,1)S(1)}, f32[32,128]{1,0:T(8,128)S(1)}) custom-call(f32[2,128,128]{2,1,0:T(8,128)S(1)} %pad_convert_fusion.grad_ref, f32[3,65,256]{2,1,0:T(8,128)S(1)} %convert_element_type.28.rev_ref, f32[2,65,128]{2,1,0:T(8,128)S(1)} %pad_convert_fusion.1.in_ref, f32[3,2]{1,0:T(4,128)S(1)} %copy.12.taps_ref), custom_call_target="tpu_custom_call" | custom-call | tf_op jit(solution)/shard_map/pallas_call | solution.py:410
  46.7 0.1 copy.16
  46.8 0.1 copy.14
  46.9 0.7 %copy.15 = f32[3,32,4]{1,2,0:T(4,128)} copy(f32[3,32,4]{0,2,1:T(4,128)S(1)} %bitcast.33) | data formatting | bytes 3072
  47.6 0.6 %copy.27 = bf16[32,4,128]{2,1,0:T(4,128)(2,1)} copy(bf16[32,4,128]{2,1,0:T(4,128)(2,1)S(1)} %get-tuple-element.23) | data formatting | bytes 65536
  48.2 0.6 %copy.28 = f32[32,128]{1,0:T(8,128)} copy(f32[32,128]{1,0:T(8,128)S(1)} %get-tuple-element.24) | data formatting | bytes 32768
  (14 shorter events, 0.2 us)
Async XLA Ops:
  0.6 0.7 %copy-start.2 = (bf16[32,128]{1,0:T(8,128)(2,1)S(1)}, bf16[32,128]{1,0:T(8,128)(2,1)}, u32[]{:S(2)}) copy-start(bf16[32,128]{1,0:T(8,128)(2,1)} %param.6) | copy-start | bytes 24580
  1.3 0.7 %copy-start.3 = (f32[3,32,4]{1,2,0:T(4,128)S(1)}, f32[3,32,4]{1,2,0:T(4,128)}, u32[]{:S(2)}) copy-start(f32[3,32,4]{1,2,0:T(4,128)} %param.5) | copy-start | bytes 4612
  2.0 0.8 %copy-start = (bf16[32,4,128]{2,1,0:T(4,128)(2,1)S(1)}, bf16[32,4,128]{2,1,0:T(4,128)(2,1)}, u32[]{:S(2)}) copy-start(bf16[32,4,128]{2,1,0:T(4,128)(2,1)} %param.4) | copy-start | bytes 98308
  2.0 0.8 %copy-start.1 = (bf16[32,4,128]{2,1,0:T(4,128)(2,1)S(1)}, bf16[32,4,128]{2,1,0:T(4,128)(2,1)}, u32[]{:S(2)}) copy-start(bf16[32,4,128]{2,1,0:T(4,128)(2,1)} %param.7) | copy-start | bytes 98308

commit v18 on v17

--- a/solution.py
+++ b/solution.py
@@ -255,7 +255,7 @@
             )
         return carry
 
-    lax.fori_loop(0, lags, fill_hankel, 0, unroll=5)
+    lax.fori_loop(0, lags, fill_hankel, 0, unroll=13)
 
     def fill_toeplitz(picked):
         def fill(lag, carry):
@@ -269,7 +269,7 @@
                 )
             return carry
 
-        lax.fori_loop(0, lags, fill, 0, unroll=5)
+        lax.fori_loop(0, lags, fill, 0, unroll=13)
 
     fill_toeplitz(range(1, sources))
 

time: 49.1 us -> 49.1 us (level)
  no operation moved by 1% of the time
where the time goes in v18:
time: 49.1 us; the launch traced here: 48.9 us
  Pallas kernels  41.2 us (84%)
  local copies, waits for them, and re-layouts  5.85 us (12%)
  other arithmetic  1.06 us (2%)
  between operations  0.79 us (2%)
    pallas_call x1, Pallas kernels, fused(): pl.pallas_call(fused_kernel, out_shape=(jax.ShapeDtypeStruct((filter_coun...  21.2 us
    pallas_call x1, Pallas kernels, relay(): pl.pallas_call(relay_kernel, out_shape=jax.ShapeDtypeStruct(second_shape,...  19.9 us
    unnamed x15, local copies, waits for them, and re-layouts  3.85 us

profile of v18, /device:TPU:1, one launch (start us, length us, event | category | flops | bytes accessed | tf_op | source)
XLA Modules:
  0.0 48.9 jit_solution(8940524334227520232)
XLA Ops:
  0.6 0.0 copy-start.2
  0.6 0.7 %copy-done.2 = bf16[32,128]{1,0:T(8,128)(2,1)S(1)} copy-done((bf16[32,128]{1,0:T(8,128)(2,1)S(1)}, bf16[32,128]{1,0:T(8,128)(2,1)}, u32[]{:S(2)}) %copy-start.2) | copy-done | bytes 8216
  1.3 0.0 copy-start.3
  1.4 0.6 %copy-done.3 = f32[3,32,4]{1,2,0:T(4,128)S(1)} copy-done((f32[3,32,4]{1,2,0:T(4,128)S(1)}, f32[3,32,4]{1,2,0:T(4,128)}, u32[]{:S(2)}) %copy-start.3) | copy-done | bytes 1560
  2.0 0.0 copy-start
  2.0 0.0 copy-start.1
  2.0 0.1 copy.11
  2.2 0.2 slice_reduce_fusion.2
  2.4 0.1 copy.12.taps_ref
  2.5 0.3 copy-done
  2.8 0.0 copy-done.1
  2.8 0.8 %pad_maximum_fusion.send_ref = bf16[8,8,5,128]{3,2,1,0:T(8,128)(2,1)} fusion(bf16[8,8,1,128]{3,2,1,0:T(2,128)(2,1)S(1)} %copy.9, bf16[8,8,2,128]{3,2,1,0:T(2,128)(2,1)S(1)} %bitcast.38, bf16[8,8,2,128]{3,2,1,0:T(2,128)(2,1)S(1)} %bitcast.39), kind=kLoop, calls=%fused_computation.2 | loop fusion | flops 245760 | bytes 163840 | tf_op jit(solution)/shard_map/concatenate | solution.py:554
  3.6 19.9 %shard_map.67 = bf16[8,8,5,128]{3,2,1,0:T(8,128)(2,1)} custom-call(bf16[8,8,5,128]{3,2,1,0:T(8,128)(2,1)} %pad_maximum_fusion.send_ref), custom_call_target="tpu_custom_call" | custom-call | tf_op jit(solution)/shard_map/pallas_call | solution.py:524
  23.5 1.0 %copy.22 = bf16[8,8,5,128]{3,1,0,2:T(8,128)(2,1)S(1)} copy(bf16[8,8,5,128]{3,2,0,1:T(8,128)(2,1)} %bitcast.29) | data formatting | bytes 163840 | tf_op jit(solution)/shard_map/transpose | solution.py:540
  24.5 0.1 copy.23
  24.6 0.2 fusion.9
  24.9 0.5 %rev.3 = bf16[3,65,256]{2,1,0:T(8,128)(2,1)S(1)} reverse(bf16[3,65,256]{2,1,0:T(8,128)(2,1)S(1)} %pad_maximum_fusion.1), dimensions={2} | reverse | bytes 199680 | tf_op jit(solution)/shard_map/rev | solution.py:403
  25.5 21.2 %shard_map.68 = (f32[32,2,128]{2,1,0:T(2,128)S(1)}, bf16[32,4,128]{2,1,0:T(4,128)(2,1)S(1)}, f32[32,128]{1,0:T(8,128)S(1)}) custom-call(f32[2,128,128]{2,1,0:T(8,128)S(1)} %pad_convert_fusion.grad_ref, f32[3,65,256]{2,1,0:T(8,128)S(1)} %convert_element_type.28.rev_ref, f32[2,65,128]{2,1,0:T(8,128)S(1)} %pad_convert_fusion.1.in_ref, f32[3,2]{1,0:T(4,128)S(1)} %copy.12.taps_ref), custom_call_target="tpu_custom_call" | custom-call | tf_op jit(solution)/shard_map/pallas_call | solution.py:410
  46.7 0.1 copy.16
  46.8 0.1 copy.14
  46.9 0.7 %copy.15 = f32[3,32,4]{1,2,0:T(4,128)} copy(f32[3,32,4]{0,2,1:T(4,128)S(1)} %bitcast.33) | data formatting | bytes 3072
  47.6 0.6 %copy.27 = bf16[32,4,128]{2,1,0:T(4,128)(2,1)} copy(bf16[32,4,128]{2,1,0:T(4,128)(2,1)S(1)} %get-tuple-element.23) | data formatting | bytes 65536
  48.2 0.6 %copy.28 = f32[32,128]{1,0:T(8,128)} copy(f32[32,128]{1,0:T(8,128)S(1)} %get-tuple-element.24) | data formatting | bytes 32768
  (14 shorter events, 0.2 us)
Async XLA Ops:
  0.6 0.7 %copy-start.2 = (bf16[32,128]{1,0:T(8,128)(2,1)S(1)}, bf16[32,128]{1,0:T(8,128)(2,1)}, u32[]{:S(2)}) copy-start(bf16[32,128]{1,0:T(8,128)(2,1)} %param.6) | copy-start | bytes 24580
  1.3 0.7 %copy-start.3 = (f32[3,32,4]{1,2,0:T(4,128)S(1)}, f32[3,32,4]{1,2,0:T(4,128)}, u32[]{:S(2)}) copy-start(f32[3,32,4]{1,2,0:T(4,128)} %param.5) | copy-start | bytes 4612
  2.0 0.8 %copy-start = (bf16[32,4,128]{2,1,0:T(4,128)(2,1)S(1)}, bf16[32,4,128]{2,1,0:T(4,128)(2,1)}, u32[]{:S(2)}) copy-start(bf16[32,4,128]{2,1,0:T(4,128)(2,1)} %param.4) | copy-start | bytes 98308
  2.0 0.8 %copy-start.1 = (bf16[32,4,128]{2,1,0:T(4,128)(2,1)S(1)}, bf16[32,4,128]{2,1,0:T(4,128)(2,1)}, u32[]{:S(2)}) copy-start(bf16[32,4,128]{2,1,0:T(4,128)(2,1)} %param.7) | copy-start | bytes 98308
